TPU v7x, 32 devices: a whole 2x2x4 slice. The times are simulated.
32 devices in a mesh: dp: 8 (over z, y), mp: 4 (over x, core).
Axes of the slice: x: 2, y: 2, z: 4, core: 2. Of those that a mesh axis runs over, the one named last changes fastest.
Arguments:
- block_in: bfloat16 [4096, 768], P(('dp', 'mp')), may hold values from -6 to 6
- coords: float32 [3, 4096], P(None, 'dp'), may hold values from -10 to 10
- lengths: int32 [8, 16], P('dp'), may hold values from 1 to 256, 512 in all within a row
- cotangent: bfloat16 [4096, 768], P(('dp', 'mp')), may hold values from -6 to 6
- step_count: int32 [1], replicated, may hold values from 1 to 20
- qkv_weight: float32 [3, 768, 768], P(None, 'mp'), may hold values from -0.21875 to 0.21875
- proj_weight: float32 [768, 768], P('mp'), may hold values from -0.625 to 0.625
- pair_weight: float32 [32, 128], P('mp'), may hold values from -3.6 to 3.6
- in_weight: float32 [3072, 768], P('mp'), may hold values from -0.21875 to 0.21875
- in_bias: float32 [3072], P('mp'), may hold values from -1.8 to 1.8
- out_weight: float32 [3072, 768], P('mp'), may hold values from -0.109375 to 0.109375
- norm_params: float32 [5, 768], replicated, may hold values from -0.4 to 1.3, as said below
- qkv_first: float32 [3, 768, 768], P(None, 'mp'), may hold values from -0.00033 to 0.00033
- proj_first: float32 [768, 768], P('mp'), may hold values from -0.000165 to 0.000165
- pair_first: float32 [32, 128], P('mp'), may hold values from -0.00016 to 0.00016
- in_first: float32 [3072, 768], P('mp'), may hold values from -0.00013 to 0.00013
- bias_first: float32 [3072], P('mp'), may hold values from -0.00013 to 0.00013
- out_first: float32 [3072, 768], P('mp'), may hold values from -0.00028 to 0.00028
- norm_first: float32 [5, 768], replicated, may hold values from -0.00046 to 0.00046
- qkv_second: float32 [3, 768, 768], P(None, 'mp'), may hold values from 1.25e-10 to 2e-09
- proj_second: float32 [768, 768], P('mp'), may hold values from 3.1e-11 to 5e-10
- pair_second: float32 [32, 128], P('mp'), may hold values from 2.9e-11 to 4.7e-10
- in_second: float32 [3072, 768], P('mp'), may hold values from 2e-11 to 3.2e-10
- bias_second: float32 [3072], P('mp'), may hold values from 2e-11 to 3.2e-10
- out_second: float32 [3072, 768], P('mp'), may hold values from 8.8e-11 to 1.4e-09
- norm_second: float32 [5, 768], replicated, may hold values from 2.45e-10 to 3.9e-09
Outputs:
- block_out: float32 [4096, 768], P(('dp', 'mp'))
- grad_input: float32 [4096, 768], P(('dp', 'mp'))
- grad_norm: float32 [1], replicated
- qkv_new: float32 [3, 768, 768], P(None, 'mp')
- qkv_first_new: float32 [3, 768, 768], P(None, 'mp')
- qkv_second_new: float32 [3, 768, 768], P(None, 'mp')
- proj_new: float32 [768, 768], P('mp')
- proj_first_new: float32 [768, 768], P('mp')
- proj_second_new: float32 [768, 768], P('mp')
- pair_new: float32 [32, 128], P('mp')
- pair_first_new: float32 [32, 128], P('mp')
- pair_second_new: float32 [32, 128], P('mp')
- in_new: float32 [3072, 768], P('mp')
- in_first_new: float32 [3072, 768], P('mp')
- in_second_new: float32 [3072, 768], P('mp')
- bias_new: float32 [3072], P('mp')
- bias_first_new: float32 [3072], P('mp')
- bias_second_new: float32 [3072], P('mp')
- out_new: float32 [3072, 768], P('mp')
- out_first_new: float32 [3072, 768], P('mp')
- out_second_new: float32 [3072, 768], P('mp')
- norm_new: float32 [5, 768], replicated
- norm_first_new: float32 [5, 768], replicated
- norm_second_new: float32 [5, 768], replicated
Inputs may be any that keep to these rules, and one draw needn't show every extreme that they name: `lengths`: each row lists, in order, the atom counts of 16 whole molecules that fill one block of 512 consecutive atoms; each row sums to 512 and its largest entry is 256. `norm_params`: rows 0 and 2 are gains, rows 1, 3 and 4 are shifts and the output bias.
All inputs are finite; a program needn't handle non-finite values.
Results may differ from a plain program's by a relative error of at most 0.012.
The roundings to bfloat16 on the way count: a program that leaves them out, or rounds other values in their place, can miss the bound.
Values may be sent and summed in bfloat16 or wider, within the bound.
A program may use at most 128 MiB of HBM per device.

v0:
```python
import math

import jax
import jax.numpy as jnp
from jax import lax
from jax.sharding import PartitionSpec as P

KERN = 128


ln_eps = 1e-05
mask_fill = -1e30
beta_one = 0.9
beta_two = 0.999
adam_eps = 1e-08
clip_level = 1.0


def layer_norm(rows, gain, shift):
    mean = jnp.mean(rows, axis=-1, keepdims=True)
    centred = rows - mean
    variance = jnp.mean(centred * centred, axis=-1, keepdims=True)
    return centred * lax.rsqrt(variance + ln_eps) * gain + shift


def exact_gelu(values):
    return jax.nn.gelu(values, approximate=False)


def segment_ids(lengths, width):
    ends = jnp.cumsum(lengths, axis=-1)
    places = lax.broadcasted_iota(jnp.int32, (lengths.shape[0], width, lengths.shape[1]), 1)
    return jnp.sum((places >= ends[:, None, :]).astype(jnp.int32), axis=-1)


def gaussians(points):
    delta = points[:, :, None] - points[:, None, :]
    dist = jnp.sqrt(jnp.sum(delta * delta, axis=0))
    spacing = 12.8 / KERN
    centres = lax.broadcasted_iota(jnp.float32, (KERN,), 0) * spacing
    scaled = (dist[:, :, None] - centres) / spacing
    return jnp.exp(-0.5 * scaled * scaled)


def block_scores(pair_low, query, keys, spots, marks, scale):
    gauss = gaussians(spots).astype(jnp.bfloat16)
    bias = jnp.einsum("ijk,hk->hij", gauss, pair_low, preferred_element_type=jnp.float32)
    score = (
        jnp.einsum("ihd,jhd->hij", query, keys, preferred_element_type=jnp.float32) * scale + bias
    )
    same = marks[:, None] == marks[None, :]
    return (jnp.where(same[None], score, mask_fill), gauss)


def adam_step(weight, grad, first, second, clip, fix_one, fix_two, rate, decay):
    scaled = grad * clip
    first_new = beta_one * first + (1.0 - beta_one) * scaled
    second_new = beta_two * second + (1.0 - beta_two) * scaled * scaled
    ratio = first_new / fix_one / (jnp.sqrt(second_new / fix_two) + adam_eps)
    return (weight - rate * (ratio + decay * weight), first_new, second_new)


def per_device(
    block_in,
    coords,
    lengths,
    cotangent,
    step_count,
    qkv_weight,
    proj_weight,
    pair_weight,
    in_weight,
    in_bias,
    out_weight,
    norm_params,
    qkv_first,
    proj_first,
    pair_first,
    in_first,
    bias_first,
    out_first,
    norm_first,
    qkv_second,
    proj_second,
    pair_second,
    in_second,
    bias_second,
    out_second,
    norm_second,
):
    group = coords.shape[1]
    blocks = lengths.shape[0]
    span = group // blocks
    heads = pair_weight.shape[0]
    inner = qkv_weight.shape[1]
    head_dim = inner // heads
    scale = 1.0 / math.sqrt(head_dim)
    rows_in = block_in.astype(jnp.float32)
    grad_out = cotangent.astype(jnp.float32)
    labels = segment_ids(lengths, span)
    points = coords.reshape(3, blocks, span).transpose(1, 0, 2)
    qkv_low = qkv_weight.astype(jnp.bfloat16)
    proj_low = proj_weight.astype(jnp.bfloat16)
    pair_low = pair_weight.astype(jnp.bfloat16)
    in_low = in_weight.astype(jnp.bfloat16)
    out_low = out_weight.astype(jnp.bfloat16)
    bias_low = in_bias.astype(jnp.bfloat16)
    first_norm = layer_norm(rows_in, norm_params[0], norm_params[1]).astype(jnp.bfloat16)
    first_all = lax.all_gather(first_norm, "mp", axis=0, tiled=True)
    qkv = jnp.einsum("rd,scd->src", first_all, qkv_low, preferred_element_type=jnp.float32).astype(
        jnp.bfloat16
    )
    split = qkv.reshape(3, blocks, span, heads, head_dim)

    def attend(items):
        query, keys, values, spots, marks = items
        score, gauss = block_scores(pair_low, query, keys, spots, marks, scale)
        top = jnp.max(score, axis=-1, keepdims=True)
        expo = jnp.exp(score - top)
        total = jnp.sum(expo, axis=-1, keepdims=True)
        probs = (expo / total).astype(jnp.bfloat16)
        mixed = jnp.einsum("hij,jhd->ihd", probs, values, preferred_element_type=jnp.float32)
        return (mixed.reshape(span, inner).astype(jnp.bfloat16), (top + jnp.log(total))[:, :, 0])

    heads_out, levels = lax.map(attend, (split[0], split[1], split[2], points, labels))
    attn_rows = heads_out.reshape(group, inner)
    piece = attn_rows
    attn = lax.psum_scatter(
        jnp.dot(piece, proj_low, preferred_element_type=jnp.float32),
        "mp",
        scatter_dimension=0,
        tiled=True,
    )
    mid = rows_in + attn
    second_norm = layer_norm(mid, norm_params[2], norm_params[3]).astype(jnp.bfloat16)
    second_all = lax.all_gather(second_norm, "mp", axis=0, tiled=True)
    pre = jnp.einsum(
        "rd,fd->rf", second_all, in_low, preferred_element_type=jnp.float32
    ) + bias_low.astype(jnp.float32)
    act_value, gelu_back = jax.vjp(exact_gelu, pre)
    act = act_value.astype(jnp.bfloat16)
    piece = act
    ffn = lax.psum_scatter(
        jnp.dot(piece, out_low, preferred_element_type=jnp.float32),
        "mp",
        scatter_dimension=0,
        tiled=True,
    )
    grad_all = lax.all_gather(cotangent, "mp", axis=0, tiled=True)
    grad_act = jnp.einsum("rd,fd->rf", grad_all, out_low, preferred_element_type=jnp.float32)
    out_grad = jnp.einsum("rf,rd->fd", act, grad_all, preferred_element_type=jnp.float32)
    grad_pre = gelu_back(grad_act)[0].astype(jnp.bfloat16)
    in_grad = jnp.einsum("rf,rd->fd", grad_pre, second_all, preferred_element_type=jnp.float32)
    bias_grad = jnp.sum(grad_pre.astype(jnp.float32), axis=0)
    piece = grad_pre
    grad_second = lax.psum_scatter(
        jnp.dot(piece, in_low, preferred_element_type=jnp.float32),
        "mp",
        scatter_dimension=0,
        tiled=True,
    )
    block_out = mid + ffn + norm_params[4]
    _, second_back = jax.vjp(layer_norm, mid, norm_params[2], norm_params[3])
    grad_mid_part, gain_two, shift_two = second_back(grad_second)
    grad_mid = grad_out + grad_mid_part
    grad_attn = grad_mid.astype(jnp.bfloat16)
    attn_all = lax.all_gather(grad_attn, "mp", axis=0, tiled=True)
    proj_grad = jnp.einsum("rc,rd->cd", attn_rows, attn_all, preferred_element_type=jnp.float32)
    grad_heads = jnp.einsum(
        "rd,cd->rc", attn_all, proj_low, preferred_element_type=jnp.float32
    ).astype(jnp.bfloat16)
    grad_split = grad_heads.reshape(blocks, span, heads, head_dim)

    def attend_back(items):
        query, keys, values, grad_mixed, level, spots, marks = items
        score, gauss = block_scores(pair_low, query, keys, spots, marks, scale)
        probs = jnp.exp(score - level[:, :, None])
        grad_values = jnp.einsum(
            "hij,ihd->jhd",
            probs.astype(jnp.bfloat16),
            grad_mixed,
            preferred_element_type=jnp.float32,
        )
        grad_probs = jnp.einsum(
            "ihd,jhd->hij", grad_mixed, values, preferred_element_type=jnp.float32
        )
        rowdot = jnp.sum(probs * grad_probs, axis=-1, keepdims=True)
        grad_score = (probs * (grad_probs - rowdot)).astype(jnp.bfloat16)
        grad_query = (
            jnp.einsum("hij,jhd->ihd", grad_score, keys, preferred_element_type=jnp.float32) * scale
        )
        grad_keys = (
            jnp.einsum("hij,ihd->jhd", grad_score, query, preferred_element_type=jnp.float32)
            * scale
        )
        pair_part = jnp.einsum("hij,ijk->hk", grad_score, gauss, preferred_element_type=jnp.float32)
        return (
            grad_query.astype(jnp.bfloat16),
            grad_keys.astype(jnp.bfloat16),
            grad_values.astype(jnp.bfloat16),
            pair_part,
        )

    grad_query, grad_keys, grad_values, pair_parts = lax.map(
        attend_back, (split[0], split[1], split[2], grad_split, levels, points, labels)
    )
    grad_qkv = jnp.stack(
        [
            grad_query.reshape(group, inner),
            grad_keys.reshape(group, inner),
            grad_values.reshape(group, inner),
        ]
    )
    qkv_grad = jnp.einsum("src,rd->scd", grad_qkv, first_all, preferred_element_type=jnp.float32)
    pair_grad = jnp.sum(pair_parts, axis=0)
    piece = grad_qkv
    grad_first = lax.psum_scatter(
        jnp.einsum("src,scd->rd", piece, qkv_low, preferred_element_type=jnp.float32),
        "mp",
        scatter_dimension=0,
        tiled=True,
    )
    _, first_back = jax.vjp(layer_norm, rows_in, norm_params[0], norm_params[1])
    grad_x_part, gain_one, shift_one = first_back(grad_first)
    grad_input = grad_mid + grad_x_part
    norm_grad = jnp.stack([gain_one, shift_one, gain_two, shift_two, jnp.sum(grad_out, axis=0)])
    qkv_grad, proj_grad, pair_grad, in_grad, bias_grad, out_grad = lax.psum(
        (qkv_grad, proj_grad, pair_grad, in_grad, bias_grad, out_grad), "dp"
    )
    norm_grad = lax.psum(norm_grad, ("dp", "mp"))
    local_squares = jnp.float32(0.0)
    for grad in (qkv_grad, proj_grad, pair_grad, in_grad, bias_grad, out_grad):
        local_squares = local_squares + jnp.sum(grad * grad)
    total = lax.psum(local_squares, "mp") + jnp.sum(norm_grad * norm_grad)
    grad_norm = jnp.sqrt(total)
    clip = clip_level / jnp.maximum(grad_norm, clip_level)
    count = step_count[0].astype(jnp.float32)
    fix_one = 1.0 - jnp.power(beta_one, count)
    fix_two = 1.0 - jnp.power(beta_two, count)
    qkv_out = adam_step(
        qkv_weight, qkv_grad, qkv_first, qkv_second, clip, fix_one, fix_two, 0.9, 0.01
    )
    proj_out = adam_step(
        proj_weight, proj_grad, proj_first, proj_second, clip, fix_one, fix_two, 2.5, 0.01
    )
    pair_out = adam_step(
        pair_weight, pair_grad, pair_first, pair_second, clip, fix_one, fix_two, 7.5, 0.01
    )
    in_out = adam_step(in_weight, in_grad, in_first, in_second, clip, fix_one, fix_two, 0.9, 0.01)
    bias_out = adam_step(
        in_bias, bias_grad, bias_first, bias_second, clip, fix_one, fix_two, 7.5, 0.0
    )
    out_out = adam_step(
        out_weight, out_grad, out_first, out_second, clip, fix_one, fix_two, 0.45, 0.01
    )
    norm_out = adam_step(
        norm_params, norm_grad, norm_first, norm_second, clip, fix_one, fix_two, 3.0, 0.0
    )
    return (
        block_out,
        grad_input,
        grad_norm.reshape(1),
        qkv_out[0],
        qkv_out[1],
        qkv_out[2],
        proj_out[0],
        proj_out[1],
        proj_out[2],
        pair_out[0],
        pair_out[1],
        pair_out[2],
        in_out[0],
        in_out[1],
        in_out[2],
        bias_out[0],
        bias_out[1],
        bias_out[2],
        out_out[0],
        out_out[1],
        out_out[2],
        norm_out[0],
        norm_out[1],
        norm_out[2],
    )


def solution(mesh):
    in_specs = (
        P(("dp", "mp"), None),
        P(None, "dp"),
        P("dp", None),
        P(("dp", "mp"), None),
        P(),
        P(None, "mp", None),
        P("mp", None),
        P("mp", None),
        P("mp", None),
        P("mp"),
        P("mp", None),
        P(),
        P(None, "mp", None),
        P("mp", None),
        P("mp", None),
        P("mp", None),
        P("mp"),
        P("mp", None),
        P(),
        P(None, "mp", None),
        P("mp", None),
        P("mp", None),
        P("mp", None),
        P("mp"),
        P("mp", None),
        P(),
    )
    out_specs = (
        P(("dp", "mp"), None),
        P(("dp", "mp"), None),
        P(),
        P(None, "mp", None),
        P(None, "mp", None),
        P(None, "mp", None),
        P("mp", None),
        P("mp", None),
        P("mp", None),
        P("mp", None),
        P("mp", None),
        P("mp", None),
        P("mp", None),
        P("mp", None),
        P("mp", None),
        P("mp"),
        P("mp"),
        P("mp"),
        P("mp", None),
        P("mp", None),
        P("mp", None),
        P(),
        P(),
        P(),
    )
    return jax.shard_map(
        per_device, mesh=mesh, in_specs=in_specs, out_specs=out_specs, check_vma=False
    )
```

profile of v0, /device:TPU:0, one launch (start us, length us, event | category | flops | bytes accessed | tf_op | source)
XLA Modules:
  0.0 553.5 jit_solution(14430814430959455791)
XLA Ops:
  7.3 1.6 slice_reduce_fusion
  8.8 1.0 convert_reduce_fusion.1
  9.9 1.1 fusion.57
  11.1 1.1 fusion.55
  12.2 10.1 %all_gather.12 = bf16[512,768]{1,0:T(8,128)(2,1)S(1)} all-gather(bf16[128,768]{1,0:T(8,128)(2,1)S(1)} %fusion.55), channel_id=1, replica_groups=mesh['dp'=8,'mp'=4] {'mp'}, dimensions={0}, use_global_device_ids=true | all-gather | bytes 983040 | tf_op jit(solution)/shard_map/all_gather | solution.py:109
  22.3 0.7 fusion.23
  23.9 1.0 copy-done.32
  24.8 47.8 %fusion.5 = f32[512,512,8]{1,2,0:T(8,128)} fusion(f32[128]{0:T(128)S(1)} %iota_multiply_fusion, f32[512,512]{1,0:T(8,128)S(1)} %sqrt.34, f32[8,128]{1,0:T(8,128)S(1)} %copy-done.63), kind=kOutput, calls=%fused_computation.6 | convolution fusion | flops 704644096 | bytes 9441792 | tf_op jit(solution)/shard_map/while/body/eval_jaxpr/ijk,hk->hij/dot_general | solution.py:47
  72.6 9.9 %copy.56 = f32[512,512,8]{0,1,2:T(8,128)} copy(f32[512,512,8]{1,2,0:T(8,128)} %fusion.5) | data formatting | bytes 16777216 | tf_op jit(solution)/shard_map/while/body/eval_jaxpr/ijk,hk->hij/dot_general | solution.py:47
  83.1 5.4 fusion.89
  88.4 1.2 fusion.8
  89.7 2.0 copy-done
  91.7 1.4 fusion.29
  93.0 0.7 copy-done.35
  93.7 1.6 fusion.61
  95.4 9.2 %all_gather.14 = bf16[512,768]{1,0:T(8,128)(2,1)} all-gather(bf16[128,768]{1,0:T(8,128)(2,1)S(1)} %copy-done.30), channel_id=1, replica_groups=mesh['dp'=8,'mp'=4] {'mp'}, dimensions={0}, use_global_device_ids=true | all-gather | bytes 983040 | tf_op jit(solution)/shard_map/all_gather | solution.py:149
  104.6 19.7 %reduce-scatter.5.cloned.1.call-done = f32[128,768]{1,0:T(8,128)} async-done(((f32[512,768]{1,0:T(8,128)}), f32[128,768]{1,0:T(8,128)}) %reduce-scatter.5.cloned.1.call-update) | async-done | bytes 393232 | tf_op jit(solution)/shard_map/reduce_scatter | solution.py:128
  124.3 1.3 fusion.87
  125.9 8.2 %all_gather.13 = bf16[512,768]{1,0:T(8,128)(2,1)S(1)} all-gather(bf16[128,768]{1,0:T(8,128)(2,1)S(1)} %add_convert_fusion.1), channel_id=1, replica_groups=mesh['dp'=8,'mp'=4] {'mp'}, dimensions={0}, use_global_device_ids=true | all-gather | bytes 983040 | tf_op jit(solution)/shard_map/all_gather | solution.py:136
  134.2 10.3 %multiply_convert_fusion.1 = (bf16[512,768]{1,0:T(8,128)(2,1)S(1)}, f32[512,768]{1,0:T(8,128)S(1)}, f32[512,768]{1,0:T(8,128)S(1)}) fusion(f32[768]{0:T(1024)S(1)} %convert_convert_fusion, bf16[512,768]{1,0:T(8,128)(2,1)S(1)} %all_gather.13, f32[768,768]{1,0:T(8,128)S(1)} %copy-done.4), kind=kOutput, calls=%fused_computation.39 | convolution fusion | flops 630521856 | bytes 7080960 | tf_op jit(solution)/shard_map/rd,fd->rf/dot_general | solution.py:137
  144.6 1.9 convert_reduce_fusion
  146.4 0.9 copy-done.12
  147.3 1.9 fusion.47
  149.3 3.6 fusion.43
  153.0 24.9 %reduce-scatter.9.cloned.1.call-done = f32[128,768]{1,0:T(8,128)} async-done(((f32[512,768]{1,0:T(8,128)}), f32[128,768]{1,0:T(8,128)}) %reduce-scatter.9.cloned.1.call-update) | async-done | bytes 393232 | tf_op jit(solution)/shard_map/reduce_scatter | solution.py:156
  177.9 1.8 multiply_reduce_fusion.6
  180.3 28.8 %reduce-scatter.7.cloned.1.call-done = f32[128,768]{1,0:T(8,128)} async-done(((f32[512,768]{1,0:T(8,128)}), f32[128,768]{1,0:T(8,128)}) %reduce-scatter.7.cloned.1.call-update) | async-done | bytes 393232 | tf_op jit(solution)/shard_map/reduce_scatter | solution.py:143
  209.1 2.2 fusion.85
  211.2 0.7 copy-done.16
  212.0 1.0 fusion.59
  213.0 8.3 %all_gather.15 = bf16[512,768]{1,0:T(8,128)(2,1)S(1)} all-gather(bf16[128,768]{1,0:T(8,128)(2,1)S(1)} %fusion.59), channel_id=1, replica_groups=mesh['dp'=8,'mp'=4] {'mp'}, dimensions={0}, use_global_device_ids=true | all-gather | bytes 983040 | tf_op jit(solution)/shard_map/all_gather | solution.py:167
  221.7 4.8 fusion.24
  226.5 5.4 multiply_reduce_fusion
  232.0 2.6 multiply_convert_fusion
  234.6 1.2 fusion.28
  235.8 0.7 copy-done.1
  236.5 0.7 fusion.27
  237.2 0.7 copy-done.39
  237.9 2.0 convolution_bitcast_fusion
  239.9 3.7 fusion.91
  243.6 2.2 fusion.92
  245.8 1.1 fusion.90
  247.0 1.8 fusion.33
  249.6 8.1 %copy.61 = bf16[8,512,512]{2,0,1:T(8,128)(2,1)} copy(bf16[8,512,512]{1,2,0:T(8,128)(2,1)} %copy-done.1) | data formatting | bytes 8388608 | tf_op jit(solution)/shard_map/while/body/eval_jaxpr/convert_element_type | solution.py:188
  257.8 48.2 %fusion.30 = f32[8,128]{1,0:T(8,128)S(1)} fusion(bf16[8,512,512]{2,0,1:T(8,128)(2,1)} %copy.61, f32[128]{0:T(128)S(1)} %copy-done.75, f32[512,512]{1,0:T(8,128)} %copy-done.32), kind=kOutput, calls=%fused_computation.64 | convolution fusion | flops 704643072 | bytes 5247488 | tf_op jit(solution)/shard_map/while/body/eval_jaxpr/hij,ijk->hk/dot_general | solution.py:196
  306.0 23.1 %all-reduce = (f32[8,128]{1,0:T(8,128)S(1)}, f32[768]{0:T(1024)S(1)}) all-reduce(f32[8,128]{1,0:T(8,128)S(1)} %fusion.30, f32[768]{0:T(1024)S(1)} %copy-done.62), channel_id=1, replica_groups=mesh['dp'=8,'mp'=4] {'dp'}, use_global_device_ids=true, to_apply=%region_22.23 | all-reduce | flops 1792 | bytes 14336 | tf_op jit(solution)/shard_map/psum | solution.py:227
  329.2 0.6 multiply_reduce_fusion.11
  330.4 1.2 fusion.77
  331.6 1.3 fusion.56
  332.9 2.0 convert_reduce_fusion.2
  335.0 39.9 %psum.63 = f32[5,768]{1,0:T(8,128)S(1)} all-reduce(f32[5,768]{1,0:T(8,128)S(1)} %stack.15), channel_id=1, replica_groups=mesh['dp'=8,'mp'=4] {'dp','mp'}, use_global_device_ids=true, to_apply=%region_37.38 | all-reduce | flops 3840 | bytes 30720 | tf_op jit(solution)/shard_map/psum | solution.py:230
  374.9 132.8 %all-reduce.4.cloned.1.call-done = (f32[3,192,768]{2,1,0:T(8,128)}, f32[192,768]{1,0:T(8,128)}, f32[768,768]{1,0:T(8,128)}, f32[768,768]{1,0:T(8,128)}) async-done(((f32[3,192,768]{2,1,0:T(8,128)}, f32[192,768]{1,0:T(8,128)}, f32[768,768]{1,0:T(8,128)}, f32[768,768]{1,0:T(8,128)}), (f32[3,192,768]{2,1,0:T(8,128)}, f32[192,768]{1,0:T(8,128)}, f32[768,768]{1,0:T(8,128)}, ...) | async-done | bytes 7077904 | tf_op jit(solution)/shard_map/psum | solution.py:227
  507.7 2.7 multiply_reduce_fusion.4
  510.4 2.0 multiply_reduce_fusion.5
  512.4 1.2 multiply_reduce_fusion.3
  513.6 1.2 multiply_reduce_fusion.2
  518.6 0.6 multiply_reduce_fusion.9
  519.3 6.9 %psum.62 = f32[]{:T(128)} all-reduce(f32[]{:T(128)S(6)} %add.256), channel_id=1, replica_groups=mesh['dp'=8,'mp'=4] {'mp'}, use_global_device_ids=true, to_apply=%region_31.32 | all-reduce | flops 1 | bytes 8 | tf_op jit(solution)/shard_map/psum | solution.py:234
  527.6 6.0 %multiply_subtract_fusion.2 = (f32[3,192,768]{2,1,0:T(8,128)}, f32[3,192,768]{2,1,0:T(8,128)}, f32[3,192,768]{2,1,0:T(8,128)}) fusion(f32[3,192,768]{2,1,0:T(8,128)S(1)} %copy-done.2, f32[]{:T(128)} %bitcast.22, f32[]{:T(128)} %bitcast.21, f32[3,192,768]{2,1,0:T(8,128)} %get-tuple-element.104, f32[]{:T(128)S(6)} %div.161, f32[3,192,768]{2,1,0:T(8,128)} %param.45, ...), kind=kLoop, calls=%fused_computation.33 | loop fusion | flops 7077888 | bytes 12386316 | tf_op jit(solution)/shard_map/sub | solution.py:60
  533.7 1.5 multiply_subtract_fusion.3
  535.8 0.6 multiply_subtract_fusion.6
  536.4 0.6 multiply_subtract_fusion.5
  537.0 0.6 multiply_subtract_fusion.4
  537.7 8.1 %multiply_subtract_fusion = (f32[768,768]{1,0:T(8,128)}, f32[768,768]{1,0:T(8,128)}, f32[768,768]{1,0:T(8,128)}, f32[768,768]{1,0:T(8,128)}, f32[768,768]{1,0:T(8,128)}, /*index=5*/f32[768,768]{1,0:T(8,128)}) fusion(f32[768,768]{1,0:T(8,128)S(1)} %copy-done.7, f32[]{:T(128)} %bitcast.22, f32[]{:T(128)} %bitcast.21, f32[768,768]{1,0:T(8,128)S(1)} %copy-done.11, ...), kind=kLoop, calls=%fused_computation.26 | loop fusion | flops 18874368 | bytes 33030156 | tf_op jit(solution)/shard_map/sub | solution.py:60
  (188 shorter events, 4.5 us)
Async XLA Ops:
  7.2 15.1 %copy-start.2 = (f32[3,192,768]{2,1,0:T(8,128)S(1)}, f32[3,192,768]{2,1,0:T(8,128)}, u32[]{:S(2)}) copy-start(f32[3,192,768]{2,1,0:T(8,128)} %param.31) | copy-start | bytes 5308420
  7.2 117.1 %reduce-scatter.5.cloned.1.call-start = ((), (), s32[]{:S(2)}) async-start(), calls=%async_computation.4 | async-start | bytes 1966080 | tf_op jit(solution)/shard_map/reduce_scatter | solution.py:128
  7.3 16.6 %copy-start.74 = (f32[128]{0:T(128)}, f32[128]{0:T(128)S(1)}, u32[]{:S(2)}) copy-start(f32[128]{0:T(128)S(1)} %iota_multiply_fusion) | copy-start | bytes 1540
  8.8 3.3 copy-start.45
  8.8 169.1 %copy-start.47 = (f32[768]{0:T(1024)}, f32[768]{0:T(1024)S(1)}, u32[]{:S(2)}) copy-start(f32[768]{0:T(1024)S(1)} %get-tuple-element.99) | copy-start | bytes 9220
  9.9 13.0 %copy-start.56 = (f32[128]{0:T(128)}, f32[128]{0:T(128)S(1)}, u32[]{:S(2)}) copy-start(f32[128]{0:T(128)S(1)} %broadcast_multiply_fusion.1) | copy-start | bytes 1540
  11.0 11.9 %copy-start.71 = (f32[128]{0:T(128)}, f32[128]{0:T(128)S(1)}, u32[]{:S(2)}) copy-start(f32[128]{0:T(128)S(1)} %fusion.57) | copy-start | bytes 1540
  11.0 11.9 %copy-start.59 = (f32[128]{0:T(128)}, f32[128]{0:T(128)S(1)}, u32[]{:S(2)}) copy-start(f32[128]{0:T(128)S(1)} %fusion.68) | copy-start | bytes 1540
  23.2 59.9 %copy-start.26 = (bf16[1,512,192]{1,2,0:T(8,128)(2,1)}, bf16[1,512,192]{1,2,0:T(8,128)(2,1)S(1)}, u32[]{:S(2)}) copy-start(bf16[1,512,192]{1,2,0:T(8,128)(2,1)S(1)} %get-tuple-element.135) | copy-start | bytes 589828
  23.2 59.9 %copy-start.28 = (bf16[1,512,192]{1,2,0:T(8,128)(2,1)}, bf16[1,512,192]{1,2,0:T(8,128)(2,1)S(1)}, u32[]{:S(2)}) copy-start(bf16[1,512,192]{1,2,0:T(8,128)(2,1)S(1)} %get-tuple-element.136) | copy-start | bytes 589828
  23.2 66.4 %copy-start.33 = (bf16[1,512,192]{1,2,0:T(8,128)(2,1)}, bf16[1,512,192]{1,2,0:T(8,128)(2,1)S(1)}, u32[]{:S(2)}) copy-start(bf16[1,512,192]{1,2,0:T(8,128)(2,1)S(1)} %get-tuple-element.137) | copy-start | bytes 589828
  72.6 9.9 %copy-start.73 = (s32[1,16]{1,0:T(1,128)S(1)}, s32[1,16]{1,0:T(1,128)}, u32[]{:S(2)}) copy-start(s32[1,16]{1,0:T(1,128)} %param.28) | copy-start | bytes 196
  88.4 3.2 copy-start
  95.3 29.0 %copy-start.3 = (bf16[128,768]{1,0:T(8,128)(2,1)S(1)}, bf16[128,768]{1,0:T(8,128)(2,1)}, u32[]{:S(2)}) copy-start(bf16[128,768]{1,0:T(8,128)(2,1)} %param.26) | copy-start | bytes 589828
  95.3 82.6 %reduce-scatter.9.cloned.1.call-start = ((), (), s32[]{:S(2)}) async-start(), calls=%async_computation.6 | async-start | bytes 1966080 | tf_op jit(solution)/shard_map/reduce_scatter | solution.py:156
  124.3 9.9 %copy-start.4 = (f32[768,768]{1,0:T(8,128)S(1)}, f32[768,768]{1,0:T(8,128)}, u32[]{:S(2)}) copy-start(f32[768,768]{1,0:T(8,128)} %param.34) | copy-start | bytes 7077892
  125.6 52.3 %copy-start.58 = (f32[128]{0:T(128)}, f32[128]{0:T(128)S(1)}, u32[]{:S(2)}) copy-start(f32[128]{0:T(128)S(1)} %broadcast_multiply_fusion) | copy-start | bytes 1540
  125.8 52.1 %copy-start.61 = (f32[128]{0:T(128)}, f32[128]{0:T(128)S(1)}, u32[]{:S(2)}) copy-start(f32[128]{0:T(128)S(1)} %fusion.69) | copy-start | bytes 1540
  134.2 10.4 %copy-start.22 = (bf16[512,768]{1,0:T(8,128)(2,1)}, bf16[512,768]{1,0:T(8,128)(2,1)S(1)}, u32[]{:S(2)}) copy-start(bf16[512,768]{1,0:T(8,128)(2,1)S(1)} %all_gather.13) | copy-start | bytes 2359300
  134.2 10.4 %copy-start.6 = (f32[768,768]{1,0:T(8,128)S(1)}, f32[768,768]{1,0:T(8,128)}, u32[]{:S(2)}) copy-start(f32[768,768]{1,0:T(8,128)} %param.36) | copy-start | bytes 7077892
  134.2 10.4 %copy-start.20 = (bf16[512,768]{1,0:T(8,128)(2,1)S(1)}, bf16[512,768]{1,0:T(8,128)(2,1)}, u32[]{:S(2)}) copy-start(bf16[512,768]{1,0:T(8,128)(2,1)} %all_gather.14) | copy-start | bytes 2359300
  149.2 59.8 %reduce-scatter.7.cloned.1.call-start = ((), (), s32[]{:S(2)}) async-start(), calls=%async_computation.5 | async-start | bytes 1966080 | tf_op jit(solution)/shard_map/reduce_scatter | solution.py:143
  152.9 177.5 %reduce-scatter.11.cloned.1.call-start = ((), (), s32[]{:S(2)}) async-start(), calls=%async_computation.7 | async-start | bytes 1966080 | tf_op jit(solution)/shard_map/reduce_scatter | solution.py:217
  209.1 12.2 %copy-start.14 = (f32[192,768]{1,0:T(8,128)S(1)}, f32[192,768]{1,0:T(8,128)}, u32[]{:S(2)}) copy-start(f32[192,768]{1,0:T(8,128)} %param.32) | copy-start | bytes 1769476
  211.2 10.5 %copy-start.69 = (f32[128]{0:T(128)}, f32[128]{0:T(128)S(1)}, u32[]{:S(2)}) copy-start(f32[128]{0:T(128)S(1)} %negate_multiply_fusion.2) | copy-start | bytes 1540
  221.7 4.8 copy-start.34
  221.7 10.2 %slice-start = ((s8[8388608]{0:T(1024)(128)(4,1)}), s8[4194304]{0:T(1024)(128)(4,1)S(1)}, s32[]{:S(2)}) async-start(s8[8388608]{0:T(1024)(128)(4,1)} %bitcast.66), calls=%async_computation.9 | async-start | bytes 8388608
  226.5 10.7 %copy-start.41 = (bf16[8,24,512]{2,1,0:T(8,128)(2,1)}, bf16[8,24,512]{2,1,0:T(8,128)(2,1)S(1)}, u32[]{:S(2)}) copy-start(bf16[8,24,512]{2,1,0:T(8,128)(2,1)S(1)} %fusion.24) | copy-start | bytes 589828
  226.5 5.5 slice-start.1
  239.9 267.8 %all-reduce.4.cloned.1.call-start = ((), (), s32[]{:S(2)}) async-start(), calls=%async_computation.8 | async-start | bytes 14155776 | tf_op jit(solution)/shard_map/psum | solution.py:227
  239.9 3.7 copy-start.21
  243.6 3.4 copy-start.19
  243.6 3.4 copy-start.38
  243.6 3.4 copy-start.40
  243.6 3.4 copy-start.42
  249.6 8.1 %copy-start.53 = (f32[768]{0:T(1024)S(1)}, f32[768]{0:T(1024)}, u32[]{:S(2)}) copy-start(f32[768]{0:T(1024)} %get-tuple-element.90) | copy-start | bytes 9220
  249.6 8.1 %copy-start.52 = (f32[768]{0:T(1024)S(1)}, f32[768]{0:T(1024)}, u32[]{:S(2)}) copy-start(f32[768]{0:T(1024)} %get-tuple-element.94) | copy-start | bytes 9220
  249.6 8.1 %copy-start.75 = (f32[128]{0:T(128)S(1)}, f32[128]{0:T(128)}, u32[]{:S(2)}) copy-start(f32[128]{0:T(128)} %copy-done.74) | copy-start | bytes 1540
  257.8 48.3 %copy-start.62 = (f32[768]{0:T(1024)S(1)}, f32[768]{0:T(1024)}, u32[]{:S(2)}) copy-start(f32[768]{0:T(1024)} %get-tuple-element.146) | copy-start | bytes 9220
  257.8 72.6 %copy-start.46 = (f32[768]{0:T(1024)S(1)}, f32[768]{0:T(1024)}, u32[]{:S(2)}) copy-start(f32[768]{0:T(1024)} %copy-done.45) | copy-start | bytes 9220
  257.8 72.6 %copy-start.57 = (f32[128]{0:T(128)S(1)}, f32[128]{0:T(128)}, u32[]{:S(2)}) copy-start(f32[128]{0:T(128)} %copy-done.56) | copy-start | bytes 1540
  257.8 73.8 %copy-start.72 = (f32[128]{0:T(128)S(1)}, f32[128]{0:T(128)}, u32[]{:S(2)}) copy-start(f32[128]{0:T(128)} %copy-done.71) | copy-start | bytes 1540
  257.8 73.8 %copy-start.60 = (f32[128]{0:T(128)S(1)}, f32[128]{0:T(128)}, u32[]{:S(2)}) copy-start(f32[128]{0:T(128)} %copy-done.59) | copy-start | bytes 1540
  257.8 75.1 %copy-start.17 = (f32[128,768]{1,0:T(8,128)S(1)}, f32[128,768]{1,0:T(8,128)}, u32[]{:S(2)}) copy-start(f32[128,768]{1,0:T(8,128)} %copy-done.16) | copy-start | bytes 1179652
  257.8 75.1 %copy-start.31 = (bf16[128,768]{1,0:T(8,128)(2,1)S(1)}, bf16[128,768]{1,0:T(8,128)(2,1)}, u32[]{:S(2)}) copy-start(bf16[128,768]{1,0:T(8,128)(2,1)} %param.29) | copy-start | bytes 589828
  257.8 75.1 %copy-start.70 = (f32[128]{0:T(128)S(1)}, f32[128]{0:T(128)}, u32[]{:S(2)}) copy-start(f32[128]{0:T(128)} %copy-done.69) | copy-start | bytes 1540
  507.7 4.7 copy-start.8
  510.4 3.2 copy-start.10
  512.3 21.2 %copy-start.43 = (f32[192,768]{1,0:T(8,128)S(1)}, f32[192,768]{1,0:T(8,128)}, u32[]{:S(2)}) copy-start(f32[192,768]{1,0:T(8,128)} %param.46) | copy-start | bytes 1769476
  512.3 21.2 %copy-start.44 = (f32[192,768]{1,0:T(8,128)S(1)}, f32[192,768]{1,0:T(8,128)}, u32[]{:S(2)}) copy-start(f32[192,768]{1,0:T(8,128)} %param.39) | copy-start | bytes 1769476
  527.5 6.0 %copy-start.15 = (f32[192,768]{1,0:T(8,128)S(1)}, f32[192,768]{1,0:T(8,128)}, u32[]{:S(2)}) copy-start(f32[192,768]{1,0:T(8,128)} %param.32) | copy-start | bytes 1769476
  527.5 6.0 %copy-start.23 = (f32[192,768]{1,0:T(8,128)S(1)}, f32[192,768]{1,0:T(8,128)}, u32[]{:S(2)}) copy-start(f32[192,768]{1,0:T(8,128)} %get-tuple-element.105) | copy-start | bytes 1769476
  527.5 10.1 %copy-start.7 = (f32[768,768]{1,0:T(8,128)S(1)}, f32[768,768]{1,0:T(8,128)}, u32[]{:S(2)}) copy-start(f32[768,768]{1,0:T(8,128)} %param.36) | copy-start | bytes 7077892
  527.5 10.1 %copy-start.9 = (f32[768,768]{1,0:T(8,128)S(1)}, f32[768,768]{1,0:T(8,128)}, u32[]{:S(2)}) copy-start(f32[768,768]{1,0:T(8,128)} %get-tuple-element.106) | copy-start | bytes 7077892
  527.6 10.1 %copy-start.11 = (f32[768,768]{1,0:T(8,128)S(1)}, f32[768,768]{1,0:T(8,128)}, u32[]{:S(2)}) copy-start(f32[768,768]{1,0:T(8,128)} %get-tuple-element.107) | copy-start | bytes 7077892
  527.6 10.1 %copy-start.24 = (f32[768,768]{1,0:T(8,128)S(1)}, f32[768,768]{1,0:T(8,128)}, u32[]{:S(2)}) copy-start(f32[768,768]{1,0:T(8,128)} %param.50) | copy-start | bytes 7077892
  527.6 10.1 %copy-start.25 = (f32[768,768]{1,0:T(8,128)S(1)}, f32[768,768]{1,0:T(8,128)}, u32[]{:S(2)}) copy-start(f32[768,768]{1,0:T(8,128)} %param.43) | copy-start | bytes 7077892
  533.6 2.8 copy-start.55
  533.6 2.8 copy-start.67
  533.6 2.8 copy-start.68
  533.6 3.4 copy-start.48
  533.6 3.4 copy-start.50
  533.7 3.4 copy-start.51
  533.7 4.0 copy-start.5
  (19 other events, 28.6 us)
Sparse Core Ops, SparseCore 0:
  95.4 28.8 reduce-scatter.4
  149.4 28.5 reduce-scatter.8
  181.0 27.9 reduce-scatter.6
  240.0 28.6 reduce-scatter.10
  274.1 233.5 all-reduce.3
where the time goes:
time: 555 us; the launch traced here: 553 us
  waiting for transfers between devices  206 us (37%)
  matrix products  146 us (26%)
  blocking collectives  106 us (19%)
  other arithmetic  45.9 us (8%)
  local copies, waits for them, and re-layouts  27.7 us (5%)
  between operations  21.9 us (4%)
    psum x1, waiting for transfers between devices, per_device(): lax.psum((qkv_grad, proj_grad, pair_grad, in_grad, bias_grad, out_grad),...  133 us
    dot_general x1, matrix products, attend_back(): jnp.einsum('hij,ijk->hk', grad_score, gauss, preferred_element_type=jnp.f...  48.2 us
    dot_general x1, matrix products, block_scores(): jnp.einsum('ijk,hk->hij', gauss, pair_low, preferred_element_type=jnp.flo...  47.8 us
    psum x1, blocking collectives, per_device(): norm_grad = lax.psum(norm_grad, ('dp', 'mp'))  39.9 us
    reduce_scatter x1, waiting for transfers between devices, per_device(): lax.psum_scatter(jnp.dot(piece, out_low, preferred_element_type=jnp.float...  28.8 us
    reduce_scatter x1, waiting for transfers between devices, per_device(): lax.psum_scatter(jnp.dot(piece, in_low, preferred_element_type=jnp.float3...  24.9 us
    psum x1, blocking collectives, per_device(): lax.psum((qkv_grad, proj_grad, pair_grad, in_grad, bias_grad, out_grad),...  23.1 us
    reduce_scatter x1, waiting for transfers between devices, per_device(): lax.psum_scatter(jnp.dot(piece, proj_low, preferred_element_type=jnp.floa...  19.7 us
  transfers between devices with their start and end apart: 5, of which 4 were waited for; matrix products, arithmetic and copies ran while one was open for 14% of the time, Pallas kernels for 0%

commit v1 on v0

v1 whole, which is shorter than its diff:
```python
import functools
import math

import jax
import jax.numpy as jnp
from jax import lax
from jax.experimental import pallas as pl
from jax.experimental.pallas import tpu as pltpu
from jax.sharding import PartitionSpec as P

ln_eps = 1e-05
beta_one = 0.9
beta_two = 0.999
adam_eps = 1e-08
clip_level = 1.0
F32, BF16 = jnp.float32, jnp.bfloat16
NT = (((1,), (1,)), ((), ()))
TN = (((0,), (0,)), ((), ()))
KERN = 128
LANE = 128
SUB = 8
CHUNK = 32
KS = math.sqrt(0.5 * math.log2(math.e))
UNIT = KS / (12.8 / KERN)

def head_mask(heads, inner):
    rows = lax.broadcasted_iota(jnp.int32, (SUB, inner), 0)
    cols = lax.broadcasted_iota(jnp.int32, (SUB, inner), 1)
    hd = inner // heads
    return ((cols >= rows * hd) & (cols < (rows + 1) * hd)).astype(F32)

def setup_pairs(len_ref, b, coords_ref, dist, labs, labr, span, mols):
    pts = coords_ref[...]
    cols = jnp.transpose(jnp.concatenate([pts, jnp.zeros((5, span), F32)], 0))
    acc = None
    for a in range(3):
        d = cols[:, a:a + 1] - pts[a:a + 1, :]
        acc = d * d if acc is None else acc + d * d
    dist[...] = jnp.sqrt(acc) * UNIT
    rows = lax.broadcasted_iota(jnp.int32, (span, LANE), 0)
    lanes = lax.broadcasted_iota(jnp.int32, (SUB, span), 1)
    lr = jnp.zeros((span, LANE), jnp.int32)
    lc = jnp.zeros((SUB, span), jnp.int32)
    end = jnp.int32(0)
    for m in range(mols):
        end = end + len_ref[b, m]
        lr = lr + (rows >= end).astype(jnp.int32)
        lc = lc + (lanes >= end).astype(jnp.int32)
    labs[...] = lr
    labr[...] = lc

def tile_range(len_ref, b, first, last, span, mols):
    lo = jnp.int32(0); hi = jnp.int32(span); end = jnp.int32(0)
    for m in range(mols):
        end = end + len_ref[b, m]
        lo = jnp.where(end <= first, end, lo)
        hi = jnp.where((end > last) & (end < hi), end, hi)
    return lo // LANE, (hi + LANE - 1) // LANE

def gauss_tile(drow):
    sub = lax.broadcasted_iota(jnp.int32, (SUB, LANE), 0).astype(F32) * KS
    base = drow - sub
    parts = []
    for c in range(KERN // SUB):
        t = base - (KS * SUB * c)
        parts.append(jnp.exp2(-(t * t)))
    return jnp.concatenate(parts, 0).astype(BF16)

def expand(rows, mask):
    n, w = rows.shape
    return (rows[:, None, :] * mask[None]).reshape(n * SUB, w).astype(BF16)

def collapse(wide, mask):
    n, w = wide.shape
    return jnp.sum(wide.reshape(n // SUB, SUB, w) * mask[None], axis=1)

def fwd_kernel(heads, mols, len_ref, coords_ref, q_ref, k_ref, v_ref, w_ref, o_ref, p_ref, dist, labs, labr, sc, qf):
    span, inner = q_ref.shape
    b = pl.program_id(0)
    scale = 1.0 / math.sqrt(inner // heads)
    setup_pairs(len_ref, b, coords_ref, dist, labs, labr, span, mols)
    mask = head_mask(heads, inner)
    qf[...] = q_ref[...].astype(F32)
    kb = k_ref[...]; vb = v_ref[...]; wb = w_ref[...]

    def chunk(ci, carry):
        sc[...] = jnp.full(sc.shape, -1e30, F32)
        def group(g, carry):
            i0 = pl.multiple_of(ci * CHUNK + g * SUB, SUB)
            lo, hi = tile_range(len_ref, b, i0, i0 + SUB - 1, span, mols)
            def tile(jt, carry):
                j0 = pl.multiple_of(jt * LANE, LANE)
                lab = labr[:, pl.ds(j0, LANE)]
                dblk = dist[pl.ds(i0, SUB), pl.ds(j0, LANE)]
                lblk = labs[pl.ds(i0, SUB), :]
                for r in range(SUB):
                    drow = jnp.broadcast_to(dblk[r:r + 1], (SUB, LANE))
                    li = jnp.broadcast_to(lblk[r:r + 1], (SUB, LANE))
                    bias = jnp.dot(wb, gauss_tile(drow), preferred_element_type=F32)
                    row0 = pl.multiple_of((g * SUB + r) * SUB, SUB)
                    sc[pl.ds(row0, SUB), pl.ds(j0, LANE)] = jnp.where(li == lab, bias, -1e30)
                return carry
            return lax.fori_loop(lo, hi, tile, carry)
        lax.fori_loop(0, CHUNK // SUB, group, 0)
        c0 = pl.multiple_of(ci * CHUNK, CHUNK)
        qt = expand(qf[pl.ds(c0, CHUNK), :], mask)
        s = lax.dot_general(qt, kb, NT, preferred_element_type=F32)
        bias = sc[...]
        s = s * scale + bias
        top = jnp.max(s, axis=-1, keepdims=True)
        e = jnp.exp(s - top)
        pr = (e / jnp.sum(e, axis=-1, keepdims=True)).astype(BF16)
        p_ref[pl.ds(pl.multiple_of(ci * CHUNK * SUB, CHUNK * SUB), CHUNK * SUB), :] = pr
        ow = jnp.dot(pr, vb, preferred_element_type=F32)
        o_ref[pl.ds(c0, CHUNK), :] = collapse(ow, mask).astype(BF16)
        return carry
    lax.fori_loop(0, span // CHUNK, chunk, 0)

def attention(qkv, coords, lengths, pair_low, heads):
    _, rows, inner = qkv.shape
    blocks, mols = lengths.shape
    span = rows // blocks
    w = jnp.pad(pair_low, ((0, SUB - heads), (0, 0)))
    part = lambda s: pl.BlockSpec((None, span, inner), lambda b, *_: (s, b, 0))
    return pl.pallas_call(
        functools.partial(fwd_kernel, heads, mols),
        out_shape=(jax.ShapeDtypeStruct((rows, inner), BF16), jax.ShapeDtypeStruct((rows * SUB, span), BF16)),
        grid_spec=pltpu.PrefetchScalarGridSpec(
            num_scalar_prefetch=1, grid=(blocks,),
            in_specs=[pl.BlockSpec((3, span), lambda b, *_: (0, b)), part(0), part(1), part(2),
                      pl.BlockSpec((SUB, KERN), lambda b, *_: (0, 0))],
            out_specs=[pl.BlockSpec((span, inner), lambda b, *_: (b, 0)),
                       pl.BlockSpec((span * SUB, span), lambda b, *_: (b, 0))],
            scratch_shapes=[pltpu.VMEM((span, span), F32), pltpu.VMEM((span, LANE), jnp.int32),
                            pltpu.VMEM((SUB, span), jnp.int32), pltpu.VMEM((CHUNK * SUB, span), F32),
                            pltpu.VMEM((span, inner), F32)]),
        name="attend",
    )(lengths, coords, qkv, qkv, qkv, w)

def bwd_kernel(heads, mols, len_ref, coords_ref, q_ref, k_ref, v_ref, do_ref, p_ref, dqkv_ref, pg_ref,
               dist, labs, labr, ds, qf, dof, dkt, dvt):
    span, inner = q_ref.shape
    b = pl.program_id(0)
    scale = 1.0 / math.sqrt(inner // heads)
    setup_pairs(len_ref, b, coords_ref, dist, labs, labr, span, mols)
    mask = head_mask(heads, inner)
    qf[...] = q_ref[...].astype(F32)
    dof[...] = do_ref[...].astype(F32)
    kb = k_ref[...]; vb = v_ref[...]
    dkt[...] = jnp.zeros_like(dkt); dvt[...] = jnp.zeros_like(dvt)
    @pl.when(b == 0)
    def _():
        pg_ref[...] = jnp.zeros_like(pg_ref)

    def chunk(ci, carry):
        c0 = pl.multiple_of(ci * CHUNK, CHUNK)
        r0 = pl.multiple_of(ci * CHUNK * SUB, CHUNK * SUB)
        qt = expand(qf[pl.ds(c0, CHUNK), :], mask)
        dot = expand(dof[pl.ds(c0, CHUNK), :], mask)
        pb = p_ref[pl.ds(r0, CHUNK * SUB), :]
        pf = pb.astype(F32)
        dp = lax.dot_general(dot, vb, NT, preferred_element_type=F32)
        rowdot = jnp.sum(pf * dp, axis=-1, keepdims=True)
        dsf = pf * (dp - rowdot)
        dsb = dsf.astype(BF16)
        ds[...] = dsf
        dqkv_ref[0, pl.ds(c0, CHUNK), :] = (collapse(jnp.dot(dsb, kb, preferred_element_type=F32), mask) * scale).astype(BF16)
        dkt[...] += lax.dot_general(qt, dsb, TN, preferred_element_type=F32)
        dvt[...] += lax.dot_general(dot, pb, TN, preferred_element_type=F32)

        def group(g, carry):
            i0 = pl.multiple_of(ci * CHUNK + g * SUB, SUB)
            lo, hi = tile_range(len_ref, b, i0, i0 + SUB - 1, span, mols)
            def tile(jt, acc):
                j0 = pl.multiple_of(jt * LANE, LANE)
                dblk = dist[pl.ds(i0, SUB), pl.ds(j0, LANE)]
                for r in range(SUB):
                    drow = jnp.broadcast_to(dblk[r:r + 1], (SUB, LANE))
                    row0 = pl.multiple_of((g * SUB + r) * SUB, SUB)
                    d = ds[pl.ds(row0, SUB), pl.ds(j0, LANE)].astype(BF16)
                    acc = acc + lax.dot_general(d, gauss_tile(drow), NT, preferred_element_type=F32)
                return acc
            return lax.fori_loop(lo, hi, tile, carry)
        return lax.fori_loop(0, CHUNK // SUB, group, carry)
    pg_ref[...] += lax.fori_loop(0, span // CHUNK, chunk, jnp.zeros((SUB, KERN), F32))
    dqkv_ref[1] = jnp.transpose(dkt[...] * scale).astype(BF16)
    dqkv_ref[2] = jnp.transpose(dvt[...]).astype(BF16)

def attention_back(qkv, grad_heads, probs, coords, lengths, heads):
    _, rows, inner = qkv.shape
    blocks, mols = lengths.shape
    span = rows // blocks
    part = lambda s: pl.BlockSpec((None, span, inner), lambda b, *_: (s, b, 0))
    return pl.pallas_call(
        functools.partial(bwd_kernel, heads, mols),
        out_shape=(jax.ShapeDtypeStruct((3, rows, inner), BF16), jax.ShapeDtypeStruct((SUB, KERN), F32)),
        grid_spec=pltpu.PrefetchScalarGridSpec(
            num_scalar_prefetch=1, grid=(blocks,),
            in_specs=[pl.BlockSpec((3, span), lambda b, *_: (0, b)), part(0), part(1), part(2),
                      pl.BlockSpec((span, inner), lambda b, *_: (b, 0)),
                      pl.BlockSpec((span * SUB, span), lambda b, *_: (b, 0))],
            out_specs=[pl.BlockSpec((3, span, inner), lambda b, *_: (0, b, 0)),
                       pl.BlockSpec((SUB, KERN), lambda b, *_: (0, 0))],
            scratch_shapes=[pltpu.VMEM((span, span), F32), pltpu.VMEM((span, LANE), jnp.int32),
                            pltpu.VMEM((SUB, span), jnp.int32), pltpu.VMEM((CHUNK * SUB, span), F32),
                            pltpu.VMEM((span, inner), F32), pltpu.VMEM((span, inner), F32),
                            pltpu.VMEM((inner, span), F32), pltpu.VMEM((inner, span), F32)]),
        name="attend_back",
    )(lengths, coords, qkv, qkv, qkv, grad_heads, probs)


MESH = pl.DeviceIdType.MESH
NN = (((1,), (0,)), ((), ()))
VM = pl.BlockSpec(memory_space=pltpu.VMEM)
HBM = pl.BlockSpec(memory_space=pl.ANY)
DMA = pltpu.SemaphoreType.DMA


def mm(a, b, dims=NN):
    return lax.dot_general(a, b, dims, preferred_element_type=F32)


def remote(src, dst, send, recv, axis, target):
    return pltpu.make_async_remote_copy(
        src_ref=src, dst_ref=dst, send_sem=send, recv_sem=recv,
        device_id={axis: target}, device_id_type=MESH)


def greet(sizes):
    barrier = pltpu.get_barrier_semaphore()
    total = 0
    for axis, size in sizes.items():
        me = lax.axis_index(axis)
        for k in range(1, size):
            pl.semaphore_signal(barrier, inc=1, device_id={axis: lax.rem(me + k, size)}, device_id_type=MESH)
        total += size - 1
    pl.semaphore_wait(barrier, total)


class Seat:
    def __init__(self, n):
        self.n, self.nx = n, n // 2
        self.me = lax.axis_index("mp")
        self.core = lax.rem(self.me, 2)
        self.x = self.me // 2
        self.sib = self.me + 1 - 2 * self.core

    def chip(self, k):
        return lax.rem(self.x + 1 + k, self.nx)

    def source(self, k):
        return lax.rem(self.x + self.nx - 1 - k, self.nx)


def scatter_scratch(n, rows, width):
    nx = n // 2
    buf = lambda m: pltpu.VMEM((m, rows, width), BF16)
    return [buf(nx), buf(nx), buf(max(nx - 1, 1)), buf(max(nx - 1, 1)), DMA((nx,)), DMA((nx,)),
            DMA((max(nx - 1, 1),)), DMA((max(nx - 1, 1),))]


class Scatter:
    def __init__(self, seat, scratch):
        self.seat = seat
        self.out1, self.in1, self.out2, self.in2, self.s1, self.r1, self.s2, self.r2 = scratch

    def first(self, k):
        return remote(self.out1.at[k], self.in1.at[k], self.s1.at[k], self.r1.at[k], "mp", self.seat.sib)

    def second(self, k):
        target = self.seat.chip(k) * 2 + self.seat.core
        return remote(self.out2.at[k], self.in2.at[k], self.s2.at[k], self.r2.at[k], "mp", target)

    def push(self, block):
        for k in range(self.seat.nx):
            self.out1[k] = block(self.seat.chip(k) * 2 + 1 - self.seat.core).astype(BF16)
            self.first(k).start()

    def pass_on(self, block):
        seat = self.seat
        parts = [block(seat.chip(k) * 2 + seat.core) for k in range(seat.nx)]
        for k in range(seat.nx):
            self.first(k).wait_recv()
            whole = parts[k] + self.in1[k].astype(F32)
            if k < seat.nx - 1:
                self.out2[k] = whole.astype(BF16)
                self.second(k).start()
        return whole

    def finish(self, whole):
        for k in range(self.seat.nx - 1):
            self.second(k).wait_recv()
            whole = whole + self.in2[k].astype(F32)
        return whole

    def drain(self):
        for k in range(self.seat.nx):
            self.first(k).wait_send()
        for k in range(self.seat.nx - 1):
            self.second(k).wait_send()


def gather_scratch(n):
    nx = n // 2
    return [DMA((max(nx - 1, 1),)), DMA((max(nx - 1, 1),)), DMA((nx,)), DMA((nx,))]


class Gather:
    def __init__(self, seat, rows, scratch):
        self.seat, self.rows = seat, rows
        self.sx, self.rx, self.sc, self.rc = scratch

    def across(self, k):
        r = self.rows.at[self.seat.me]
        return remote(r, r, self.sx.at[k], self.rx.at[k], "mp", self.seat.chip(k) * 2 + self.seat.core)

    def along(self, k):
        chip = self.seat.x if k == self.seat.nx - 1 else self.seat.source(k)
        r = self.rows.at[chip * 2 + self.seat.core]
        return remote(r, r, self.sc.at[k], self.rc.at[k], "mp", self.seat.sib)

    def start(self):
        for k in range(self.seat.nx - 1):
            self.across(k).start()
        self.along(self.seat.nx - 1).start()

    def forward(self):
        for k in range(self.seat.nx - 1):
            self.across(k).wait_recv()
            self.along(k).start()

    def finish(self):
        for k in range(self.seat.nx):
            self.along(k).wait_recv()

    def drain(self):
        for k in range(self.seat.nx - 1):
            self.across(k).wait_send()
        for k in range(self.seat.nx):
            self.along(k).wait_send()


def centre(rows):
    c = rows - jnp.mean(rows, axis=-1, keepdims=True)
    r = lax.rsqrt(jnp.mean(c * c, axis=-1, keepdims=True) + ln_eps)
    return c * r, r


def norm_back(rows, gain, e):
    vhat, r = centre(rows)
    ge = e * gain
    dv = r * (ge - jnp.mean(ge, axis=-1, keepdims=True) - vhat * jnp.mean(ge * vhat, axis=-1, keepdims=True))
    return dv, jnp.sum(e * vhat, axis=0, keepdims=True), jnp.sum(e, axis=0, keepdims=True)


def enter_kernel(n, x_ref, dy_ref, np_ref, w_hbm, h_ref, dyall_ref, qkv_ref, w32, wsem, *sems):
    seat = Seat(n)
    load = pltpu.make_async_copy(w_hbm, w32, wsem)
    load.start()
    greet({"mp": n})
    vhat, _ = centre(x_ref[...].astype(F32))
    h_ref[seat.me] = (vhat * np_ref[0:1] + np_ref[1:2]).astype(BF16)
    dyall_ref[seat.me] = dy_ref[...]
    gh = Gather(seat, h_ref, sems[:4])
    gd = Gather(seat, dyall_ref, sems[4:])
    gh.start()
    load.wait()
    gh.forward()
    gd.start()
    gh.finish()
    rows = h_ref.shape[1]
    for s in range(3):
        w = w32[s].astype(BF16)

        def block(b, carry):
            r0 = pl.multiple_of(b * rows, rows)
            qkv_ref[s, pl.ds(r0, rows), :] = mm(h_ref[b], w, NT).astype(BF16)
            return carry

        lax.fori_loop(0, n, block, 0)
    gd.forward()
    gd.finish()
    gh.drain()
    gd.drain()


def enter(n, x, dy, params, qkv_weight):
    rows, width = x.shape
    _, inner, _ = qkv_weight.shape
    return pl.pallas_call(
        functools.partial(enter_kernel, n),
        out_shape=(jax.ShapeDtypeStruct((n, rows, width), BF16), jax.ShapeDtypeStruct((n, rows, width), BF16),
                   jax.ShapeDtypeStruct((3, n * rows, inner), BF16)),
        in_specs=[VM, VM, VM, HBM], out_specs=[VM, VM, VM],
        scratch_shapes=[pltpu.VMEM(qkv_weight.shape, F32), DMA, *gather_scratch(n), *gather_scratch(n)],
        compiler_params=pltpu.CompilerParams(collective_id=0, has_side_effects=True),
        name="enter",
    )(x, dy, params, qkv_weight)


def middle_kernel(n, x_ref, dy_ref, dyall_ref, o_ref, np_ref, bias_ref, pw_hbm, iw_hbm, ow_hbm,
                  block_ref, mid_ref, do_ref, og_ref, ig_ref, pg_ref, bg_ref, small_ref,
                  pw32, iw32, ow32, pw, iw, ow, h2, da, act, dpre, dact, wsem, *rest):
    seat = Seat(n)
    rows, width = x_ref.shape
    loads = [pltpu.make_async_copy(a, b, wsem.at[i])
             for i, (a, b) in enumerate([(pw_hbm, pw32), (ow_hbm, ow32), (iw_hbm, iw32)])]
    for c in loads:
        c.start()
    scat = [Scatter(seat, rest[8 * i:8 * i + 8]) for i in range(3)]
    gath = [Gather(seat, r, rest[24 + 4 * i:28 + 4 * i]) for i, r in enumerate((h2, da))]
    greet({"mp": n})
    at = lambda b: pl.ds(pl.multiple_of(b * rows, rows), rows)

    loads[0].wait()
    pw[...] = pw32[...].astype(BF16)
    attn_block = lambda b: mm(o_ref[at(b), :], pw[...])
    scat[0].push(attn_block)
    loads[1].wait()
    ow[...] = ow32[...].astype(BF16)
    whole = scat[0].pass_on(attn_block)
    loads[2].wait()
    iw[...] = iw32[...].astype(BF16)

    def back_act(b, carry):
        dact[b] = mm(dyall_ref[b], ow[...], NT)
        return carry

    lax.fori_loop(0, n, back_act, 0)
    mid = x_ref[...].astype(F32) + scat[0].finish(whole)
    vhat, _ = centre(mid)
    h2[seat.me] = (vhat * np_ref[2:3] + np_ref[3:4]).astype(BF16)
    mid_ref[...] = mid
    gath[0].start()
    gath[0].forward()
    gath[0].finish()

    bg_ref[...] = jnp.zeros_like(bg_ref)
    bias = bias_ref[...].astype(BF16).astype(F32)

    def feed_block(b):
        pre = mm(h2[b], iw[...], NT) + bias
        phi = 0.5 + 0.5 * lax.erf(pre * math.sqrt(0.5))
        act[b] = (pre * phi).astype(BF16)
        slope = phi + pre * (jnp.exp(-0.5 * pre * pre) * (1.0 / math.sqrt(2.0 * math.pi)))
        d = (dact[b] * slope).astype(BF16)
        dpre[b] = d
        bg_ref[...] += jnp.sum(d.astype(F32), axis=0, keepdims=True)
        return mm(d, iw[...])

    scat[1].push(feed_block)
    whole = scat[1].pass_on(feed_block)
    out_block = lambda b: mm(act[b], ow[...])
    scat[2].push(out_block)
    dh2 = scat[1].finish(whole)
    dv, gain, shift = norm_back(mid_ref[...], np_ref[2:3], dh2)
    dy = dy_ref[...].astype(F32)
    dx1 = dy + dv
    da[seat.me] = dx1.astype(BF16)
    gath[1].start()
    small_ref[...] = jnp.concatenate(
        [gain, shift, jnp.sum(dy, axis=0, keepdims=True), jnp.zeros((5, width), F32)], 0)
    whole = scat[2].pass_on(out_block)
    gath[1].forward()

    hidden = iw.shape[0]
    step = LANE if hidden % LANE == 0 else hidden

    def grads(i, carry):
        c0 = pl.multiple_of(i * step, step)
        acc_o = jnp.zeros((step, width), F32)
        acc_i = jnp.zeros((step, width), F32)
        for b in range(n):
            acc_o += mm(act[b, :, pl.ds(c0, step)], dyall_ref[b], TN)
            acc_i += mm(dpre[b, :, pl.ds(c0, step)], h2[b], TN)
        og_ref[pl.ds(c0, step), :] = acc_o
        ig_ref[pl.ds(c0, step), :] = acc_i
        return carry

    lax.fori_loop(0, hidden // step, grads, 0)
    block_ref[...] = mid_ref[...] + scat[2].finish(whole) + np_ref[4:5]
    mid_ref[...] = dx1
    gath[1].finish()

    def heads_block(b, carry):
        do_ref[at(b), :] = mm(da[b], pw[...], NT).astype(BF16)
        pg_ref[...] += mm(o_ref[at(b), :], da[b], TN)
        return carry

    pg_ref[...] = jnp.zeros_like(pg_ref)
    lax.fori_loop(0, n, heads_block, 0)
    for c in scat + gath:
        c.drain()


def middle(n, x, dy, dy_all, o, params, bias, proj_weight, in_weight, out_weight):
    rows, width = x.shape
    hidden = in_weight.shape[0]
    inner = proj_weight.shape[0]
    f = lambda *s: jax.ShapeDtypeStruct(s, F32)
    return pl.pallas_call(
        functools.partial(middle_kernel, n),
        out_shape=(f(rows, width), f(rows, width), jax.ShapeDtypeStruct((n * rows, inner), BF16),
                   f(hidden, width), f(hidden, width), f(inner, width), f(1, hidden), f(8, width)),
        in_specs=[VM] * 6 + [HBM] * 3, out_specs=[VM] * 8,
        scratch_shapes=[pltpu.VMEM((inner, width), F32), pltpu.VMEM((hidden, width), F32),
                        pltpu.VMEM((hidden, width), F32), pltpu.VMEM((inner, width), BF16),
                        pltpu.VMEM((hidden, width), BF16), pltpu.VMEM((hidden, width), BF16),
                        pltpu.VMEM((n, rows, width), BF16), pltpu.VMEM((n, rows, width), BF16),
                        pltpu.VMEM((n, rows, hidden), BF16), pltpu.VMEM((n, rows, hidden), BF16),
                        pltpu.VMEM((n, rows, hidden), F32), DMA((3,)),
                        *[s for _ in range(3) for s in scatter_scratch(n, rows, width)],
                        *gather_scratch(n), *gather_scratch(n)],
        compiler_params=pltpu.CompilerParams(collective_id=1, has_side_effects=True, vmem_limit_bytes=60 << 20),
        name="middle",
    )(x, dy, dy_all, o, params, bias, proj_weight, in_weight, out_weight)


class Grid:
    def __init__(self, ny, nz):
        self.ny, self.nz = ny, nz
        self.me = lax.axis_index("dp")
        self.z, self.y = self.me // ny, lax.rem(self.me, ny)

    def yto(self, k):
        return lax.rem(self.y + 1 + k, self.ny)

    def yfrom(self, k):
        return lax.rem(self.y + self.ny - 1 - k, self.ny)

    def zto(self, k):
        return lax.rem(self.z + 1 + k, self.nz)

    def zfrom(self, k):
        return lax.rem(self.z + self.nz - 1 - k, self.nz)


def sum_scratch(ny, nz, chunk, width):
    y, z = max(ny - 1, 1), max(nz - 1, 1)
    return [pltpu.VMEM((y, nz, chunk, width), BF16), pltpu.VMEM((y, nz, chunk, width), BF16),
            pltpu.VMEM((z, chunk, width), BF16), pltpu.VMEM((z, chunk, width), BF16),
            DMA((y,)), DMA((y,)), DMA((z,)), DMA((z,)), DMA((z,)), DMA((z,)), DMA((nz, y)), DMA((nz, y))]


class Sum:
    def __init__(self, grid, grad, result, scratch):
        self.grid, self.grad, self.result = grid, grad, result
        (self.oa, self.ia, self.ob, self.ib, self.sa, self.ra, self.sb, self.rb,
         self.sz, self.rz, self.sy, self.ry) = scratch
        self.chunk = result.shape[1]

    def piece(self, z, y):
        start = pl.multiple_of((z * self.grid.ny + y) * self.chunk, 8)
        return self.grad[pl.ds(start, self.chunk), :]

    def copy_y(self, k):
        g = self.grid
        return remote(self.oa.at[k], self.ia.at[k], self.sa.at[k], self.ra.at[k], "dp", g.z * g.ny + g.yto(k))

    def copy_z(self, k):
        g = self.grid
        return remote(self.ob.at[k], self.ib.at[k], self.sb.at[k], self.rb.at[k], "dp", g.zto(k) * g.ny + g.y)

    def push(self):
        g = self.grid
        for k in range(g.ny - 1):
            for z in range(g.nz):
                self.oa[k, z] = self.piece(z, g.yto(k)).astype(BF16)
            self.copy_y(k).start()

    def pass_on(self):
        g = self.grid
        for k in range(g.ny - 1):
            self.copy_y(k).wait_recv()
        for k in range(g.nz):
            z = g.zto(k)
            whole = self.piece(z, g.y)
            for j in range(g.ny - 1):
                whole = whole + self.ia[j, z].astype(F32)
            if k < g.nz - 1:
                self.ob[k] = whole.astype(BF16)
                self.copy_z(k).start()
        self.own = whole

    def finish(self):
        for k in range(self.grid.nz - 1):
            self.copy_z(k).wait_recv()
            self.own = self.own + self.ib[k].astype(F32)
        self.result[self.grid.me] = self.own.astype(BF16)
        for k in range(self.grid.nz - 1):
            self.back_z(k).start()
        for k in range(self.grid.ny - 1):
            self.back_y(self.grid.nz - 1, k).start()
        return self.own

    def back_z(self, k):
        g = self.grid
        r = self.result.at[g.me]
        return remote(r, r, self.sz.at[k], self.rz.at[k], "dp", g.zto(k) * g.ny + g.y)

    def back_y(self, k, j):
        g = self.grid
        z = g.z if k == g.nz - 1 else g.zfrom(k)
        r = self.result.at[z * g.ny + g.y]
        return remote(r, r, self.sy.at[k, j], self.ry.at[k, j], "dp", g.z * g.ny + g.yto(j))

    def forward(self):
        g = self.grid
        for k in range(g.nz - 1):
            self.back_z(k).wait_recv()
            for j in range(g.ny - 1):
                self.back_y(k, j).start()

    def close(self):
        g = self.grid
        for k in range(g.nz):
            for j in range(g.ny - 1):
                self.back_y(k, j).wait_recv()
        for k in range(g.ny - 1):
            self.copy_y(k).wait_send()
        for k in range(g.nz - 1):
            self.copy_z(k).wait_send()
            self.back_z(k).wait_send()
        for k in range(g.nz):
            for j in range(g.ny - 1):
                self.back_y(k, j).wait_send()


class Share:
    def __init__(self, axis, slots, send, recv):
        self.axis, self.slots, self.send, self.recv = axis, slots, send, recv
        self.size = slots.shape[0]
        self.me = lax.axis_index(axis)

    def copy(self, k):
        r = self.slots.at[self.me]
        return remote(r, r, self.send.at[k], self.recv.at[k], self.axis, lax.rem(self.me + 1 + k, self.size))

    def start(self, value):
        self.slots[self.me] = value
        for k in range(self.size - 1):
            self.copy(k).start()

    def total(self):
        for k in range(self.size - 1):
            self.copy(k).wait_recv()
        out = self.slots[0]
        for i in range(1, self.size):
            out = out + self.slots[i]
        return out

    def drain(self):
        for k in range(self.size - 1):
            self.copy(k).wait_send()


def share_scratch(size, rows, width):
    return [pltpu.VMEM((size, rows, width), F32), DMA((max(size - 1, 1),)), DMA((max(size - 1, 1),))]


def square(v):
    return jnp.sum(jnp.sum(v * v, axis=1, keepdims=True), axis=0, keepdims=True)


def leave_kernel(n, ny, nz, x_ref, dx_ref, np_ref, dqkv_ref, h_ref, og_ref, ig_ref, pg_ref, bg_ref, pair_ref,
                 mid_small_ref, w_hbm, gi_ref, so_ref, si_ref, sp_ref, sq_ref, small_ref, bias_ref, pairs_ref, norm_ref,
                 w32, w, qg, wsem, *rest):
    seat, grid = Seat(n), Grid(ny, nz)
    rows, width = x_ref.shape
    inner = w.shape[1]
    load = pltpu.make_async_copy(w_hbm, w32, wsem)
    load.start()
    scat = Scatter(seat, rest[:8])
    sums = [Sum(grid, g, r, rest[8 + 12 * i:20 + 12 * i])
            for i, (g, r) in enumerate([(og_ref, so_ref), (ig_ref, si_ref), (pg_ref, sp_ref), (qg, sq_ref)])]
    shares = [Share(a, *rest[56 + 3 * i:59 + 3 * i]) for i, a in enumerate(("mp", "dp", "dp", "dp", "mp", "dp"))]
    small_mp, small_dp, bias_dp, pair_dp, sq_mp, sq_dp = shares
    greet({"mp": n, "dp": ny * nz})
    at = lambda b: pl.ds(pl.multiple_of(b * rows, rows), rows)

    load.wait()
    w[...] = w32[...].astype(BF16)

    def first_block(b):
        return sum(mm(dqkv_ref[s, at(b), :], w[s]) for s in range(3))

    scat.push(first_block)
    whole = scat.pass_on(first_block)
    for s in sums[:3]:
        s.push()
    bias_dp.start(jnp.broadcast_to(bg_ref[...], bias_dp.slots.shape[1:]))
    pair_dp.start(pair_ref[...])
    for s in range(3):
        acc = jnp.zeros((inner, width), F32)
        for b in range(n):
            acc = acc + mm(dqkv_ref[s, at(b), :], h_ref[b], TN)
        qg[pl.ds(s * inner, inner), :] = acc
    sums[3].push()
    dh1 = scat.finish(whole)
    dv, gain, shift = norm_back(x_ref[...].astype(F32), np_ref[0:1], dh1)
    gi_ref[...] = dx_ref[...] + dv
    small_mp.start(jnp.concatenate([gain, shift, mid_small_ref[0:6]], 0))
    sums[0].pass_on()
    small_dp.start(small_mp.total())
    sums[1].pass_on()
    squares = square(sums[0].finish())
    sums[2].pass_on()
    sums[3].pass_on()
    squares = squares + square(sums[1].finish())
    squares = squares + square(sums[2].finish())
    squares = squares + square(sums[3].finish())
    small = small_dp.total()
    small_ref[...] = small
    bias = bias_dp.total()
    bias_ref[...] = bias
    pairs = pair_dp.total()
    pairs_ref[...] = pairs
    row = lax.broadcasted_iota(jnp.int32, (8, LANE), 0)
    local = square(bias[0:1]) + square(pairs)
    sq_mp.start(jnp.where(row == 0, squares, jnp.where(row == 1, local, 0.0)))
    sums[0].forward()
    sq_dp.start(sq_mp.total())
    for s in sums[1:]:
        s.forward()
    norm_ref[...] = sq_dp.total()[0:1] + sq_dp.slots[0, 1:2] + square(small)
    for s in sums:
        s.close()
    scat.drain()
    for s in shares:
        s.drain()


def leave(n, ny, nz, x, dx, params, dqkv, h, grads, bias_grad, pair_grad, small, qkv_weight):
    rows, width = x.shape
    inner = qkv_weight.shape[1]
    ndp = ny * nz
    tall = [g.shape[0] for g in grads] + [3 * inner]
    hidden = bias_grad.shape[1]
    f = lambda *s: jax.ShapeDtypeStruct(s, F32)
    return pl.pallas_call(
        functools.partial(leave_kernel, n, ny, nz),
        out_shape=(f(rows, width), *[jax.ShapeDtypeStruct((ndp, t // ndp, width), BF16) for t in tall],
                   f(8, width), f(8, hidden), f(8, LANE), f(1, LANE)),
        in_specs=[VM] * 11 + [HBM], out_specs=[VM] * 9,
        scratch_shapes=[pltpu.VMEM(qkv_weight.shape, F32), pltpu.VMEM(qkv_weight.shape, BF16),
                        pltpu.VMEM((3 * inner, width), F32), DMA, *scatter_scratch(n, rows, width),
                        *[s for t in tall for s in sum_scratch(ny, nz, t // ndp, width)],
                        *share_scratch(n, 8, width), *share_scratch(ndp, 8, width), *share_scratch(ndp, 8, hidden),
                        *share_scratch(ndp, 8, LANE), *share_scratch(n, 8, LANE), *share_scratch(ndp, 8, LANE)],
        compiler_params=pltpu.CompilerParams(collective_id=2, has_side_effects=True, vmem_limit_bytes=60 << 20),
        name="leave",
    )(x, dx, params, dqkv, h, *grads, bias_grad, pair_grad, small, qkv_weight)


def leave_plain(n, x, dx, params, dqkv, h, grads, bias_grad, pair_grad, small, qkv_weight):
    part = sum(mm(dqkv[s], qkv_weight[s].astype(BF16)) for s in range(3))
    dh1 = lax.psum_scatter(part, "mp", scatter_dimension=0, tiled=True)
    dv, gain, shift = norm_back(x.astype(F32), params[0:1], dh1)
    hh = h.reshape(-1, h.shape[-1])
    qg = jnp.concatenate([mm(dqkv[s], hh, TN) for s in range(3)], 0)
    og, ig, pg, qg, bias, pair = lax.psum((*grads, qg, bias_grad, pair_grad), "dp")
    small = lax.psum(jnp.concatenate([gain, shift, small[0:6]], 0), ("dp", "mp"))
    local = sum(square(v) for v in (og, ig, pg, qg, bias, pair))
    total = lax.psum(local, "mp") + square(small)
    return dx + dv, og, ig, pg, qg, small, bias, pair, total


def adam_step(weight, grad, first, second, clip, fix_one, fix_two, rate, decay):
    scaled = grad * clip
    first_new = beta_one * first + (1.0 - beta_one) * scaled
    second_new = beta_two * second + (1.0 - beta_two) * scaled * scaled
    ratio = first_new / fix_one / (jnp.sqrt(second_new / fix_two) + adam_eps)
    return (weight - rate * (ratio + decay * weight), first_new, second_new)


def per_device(n, ndp, block_in, coords, lengths, cotangent, step_count, *state):
    weights, firsts, seconds = state[:7], state[7:14], state[14:]
    qkv_weight, proj_weight, pair_weight, in_weight, in_bias, out_weight, params = weights
    heads = pair_weight.shape[0]
    pair_low = pair_weight.astype(BF16)
    h, dy_all, qkv = enter(n, block_in, cotangent, params, qkv_weight)
    o, probs = attention(qkv, coords, lengths, pair_low, heads)
    block_out, dx, do, og, ig, pg, bg, small = middle(
        n, block_in, cotangent, dy_all, o, params, in_bias.reshape(1, -1), proj_weight, in_weight, out_weight)
    dqkv, pair_grad = attention_back(qkv, do, probs, coords, lengths, heads)
    ny = n // 2 if ndp % (n // 2) == 0 else 1
    rest = (block_in, dx, params, dqkv, h, (og, ig, pg), bg, pair_grad, small, qkv_weight)
    if all(t % (8 * ndp) == 0 for t in (og.shape[0], pg.shape[0], 3 * qkv_weight.shape[1])):
        done = leave(n, ny, ndp // ny, *rest)
    else:
        done = leave_plain(n, *rest)
    grad_input, og, ig, pg, qg, small, bias, pair, total = done
    grad_norm = jnp.sqrt(total[0, 0])
    clip = clip_level / jnp.maximum(grad_norm, clip_level)
    count = step_count[0].astype(F32)
    fix_one = 1.0 - jnp.power(beta_one, count)
    fix_two = 1.0 - jnp.power(beta_two, count)
    grads = (qg.reshape(qkv_weight.shape), pg.reshape(proj_weight.shape), pair[:heads], ig.reshape(in_weight.shape),
             bias[0], og.reshape(out_weight.shape), small[:5])
    rates = (0.9, 2.5, 7.5, 0.9, 7.5, 0.45, 3.0)
    decays = (0.01, 0.01, 0.01, 0.01, 0.0, 0.01, 0.0)
    outs = [block_out, grad_input, grad_norm.reshape(1)]
    for w, g, m, u, rate, decay in zip(weights, grads, firsts, seconds, rates, decays):
        outs.extend(adam_step(w, g.astype(F32), m, u, clip, fix_one, fix_two, rate, decay))
    return tuple(outs)


def solution(mesh):
    rows, mp = P(("dp", "mp"), None), P("mp", None)
    stacked = P(None, "mp", None)
    params = (stacked, mp, mp, mp, P("mp"), mp, P())
    in_specs = (rows, P(None, "dp"), P("dp", None), rows, P(), *params, *params, *params)
    out_specs = (rows, rows, P(), *[s for s in params for _ in range(3)])
    return jax.shard_map(
        functools.partial(per_device, mesh.shape["mp"], mesh.shape["dp"]),
        mesh=mesh, in_specs=in_specs, out_specs=out_specs, check_vma=False)
```

time: 555 us -> 315 us (0.57)
  Pallas kernels: 0 us -> 282 us
  waiting for transfers between devices: 206 us -> 0 us
  matrix products: 146 us -> 0 us
  blocking collectives: 106 us -> 0 us
  other arithmetic: 45.9 us -> 19.5 us
  local copies, waits for them, and re-layouts: 27.7 us -> 5.67 us
  between operations: 21.9 us -> 3.98 us
    pallas_call x0 -> x5, Pallas kernels: none -> 282 us  [the longest x1 124 us: leave(): pl.pallas_call(functools.partial(leave_kernel, n, ny, nz), out_shape=(f(r...]
    dot_general x20 -> x0, matrix products: 146 us -> none  [the longest x1 48.2 us: attend_back(): jnp.einsum('hij,ijk->hk', grad_score, gauss, preferred_element_type=jnp.f...]
    psum x1 -> x0, waiting for transfers between devices: 133 us -> none  [per_device(): lax.psum((qkv_grad, proj_grad, pair_grad, in_grad, bias_grad, out_grad),...]
    reduce_scatter x4 -> x0, waiting for transfers between devices: 73.5 us -> none  [the longest x1 28.8 us: per_device(): lax.psum_scatter(jnp.dot(piece, out_low, preferred_element_type=jnp.float...]
    psum x3 -> x0, blocking collectives: 69.9 us -> none  [the longest x1 39.9 us: per_device(): norm_grad = lax.psum(norm_grad, ('dp', 'mp'))]
    all_gather x4 -> x0, blocking collectives: 35.7 us -> none  [the longest x1 10.1 us: per_device(): first_all = lax.all_gather(first_norm, 'mp', axis=0, tiled=True)]
    reduce_sum x19 -> x0, other arithmetic: 22.5 us -> none  [the longest x6 8.26 us: per_device(): local_squares = local_squares + jnp.sum(grad * grad)]
    dot_general x1 -> x0, local copies, waits for them, and re-layouts: 9.93 us -> none  [block_scores(): jnp.einsum('ijk,hk->hij', gauss, pair_low, preferred_element_type=jnp.flo...]
  transfers between devices with their start and end apart: 5 -> 0, of which waited for: 4 -> 0; matrix products, arithmetic and copies ran while one was open for 14% -> 0% of each run, Pallas kernels for 0% -> 0%
where the time goes in v1:
time: 315 us; the launch traced here: 311 us
  Pallas kernels  282 us (90%)
  other arithmetic  19.5 us (6%)
  local copies, waits for them, and re-layouts  5.67 us (2%)
  between operations  3.98 us (1%)
    pallas_call x1, Pallas kernels, leave(): pl.pallas_call(functools.partial(leave_kernel, n, ny, nz), out_shape=(f(r...  124 us
    pallas_call x1, Pallas kernels, attention_back(): pl.pallas_call(functools.partial(bwd_kernel, heads, mols), out_shape=(jax...  51.7 us
    pallas_call x1, Pallas kernels, attention(): pl.pallas_call(functools.partial(fwd_kernel, heads, mols), out_shape=(jax...  46.5 us
    pallas_call x1, Pallas kernels, middle(): pl.pallas_call(functools.partial(middle_kernel, n), out_shape=(f(rows, wi...  41.7 us
    pallas_call x1, Pallas kernels, enter(): pl.pallas_call(functools.partial(enter_kernel, n), out_shape=(jax.ShapeDt...  18.6 us
    sub x7, other arithmetic, adam_step(): return (weight - rate * (ratio + decay * weight), first_new, second_new)  15 us

profile of v1, /device:TPU:0, one launch (start us, length us, event | category | flops | bytes accessed | tf_op | source)
XLA Modules:
  0.0 311.5 jit_solution(5506780287308836911)
XLA Ops:
  0.7 0.0 copy-start.20
  0.7 18.6 %enter.1 = (bf16[4,128,768]{2,1,0:T(8,128)(2,1)}, bf16[4,128,768]{2,1,0:T(8,128)(2,1)}, bf16[3,512,192]{2,1,0:T(8,128)(2,1)}) custom-call(bf16[128,768]{1,0:T(8,128)(2,1)} %x_ref.5, bf16[128,768]{1,0:T(8,128)(2,1)} %dy_ref.3, f32[5,768]{1,0:T(8,128)} %np_ref.5, f32[3,192,768]{2,1,0:T(8,128)} %w_hbm.3), custom_call_target="tpu_custom_call" | custom-call | tf_op jit(solution)/shard_map/enter/pallas_call | solution.py:390
  19.3 1.3 convert_element_type.23.w_ref
  20.5 46.5 %attend.1 = (bf16[512,192]{1,0:T(8,128)(2,1)}, bf16[4096,512]{1,0:T(8,128)(2,1)}) custom-call(s32[1,16]{1,0:T(1,128)} %len_ref.3, f32[3,512]{1,0:T(4,128)} %coords_ref.3, bf16[3,512,192]{2,1,0:T(8,128)(2,1)} %get-tuple-element.49.q_ref.k_ref.v_ref, bf16[3,512,192]{2,1,0:T(8,128)(2,1)} %get-tuple-element.49.q_ref.k_ref.v_ref, ...), custom_call_target="tpu_custom_call" | custom-call | tf_op jit(solution)/shard_map/attend/pallas_call | solution.py:125
  67.1 0.0 copy-done.20
  67.1 0.6 reshape.87.bias_ref
  67.7 41.7 %middle.1 = (f32[128,768]{1,0:T(8,128)}, f32[128,768]{1,0:T(8,128)}, bf16[512,192]{1,0:T(8,128)(2,1)}, f32[768,768]{1,0:T(8,128)}, f32[768,768]{1,0:T(8,128)}, /...) custom-call(bf16[128,768]{1,0:T(8,128)(2,1)} %x_ref.5, bf16[128,768]{1,0:T(8,128)(2,1)} %dy_ref.3, ...), custom_call_target="tpu_custom_call" | custom-call | tf_op jit(solution)/shard_map/middle/pallas_call | solution.py:501
  109.3 51.7 %attend_back.1 = (bf16[3,512,192]{2,1,0:T(8,128)(2,1)}, f32[8,128]{1,0:T(8,128)}) custom-call(s32[1,16]{1,0:T(1,128)} %len_ref.3, f32[3,512]{1,0:T(4,128)} %coords_ref.3, bf16[3,512,192]{2,1,0:T(8,128)(2,1)} %get-tuple-element.49.q_ref.k_ref.v_ref, bf16[3,512,192]{2,1,0:T(8,128)(2,1)} %get-tuple-element.49.q_ref.k_ref.v_ref, ...), custom_call_target="tpu_custom_call" | custom-call | tf_op jit(solution)/shard_map/attend_back/pallas_call | solution.py:194
  161.0 123.9 %leave.1 = (f32[128,768]{1,0:T(8,128)}, bf16[8,96,768]{2,1,0:T(8,128)(2,1)}, bf16[8,96,768]{2,1,0:T(8,128)(2,1)}, bf16[8,24,768]{2,1,0:T(8,128)(2,1)}, bf16[8,72...) custom-call(bf16[128,768]{1,0:T(8,128)(2,1)} %x_ref.5, ...), custom_call_target="tpu_custom_call" | custom-call | tf_op jit(solution)/shard_map/leave/pallas_call | solution.py:740
  285.6 0.0 copy-start.1
  285.6 0.0 copy-start.4
  285.6 0.0 copy-start.5
  285.6 2.3 convert_multiply_fusion
  289.2 0.0 copy-done.1
  289.2 0.0 copy-done.4
  289.2 0.3 copy-done.5
  289.4 0.0 copy-start.2
  289.4 0.0 copy-start.6
  289.4 4.3 %multiply_subtract_fusion = (f32[768,768]{1,0:T(8,128)}, f32[768,768]{1,0:T(8,128)}, f32[768,768]{1,0:T(8,128)}) fusion(f32[768,768]{1,0:T(8,128)S(1)} %copy-done.1, f32[]{:T(128)} %bitcast.4, f32[]{:T(128)} %bitcast.3, f32[8,96,768]{2,1,0:T(8,128)S(1)} %get-tuple-element.93, f32[768,768]{1,0:T(8,128)S(1)} %copy-done.4, f32[768,768]{1,0:T(8,128)S(1)} %copy-done.5), kind=kLoop, calls=%fused_computation.9 | loop fusion | flops 8847360 | bytes 16515080 | tf_op jit(solution)/shard_map/sub | solution.py:773
  293.7 0.0 copy-done.2
  293.8 0.0 copy-done.6
  293.8 1.3 copy-done.7
  295.1 0.0 copy-start.22
  295.1 0.0 copy-start.23
  295.1 0.0 copy-start.21
  295.1 0.0 copy-start.24
  295.1 0.0 copy-start.25
  295.1 0.0 copy-start.26
  295.2 0.0 copy-start.16
  295.2 0.0 copy-start.3
  295.2 0.0 copy-start.11
  295.2 0.0 copy-start.12
  295.2 4.1 %multiply_subtract_fusion.1 = (f32[768,768]{1,0:T(8,128)}, f32[768,768]{1,0:T(8,128)}, f32[768,768]{1,0:T(8,128)}) fusion(f32[768,768]{1,0:T(8,128)S(1)} %copy-done.2, f32[]{:T(128)} %bitcast.4, f32[]{:T(128)} %bitcast.3, f32[8,96,768]{2,1,0:T(8,128)S(1)} %get-tuple-element.94, f32[768,768]{1,0:T(8,128)S(1)} %copy-done.6, f32[768,768]{1,0:T(8,128)S(1)} %copy-done.7), kind=kLoop, calls=%fused_computation.11 | loop fusion | flops 8847360 | bytes 16515080 | tf_op jit(solution)/shard_map/sub | solution.py:773
  299.3 0.0 copy-done.13
  299.3 0.0 copy-done.17
  299.3 0.0 copy-done.18
  299.3 0.0 copy-done.19
  299.3 0.6 multiply_subtract_fusion.4
  300.0 0.8 multiply_reduce_fusion
  300.7 0.0 copy-done.22
  300.7 0.0 copy-done.23
  300.7 0.6 multiply_subtract_fusion.5
  301.4 0.0 copy-done.21
  301.4 0.0 copy-done.24
  301.4 0.0 copy-done.25
  301.4 0.0 copy-done.26
  301.4 0.6 multiply_subtract_fusion.6
  302.0 0.0 copy-done.16
  302.1 0.0 copy-done.3
  302.1 0.0 copy-done.11
  302.1 0.0 copy-done.12
  302.1 0.0 copy-start.8
  302.1 0.0 copy-start.9
  302.1 1.5 multiply_subtract_fusion.3
  303.6 0.0 copy-done.10
  303.6 0.1 convert_multiply_fusion.2
  303.7 0.7 copy-done.8
  304.4 0.5 copy-done.9
  305.0 0.7 copy-done
  305.6 3.2 %multiply_subtract_fusion.2 = (f32[3,192,768]{2,1,0:T(8,128)}, f32[3,192,768]{2,1,0:T(8,128)}, f32[3,192,768]{2,1,0:T(8,128)}) fusion(f32[3,192,768]{2,1,0:T(8,128)S(1)} %copy-done, f32[]{:T(128)} %bitcast.4, f32[]{:T(128)} %bitcast.3, f32[3,192,768]{2,1,0:T(8,128)S(1)} %bitcast.27, f32[3,192,768]{2,1,0:T(8,128)S(1)} %copy-done.8, ...), kind=kLoop, calls=%fused_computation.14 | loop fusion | flops 6635520 | bytes 12386312 | tf_op jit(solution)/shard_map/sub | solution.py:773
  308.9 0.0 copy-done.14
  308.9 0.7 copy.53
  309.6 0.0 copy-done.15
  309.6 0.7 copy.54
  (10 shorter events, 0.1 us)
Async XLA Ops:
  0.7 66.4 %copy-start.20 = (f32[768]{0:T(1024)S(1)}, f32[768]{0:T(1024)}, u32[]{:S(2)}) copy-start(f32[768]{0:T(1024)} %param.35) | copy-start | bytes 9220
  285.6 3.5 %copy-start.1 = (f32[768,768]{1,0:T(8,128)S(1)}, f32[768,768]{1,0:T(8,128)}, u32[]{:S(2)}) copy-start(f32[768,768]{1,0:T(8,128)} %ow_hbm.1) | copy-start | bytes 7077892
  285.6 3.5 %copy-start.4 = (f32[768,768]{1,0:T(8,128)S(1)}, f32[768,768]{1,0:T(8,128)}, u32[]{:S(2)}) copy-start(f32[768,768]{1,0:T(8,128)} %param.50) | copy-start | bytes 7077892
  285.6 3.8 %copy-start.5 = (f32[768,768]{1,0:T(8,128)S(1)}, f32[768,768]{1,0:T(8,128)}, u32[]{:S(2)}) copy-start(f32[768,768]{1,0:T(8,128)} %param.43) | copy-start | bytes 7077892
  289.4 4.3 %copy-start.2 = (f32[768,768]{1,0:T(8,128)S(1)}, f32[768,768]{1,0:T(8,128)}, u32[]{:S(2)}) copy-start(f32[768,768]{1,0:T(8,128)} %iw_hbm.1) | copy-start | bytes 7077892
  289.4 4.3 %copy-start.6 = (f32[768,768]{1,0:T(8,128)S(1)}, f32[768,768]{1,0:T(8,128)}, u32[]{:S(2)}) copy-start(f32[768,768]{1,0:T(8,128)} %param.48) | copy-start | bytes 7077892
  289.4 5.6 %copy-start.7 = (f32[768,768]{1,0:T(8,128)S(1)}, f32[768,768]{1,0:T(8,128)}, u32[]{:S(2)}) copy-start(f32[768,768]{1,0:T(8,128)} %param.41) | copy-start | bytes 7077892
  295.1 4.2 %copy-start.13 = (f32[5,768]{1,0:T(8,128)S(1)}, f32[5,768]{1,0:T(8,128)}, u32[]{:S(2)}) copy-start(f32[5,768]{1,0:T(8,128)} %np_ref.5) | copy-start | bytes 46084
  295.1 4.2 %copy-start.17 = (f32[5,768]{1,0:T(8,128)S(1)}, f32[5,768]{1,0:T(8,128)}, u32[]{:S(2)}) copy-start(f32[5,768]{1,0:T(8,128)} %param.51) | copy-start | bytes 46084
  295.1 4.2 %copy-start.18 = (f32[5,768]{1,0:T(8,128)S(1)}, f32[5,768]{1,0:T(8,128)}, u32[]{:S(2)}) copy-start(f32[5,768]{1,0:T(8,128)} %param.44) | copy-start | bytes 46084
  295.1 4.2 %copy-start.19 = (f32[8,768]{1,0:T(8,128)S(1)}, f32[8,768]{1,0:T(8,128)}, u32[]{:S(2)}) copy-start(f32[8,768]{1,0:T(8,128)} %get-tuple-element.71) | copy-start | bytes 73732
  295.1 5.6 %copy-start.22 = (f32[768]{0:T(1024)S(1)}, f32[768]{0:T(1024)}, u32[]{:S(2)}) copy-start(f32[768]{0:T(1024)} %param.49) | copy-start | bytes 9220
  295.1 5.6 %copy-start.23 = (f32[768]{0:T(1024)S(1)}, f32[768]{0:T(1024)}, u32[]{:S(2)}) copy-start(f32[768]{0:T(1024)} %param.42) | copy-start | bytes 9220
  295.1 6.3 %copy-start.21 = (f32[8,128]{1,0:T(8,128)S(1)}, f32[8,128]{1,0:T(8,128)}, u32[]{:S(2)}) copy-start(f32[8,128]{1,0:T(8,128)} %param.33) | copy-start | bytes 12292
  295.1 6.3 %copy-start.24 = (f32[8,128]{1,0:T(8,128)S(1)}, f32[8,128]{1,0:T(8,128)}, u32[]{:S(2)}) copy-start(f32[8,128]{1,0:T(8,128)} %param.47) | copy-start | bytes 12292
  295.1 6.2 %copy-start.25 = (f32[8,128]{1,0:T(8,128)S(1)}, f32[8,128]{1,0:T(8,128)}, u32[]{:S(2)}) copy-start(f32[8,128]{1,0:T(8,128)} %param.40) | copy-start | bytes 12292
  295.1 6.2 %copy-start.26 = (f32[8,128]{1,0:T(8,128)S(1)}, f32[8,128]{1,0:T(8,128)}, u32[]{:S(2)}) copy-start(f32[8,128]{1,0:T(8,128)} %get-tuple-element.67) | copy-start | bytes 12292
  295.2 6.9 %copy-start.16 = (bf16[8,24,768]{2,1,0:T(8,128)(2,1)S(1)}, bf16[8,24,768]{2,1,0:T(8,128)(2,1)}, u32[]{:S(2)}) copy-start(bf16[8,24,768]{2,1,0:T(8,128)(2,1)} %get-tuple-element.66) | copy-start | bytes 884740
  295.2 6.9 %copy-start.3 = (f32[192,768]{1,0:T(8,128)S(1)}, f32[192,768]{1,0:T(8,128)}, u32[]{:S(2)}) copy-start(f32[192,768]{1,0:T(8,128)} %pw_hbm.1) | copy-start | bytes 1769476
  295.2 6.9 %copy-start.11 = (f32[192,768]{1,0:T(8,128)S(1)}, f32[192,768]{1,0:T(8,128)}, u32[]{:S(2)}) copy-start(f32[192,768]{1,0:T(8,128)} %param.46) | copy-start | bytes 1769476
  295.2 6.9 %copy-start.12 = (f32[192,768]{1,0:T(8,128)S(1)}, f32[192,768]{1,0:T(8,128)}, u32[]{:S(2)}) copy-start(f32[192,768]{1,0:T(8,128)} %param.39) | copy-start | bytes 1769476
  302.0 1.6 copy-start.10
  302.1 2.3 copy-start.8
  302.1 2.9 copy-start.9
  303.6 2.0 copy-start
  305.6 3.2 %copy-start.14 = (f32[128,768]{1,0:T(8,128)S(1)}, f32[128,768]{1,0:T(8,128)}, u32[]{:S(2)}) copy-start(f32[128,768]{1,0:T(8,128)} %get-tuple-element.119) | copy-start | bytes 1179652
  305.6 4.0 %copy-start.15 = (f32[128,768]{1,0:T(8,128)S(1)}, f32[128,768]{1,0:T(8,128)}, u32[]{:S(2)}) copy-start(f32[128,768]{1,0:T(8,128)} %get-tuple-element.120) | copy-start | bytes 1179652

commit v2 on v1

--- a/solution.py
+++ b/solution.py
@@ -473,8 +473,8 @@
         for b in range(n):
             acc_o += mm(act[b, :, pl.ds(c0, step)], dyall_ref[b], TN)
             acc_i += mm(dpre[b, :, pl.ds(c0, step)], h2[b], TN)
-        og_ref[pl.ds(c0, step), :] = acc_o
-        ig_ref[pl.ds(c0, step), :] = acc_i
+        og_ref[pl.ds(c0, step), :] = acc_o.astype(BF16)
+        ig_ref[pl.ds(c0, step), :] = acc_i.astype(BF16)
         return carry
 
     lax.fori_loop(0, hidden // step, grads, 0)
@@ -482,13 +482,11 @@
     mid_ref[...] = dx1
     gath[1].finish()
 
-    def heads_block(b, carry):
+    def heads_block(b, acc):
         do_ref[at(b), :] = mm(da[b], pw[...], NT).astype(BF16)
-        pg_ref[...] += mm(o_ref[at(b), :], da[b], TN)
-        return carry
-
-    pg_ref[...] = jnp.zeros_like(pg_ref)
-    lax.fori_loop(0, n, heads_block, 0)
+        return acc + mm(o_ref[at(b), :], da[b], TN)
+
+    pg_ref[...] = lax.fori_loop(0, n, heads_block, jnp.zeros(pg_ref.shape, F32)).astype(BF16)
     for c in scat + gath:
         c.drain()
 
@@ -501,7 +499,7 @@
     return pl.pallas_call(
         functools.partial(middle_kernel, n),
         out_shape=(f(rows, width), f(rows, width), jax.ShapeDtypeStruct((n * rows, inner), BF16),
-                   f(hidden, width), f(hidden, width), f(inner, width), f(1, hidden), f(8, width)),
+                   *[jax.ShapeDtypeStruct((t, width), BF16) for t in (hidden, hidden, inner)], f(1, hidden), f(8, width)),
         in_specs=[VM] * 6 + [HBM] * 3, out_specs=[VM] * 8,
         scratch_shapes=[pltpu.VMEM((inner, width), F32), pltpu.VMEM((hidden, width), F32),
                         pltpu.VMEM((hidden, width), F32), pltpu.VMEM((inner, width), BF16),
@@ -537,35 +535,41 @@
 
 def sum_scratch(ny, nz, chunk, width):
     y, z = max(ny - 1, 1), max(nz - 1, 1)
-    return [pltpu.VMEM((y, nz, chunk, width), BF16), pltpu.VMEM((y, nz, chunk, width), BF16),
-            pltpu.VMEM((z, chunk, width), BF16), pltpu.VMEM((z, chunk, width), BF16),
+    return [pltpu.VMEM((y, nz, chunk, width), BF16), pltpu.VMEM((z, chunk, width), BF16),
+            pltpu.VMEM((z, chunk, width), BF16), pltpu.VMEM((chunk, width), F32),
             DMA((y,)), DMA((y,)), DMA((z,)), DMA((z,)), DMA((z,)), DMA((z,)), DMA((nz, y)), DMA((nz, y))]
+
+
+SUMS = 12
 
 
 class Sum:
     def __init__(self, grid, grad, result, scratch):
         self.grid, self.grad, self.result = grid, grad, result
-        (self.oa, self.ia, self.ob, self.ib, self.sa, self.ra, self.sb, self.rb,
+        (self.ia, self.ob, self.ib, self.own, self.sa, self.ra, self.sb, self.rb,
          self.sz, self.rz, self.sy, self.ry) = scratch
-        self.chunk = result.shape[1]
-
-    def piece(self, z, y):
-        start = pl.multiple_of((z * self.grid.ny + y) * self.chunk, 8)
-        return self.grad[pl.ds(start, self.chunk), :]
 
     def copy_y(self, k):
         g = self.grid
-        return remote(self.oa.at[k], self.ia.at[k], self.sa.at[k], self.ra.at[k], "dp", g.z * g.ny + g.yto(k))
+        return remote(self.grad.at[g.yto(k)], self.ia.at[k], self.sa.at[k], self.ra.at[k], "dp",
+                      g.z * g.ny + g.yto(k))
 
     def copy_z(self, k):
         g = self.grid
         return remote(self.ob.at[k], self.ib.at[k], self.sb.at[k], self.rb.at[k], "dp", g.zto(k) * g.ny + g.y)
 
+    def back_z(self, k):
+        g = self.grid
+        r = self.result.at[g.y, g.z]
+        return remote(r, r, self.sz.at[k], self.rz.at[k], "dp", g.zto(k) * g.ny + g.y)
+
+    def back_y(self, k, j):
+        g = self.grid
+        r = self.result.at[g.y, g.z if k == g.nz - 1 else g.zfrom(k)]
+        return remote(r, r, self.sy.at[k, j], self.ry.at[k, j], "dp", g.z * g.ny + g.yto(j))
+
     def push(self):
-        g = self.grid
-        for k in range(g.ny - 1):
-            for z in range(g.nz):
-                self.oa[k, z] = self.piece(z, g.yto(k)).astype(BF16)
+        for k in range(self.grid.ny - 1):
             self.copy_y(k).start()
 
     def pass_on(self):
@@ -574,35 +578,27 @@
             self.copy_y(k).wait_recv()
         for k in range(g.nz):
             z = g.zto(k)
-            whole = self.piece(z, g.y)
+            whole = self.grad[g.y, z].astype(F32)
             for j in range(g.ny - 1):
                 whole = whole + self.ia[j, z].astype(F32)
             if k < g.nz - 1:
                 self.ob[k] = whole.astype(BF16)
                 self.copy_z(k).start()
-        self.own = whole
+            else:
+                self.own[...] = whole
 
     def finish(self):
-        for k in range(self.grid.nz - 1):
+        g = self.grid
+        whole = self.own[...]
+        for k in range(g.nz - 1):
             self.copy_z(k).wait_recv()
-            self.own = self.own + self.ib[k].astype(F32)
-        self.result[self.grid.me] = self.own.astype(BF16)
-        for k in range(self.grid.nz - 1):
+            whole = whole + self.ib[k].astype(F32)
+        self.result[g.y, g.z] = whole.astype(BF16)
+        for k in range(g.nz - 1):
             self.back_z(k).start()
-        for k in range(self.grid.ny - 1):
-            self.back_y(self.grid.nz - 1, k).start()
-        return self.own
-
-    def back_z(self, k):
-        g = self.grid
-        r = self.result.at[g.me]
-        return remote(r, r, self.sz.at[k], self.rz.at[k], "dp", g.zto(k) * g.ny + g.y)
-
-    def back_y(self, k, j):
-        g = self.grid
-        z = g.z if k == g.nz - 1 else g.zfrom(k)
-        r = self.result.at[z * g.ny + g.y]
-        return remote(r, r, self.sy.at[k, j], self.ry.at[k, j], "dp", g.z * g.ny + g.yto(j))
+        for k in range(g.ny - 1):
+            self.back_y(g.nz - 1, k).start()
+        return square(whole)
 
     def forward(self):
         g = self.grid
@@ -662,8 +658,8 @@
     return jnp.sum(jnp.sum(v * v, axis=1, keepdims=True), axis=0, keepdims=True)
 
 
-def leave_kernel(n, ny, nz, x_ref, dx_ref, np_ref, dqkv_ref, h_ref, og_ref, ig_ref, pg_ref, bg_ref, pair_ref,
-                 mid_small_ref, w_hbm, gi_ref, so_ref, si_ref, sp_ref, sq_ref, small_ref, bias_ref, pairs_ref, norm_ref,
+def leave_kernel(n, ny, nz, x_ref, dx_ref, np_ref, dqkv_ref, h_ref, bg_ref, pair_ref, squares_ref,
+                 mid_small_ref, w_hbm, gi_ref, sq_ref, small_ref, bias_ref, pairs_ref, norm_ref,
                  w32, w, qg, wsem, *rest):
     seat, grid = Seat(n), Grid(ny, nz)
     rows, width = x_ref.shape
@@ -671,9 +667,9 @@
     load = pltpu.make_async_copy(w_hbm, w32, wsem)
     load.start()
     scat = Scatter(seat, rest[:8])
-    sums = [Sum(grid, g, r, rest[8 + 12 * i:20 + 12 * i])
-            for i, (g, r) in enumerate([(og_ref, so_ref), (ig_ref, si_ref), (pg_ref, sp_ref), (qg, sq_ref)])]
-    shares = [Share(a, *rest[56 + 3 * i:59 + 3 * i]) for i, a in enumerate(("mp", "dp", "dp", "dp", "mp", "dp"))]
+    sums = [Sum(grid, qg.at[s], sq_ref.at[s], rest[8 + SUMS * s:8 + SUMS * (s + 1)]) for s in range(3)]
+    rest = rest[8 + 3 * SUMS:]
+    shares = [Share(a, *rest[3 * i:3 * i + 3]) for i, a in enumerate(("mp", "dp", "dp", "dp", "mp", "dp"))]
     small_mp, small_dp, bias_dp, pair_dp, sq_mp, sq_dp = shares
     greet({"mp": n, "dp": ny * nz})
     at = lambda b: pl.ds(pl.multiple_of(b * rows, rows), rows)
@@ -685,17 +681,16 @@
         return sum(mm(dqkv_ref[s, at(b), :], w[s]) for s in range(3))
 
     scat.push(first_block)
-    whole = scat.pass_on(first_block)
-    for s in sums[:3]:
-        s.push()
-    bias_dp.start(jnp.broadcast_to(bg_ref[...], bias_dp.slots.shape[1:]))
-    pair_dp.start(pair_ref[...])
     for s in range(3):
         acc = jnp.zeros((inner, width), F32)
         for b in range(n):
             acc = acc + mm(dqkv_ref[s, at(b), :], h_ref[b], TN)
-        qg[pl.ds(s * inner, inner), :] = acc
-    sums[3].push()
+        qg[s] = acc.reshape(qg.shape[1:]).astype(BF16)
+        sums[s].push()
+        if s == 0:
+            whole = scat.pass_on(first_block)
+            bias_dp.start(jnp.broadcast_to(bg_ref[...], bias_dp.slots.shape[1:]))
+            pair_dp.start(pair_ref[...])
     dh1 = scat.finish(whole)
     dv, gain, shift = norm_back(x_ref[...].astype(F32), np_ref[0:1], dh1)
     gi_ref[...] = dx_ref[...] + dv
@@ -703,14 +698,11 @@
     sums[0].pass_on()
     small_dp.start(small_mp.total())
     sums[1].pass_on()
-    squares = square(sums[0].finish())
+    squares = squares_ref[0:1] + sums[0].finish()
     sums[2].pass_on()
-    sums[3].pass_on()
-    squares = squares + square(sums[1].finish())
-    squares = squares + square(sums[2].finish())
-    squares = squares + square(sums[3].finish())
-    small = small_dp.total()
-    small_ref[...] = small
+    squares = squares + sums[1].finish()
+    squares = squares + sums[2].finish()
+    sums[0].forward()
     bias = bias_dp.total()
     bias_ref[...] = bias
     pairs = pair_dp.total()
@@ -718,10 +710,11 @@
     row = lax.broadcasted_iota(jnp.int32, (8, LANE), 0)
     local = square(bias[0:1]) + square(pairs)
     sq_mp.start(jnp.where(row == 0, squares, jnp.where(row == 1, local, 0.0)))
-    sums[0].forward()
+    small = small_dp.total()
+    small_ref[...] = small
+    sums[1].forward()
     sq_dp.start(sq_mp.total())
-    for s in sums[1:]:
-        s.forward()
+    sums[2].forward()
     norm_ref[...] = sq_dp.total()[0:1] + sq_dp.slots[0, 1:2] + square(small)
     for s in sums:
         s.close()
@@ -730,26 +723,144 @@
         s.drain()
 
 
-def leave(n, ny, nz, x, dx, params, dqkv, h, grads, bias_grad, pair_grad, small, qkv_weight):
+def leave(n, ny, nz, x, dx, params, dqkv, h, bias_grad, pair_grad, squares, small, qkv_weight):
     rows, width = x.shape
     inner = qkv_weight.shape[1]
     ndp = ny * nz
-    tall = [g.shape[0] for g in grads] + [3 * inner]
     hidden = bias_grad.shape[1]
+    chunks = (3, ny, nz, inner // ndp, width)
     f = lambda *s: jax.ShapeDtypeStruct(s, F32)
     return pl.pallas_call(
         functools.partial(leave_kernel, n, ny, nz),
-        out_shape=(f(rows, width), *[jax.ShapeDtypeStruct((ndp, t // ndp, width), BF16) for t in tall],
-                   f(8, width), f(8, hidden), f(8, LANE), f(1, LANE)),
-        in_specs=[VM] * 11 + [HBM], out_specs=[VM] * 9,
+        out_shape=(f(rows, width), jax.ShapeDtypeStruct(chunks, BF16), f(8, width), f(8, hidden), f(8, LANE), f(1, LANE)),
+        in_specs=[VM] * 9 + [HBM], out_specs=[VM] * 6,
         scratch_shapes=[pltpu.VMEM(qkv_weight.shape, F32), pltpu.VMEM(qkv_weight.shape, BF16),
-                        pltpu.VMEM((3 * inner, width), F32), DMA, *scatter_scratch(n, rows, width),
-                        *[s for t in tall for s in sum_scratch(ny, nz, t // ndp, width)],
+                        pltpu.VMEM(chunks, BF16), DMA, *scatter_scratch(n, rows, width),
+                        *[s for _ in range(3) for s in sum_scratch(ny, nz, inner // ndp, width)],
                         *share_scratch(n, 8, width), *share_scratch(ndp, 8, width), *share_scratch(ndp, 8, hidden),
                         *share_scratch(ndp, 8, LANE), *share_scratch(n, 8, LANE), *share_scratch(ndp, 8, LANE)],
         compiler_params=pltpu.CompilerParams(collective_id=2, has_side_effects=True, vmem_limit_bytes=60 << 20),
         name="leave",
-    )(x, dx, params, dqkv, h, *grads, bias_grad, pair_grad, small, qkv_weight)
+    )(x, dx, params, dqkv, h, bias_grad, pair_grad, squares, small, qkv_weight)
+
+
+def back_kernel(heads, ny, nz, coords_ref, qkv_ref, do_ref, p_ref, og_ref, ig_ref, pg_ref,
+                dqkv_ref, pair_ref, so_ref, si_ref, sp_ref, squares_ref,
+                dist, ds, qf, dof, dkt, dvt, *rest):
+    span, inner = do_ref.shape
+    scale = 1.0 / math.sqrt(inner // heads)
+    grid = Grid(ny, nz)
+    parts = og_ref.shape[0]
+    pieces = [(g.at[i], r.at[i]) for g, r in ((og_ref, so_ref), (ig_ref, si_ref)) for i in range(parts)]
+    pieces.append((pg_ref, sp_ref))
+    sums = [Sum(grid, g, r, rest[SUMS * i:SUMS * (i + 1)]) for i, (g, r) in enumerate(pieces)]
+    greet({"dp": ny * nz})
+    for s in sums:
+        s.push()
+    squares_ref[...] = jnp.zeros_like(squares_ref)
+
+    def finish(s):
+        squares_ref[...] += s.finish()
+
+    jobs = {}
+    for i, s in enumerate(sums):
+        jobs.setdefault(PASS_AT[i], []).append(s.pass_on)
+        jobs.setdefault(FINISH_AT[i], []).append(functools.partial(finish, s))
+        jobs.setdefault(FORWARD_AT[i], []).append(s.forward)
+    last = span // CHUNK
+
+    pair_distances(coords_ref, dist, span)
+    mask = head_mask(heads, inner)
+    qf[...] = qkv_ref[0].astype(F32)
+    dof[...] = do_ref[...].astype(F32)
+    dkt[...] = jnp.zeros_like(dkt)
+    dvt[...] = jnp.zeros_like(dvt)
+
+    def chunk(ci, acc):
+        for when in sorted(jobs):
+            if when < last:
+                @pl.when(ci == when)
+                def _():
+                    for job in jobs[when]:
+                        job()
+        c0 = pl.multiple_of(ci * CHUNK, CHUNK)
+        r0 = pl.multiple_of(ci * CHUNK * SUB, CHUNK * SUB)
+        qt = expand(qf[pl.ds(c0, CHUNK), :], mask)
+        dot = expand(dof[pl.ds(c0, CHUNK), :], mask)
+        pb = p_ref[pl.ds(r0, CHUNK * SUB), :]
+        pf = pb.astype(F32)
+        dp = mm(dot, qkv_ref[2], NT)
+        rowdot = jnp.sum(pf * dp, axis=-1, keepdims=True)
+        dsf = pf * (dp - rowdot)
+        dsb = dsf.astype(BF16)
+        ds[...] = dsf
+        dqkv_ref[0, pl.ds(c0, CHUNK), :] = (collapse(mm(dsb, qkv_ref[1]), mask) * scale).astype(BF16)
+        dkt[...] += mm(qt, dsb, TN)
+        dvt[...] += mm(dot, pb, TN)
+
+        def group(g, acc):
+            i0 = pl.multiple_of(ci * CHUNK + g * SUB, SUB)
+
+            def tile(jt, acc):
+                j0 = pl.multiple_of(jt * LANE, LANE)
+                dblk = dist[pl.ds(i0, SUB), pl.ds(j0, LANE)]
+                left, right = [], []
+                for r in range(SUB):
+                    row0 = pl.multiple_of((g * SUB + r) * SUB, SUB)
+                    left.append(ds[pl.ds(row0, SUB), pl.ds(j0, LANE)].astype(BF16))
+                    right.append(gauss_tile(jnp.broadcast_to(dblk[r:r + 1], (SUB, LANE))))
+                return acc + mm(jnp.concatenate(left, 1), jnp.concatenate(right, 1), NT)
+
+            return lax.fori_loop(0, span // LANE, tile, acc)
+
+        return lax.fori_loop(0, CHUNK // SUB, group, acc)
+
+    pair_ref[...] = lax.fori_loop(0, last, chunk, jnp.zeros((SUB, KERN), F32))
+    dqkv_ref[1] = jnp.transpose(dkt[...] * scale).astype(BF16)
+    dqkv_ref[2] = jnp.transpose(dvt[...]).astype(BF16)
+    for when in sorted(jobs):
+        if when >= last:
+            for job in jobs[when]:
+                job()
+    for s in sums:
+        s.close()
+
+
+PASS_AT = (2, 4, 6, 8, 9)
+FINISH_AT = (5, 7, 10, 12, 14)
+FORWARD_AT = (8, 10, 13, 16, 16)
+
+
+def pair_distances(coords_ref, dist, span):
+    pts = coords_ref[...]
+    cols = jnp.transpose(jnp.concatenate([pts, jnp.zeros((5, span), F32)], 0))
+    acc = None
+    for a in range(3):
+        d = cols[:, a:a + 1] - pts[a:a + 1, :]
+        acc = d * d if acc is None else acc + d * d
+    dist[...] = jnp.sqrt(acc) * UNIT
+
+
+def attention_back_sums(qkv, do, probs, coords, heads, ny, nz, og, ig, pg):
+    _, span, inner = qkv.shape
+    width = og.shape[1]
+    ndp, parts = ny * nz, 2
+    cut = lambda g, p: g.reshape(p, ny, nz, g.shape[0] // (p * ndp), width)
+    og, ig, pg = cut(og, parts), cut(ig, parts), cut(pg, 1)[0]
+    shapes = [og.shape[1:]] * parts + [ig.shape[1:]] * parts + [pg.shape]
+    out = lambda a: jax.ShapeDtypeStruct(a.shape, BF16)
+    return pl.pallas_call(
+        functools.partial(back_kernel, heads, ny, nz),
+        out_shape=(jax.ShapeDtypeStruct((3, span, inner), BF16), jax.ShapeDtypeStruct((SUB, KERN), F32),
+                   out(og), out(ig), out(pg), jax.ShapeDtypeStruct((SUB, LANE), F32)),
+        in_specs=[VM] * 7, out_specs=[VM] * 6,
+        scratch_shapes=[pltpu.VMEM((span, span), F32), pltpu.VMEM((CHUNK * SUB, span), F32),
+                        pltpu.VMEM((span, inner), F32), pltpu.VMEM((span, inner), F32),
+                        pltpu.VMEM((inner, span), F32), pltpu.VMEM((inner, span), F32),
+                        *[s for shape in shapes for s in sum_scratch(ny, nz, shape[2], width)]],
+        compiler_params=pltpu.CompilerParams(collective_id=3, has_side_effects=True, vmem_limit_bytes=60 << 20),
+        name="attend_back_sums",
+    )(coords, qkv, do, probs, og, ig, pg)
 
 
 def leave_plain(n, x, dx, params, dqkv, h, grads, bias_grad, pair_grad, small, qkv_weight):
@@ -758,7 +869,7 @@
     dv, gain, shift = norm_back(x.astype(F32), params[0:1], dh1)
     hh = h.reshape(-1, h.shape[-1])
     qg = jnp.concatenate([mm(dqkv[s], hh, TN) for s in range(3)], 0)
-    og, ig, pg, qg, bias, pair = lax.psum((*grads, qg, bias_grad, pair_grad), "dp")
+    og, ig, pg, qg, bias, pair = lax.psum((*[g.astype(F32) for g in grads], qg, bias_grad, pair_grad), "dp")
     small = lax.psum(jnp.concatenate([gain, shift, small[0:6]], 0), ("dp", "mp"))
     local = sum(square(v) for v in (og, ig, pg, qg, bias, pair))
     total = lax.psum(local, "mp") + square(small)
@@ -782,14 +893,17 @@
     o, probs = attention(qkv, coords, lengths, pair_low, heads)
     block_out, dx, do, og, ig, pg, bg, small = middle(
         n, block_in, cotangent, dy_all, o, params, in_bias.reshape(1, -1), proj_weight, in_weight, out_weight)
-    dqkv, pair_grad = attention_back(qkv, do, probs, coords, lengths, heads)
     ny = n // 2 if ndp % (n // 2) == 0 else 1
-    rest = (block_in, dx, params, dqkv, h, (og, ig, pg), bg, pair_grad, small, qkv_weight)
-    if all(t % (8 * ndp) == 0 for t in (og.shape[0], pg.shape[0], 3 * qkv_weight.shape[1])):
-        done = leave(n, ny, ndp // ny, *rest)
+    nz = ndp // ny
+    inner = proj_weight.shape[0]
+    if lengths.shape[0] == 1 and inner % (8 * ndp) == 0 and og.shape[0] % (32 * ndp) == 0:
+        dqkv, pair_grad, og, ig, pg, squares = attention_back_sums(qkv, do, probs, coords, heads, ny, nz, og, ig, pg)
+        grad_input, qg, small, bias, pair, total = leave(
+            n, ny, nz, block_in, dx, params, dqkv, h, bg, pair_grad, squares, small, qkv_weight)
     else:
-        done = leave_plain(n, *rest)
-    grad_input, og, ig, pg, qg, small, bias, pair, total = done
+        dqkv, pair_grad = attention_back(qkv, do, probs, coords, lengths, heads)
+        grad_input, og, ig, pg, qg, small, bias, pair, total = leave_plain(
+            n, block_in, dx, params, dqkv, h, (og, ig, pg), bg, pair_grad, small, qkv_weight)
     grad_norm = jnp.sqrt(total[0, 0])
     clip = clip_level / jnp.maximum(grad_norm, clip_level)
     count = step_count[0].astype(F32)

time: 315 us -> 273 us (0.87); the launches traced: 311 us -> 273 us
  Pallas kernels: 282 us -> 245 us
    pallas_call x1, Pallas kernels: 124 us -> 47.7 us  [leave(): pl.pallas_call(functools.partial(leave_kernel, n, ny, nz), out_shape=(f(r...]
    pallas_call x1, Pallas kernels: 51.7 us -> 90 us  [attention_back_sums(): pl.pallas_call(functools.partial(back_kernel, heads, ny, nz), out_shape=(...]
where the time goes in v2:
time: 273 us
  Pallas kernels  245 us (90%)
  other arithmetic  17.8 us (7%)
  local copies, waits for them, and re-layouts  6.81 us (2%)
  between operations  3.77 us (1%)
    pallas_call x1, Pallas kernels, attention_back_sums(): pl.pallas_call(functools.partial(back_kernel, heads, ny, nz), out_shape=(...  90 us
    pallas_call x1, Pallas kernels, leave(): pl.pallas_call(functools.partial(leave_kernel, n, ny, nz), out_shape=(f(r...  47.7 us
    pallas_call x1, Pallas kernels, attention(): pl.pallas_call(functools.partial(fwd_kernel, heads, mols), out_shape=(jax...  47.6 us
    pallas_call x1, Pallas kernels, middle(): pl.pallas_call(functools.partial(middle_kernel, n), out_shape=(f(rows, wi...  41 us
    pallas_call x1, Pallas kernels, enter(): pl.pallas_call(functools.partial(enter_kernel, n), out_shape=(jax.ShapeDt...  18.6 us
    sub x7, other arithmetic, adam_step(): return (weight - rate * (ratio + decay * weight), first_new, second_new)  15 us
    unnamed x60, local copies, waits for them, and re-layouts  6.23 us

profile of v2, /device:TPU:0, one launch (start us, length us, event | category | flops | bytes accessed | tf_op | source)
XLA Modules:
  0.0 273.4 jit_solution(7508799655894164357)
XLA Ops:
  0.7 0.0 copy-start.22
  0.7 18.6 %enter.1 = (bf16[4,128,768]{2,1,0:T(8,128)(2,1)}, bf16[4,128,768]{2,1,0:T(8,128)(2,1)}, bf16[3,512,192]{2,1,0:T(8,128)(2,1)}) custom-call(bf16[128,768]{1,0:T(8,128)(2,1)} %x_ref.5, bf16[128,768]{1,0:T(8,128)(2,1)} %dy_ref.3, f32[5,768]{1,0:T(8,128)} %np_ref.5, f32[3,192,768]{2,1,0:T(8,128)} %w_hbm.3), custom_call_target="tpu_custom_call" | custom-call | tf_op jit(solution)/shard_map/enter/pallas_call | solution.py:390
  19.3 1.3 convert_element_type.23.w_ref
  20.6 47.6 %attend.1 = (bf16[512,192]{1,0:T(8,128)(2,1)}, bf16[4096,512]{1,0:T(8,128)(2,1)}) custom-call(s32[1,16]{1,0:T(1,128)} %len_ref.1, f32[3,512]{1,0:T(4,128)} %coords_ref.3, bf16[3,512,192]{2,1,0:T(8,128)(2,1)} %get-tuple-element.50.q_ref.k_ref.v_ref.qkv_ref, bf16[3,512,192]{2,1,0:T(8,128)(2,1)} %get-tuple-element.50.q_ref.k_ref.v_ref.qkv_ref, ...), custom_call_target="tpu_custom_call" | custom-call | tf_op jit(solution)/shard_map/attend/pallas_call | solution.py:125
  68.1 0.0 copy-done.22
  68.1 0.6 reshape.93.bias_ref
  68.7 41.0 %middle.1 = (f32[128,768]{1,0:T(8,128)}, f32[128,768]{1,0:T(8,128)}, bf16[512,192]{1,0:T(8,128)(2,1)}, bf16[768,768]{1,0:T(8,128)(2,1)}, bf16[768,768]{1,0:T(8,1...) custom-call(bf16[128,768]{1,0:T(8,128)(2,1)} %x_ref.5, bf16[128,768]{1,0:T(8,128)(2,1)} %dy_ref.3, ...), custom_call_target="tpu_custom_call" | custom-call | tf_op jit(solution)/shard_map/middle/pallas_call | solution.py:499
  109.8 90.0 %attend_back_sums.1 = (bf16[3,512,192]{2,1,0:T(8,128)(2,1)}, f32[8,128]{1,0:T(8,128)}, bf16[2,2,4,48,768]{4,3,2,1,0:T(8,128)(2,1)}, bf16[2,2,4,48,768]{4,3,2,1,0...) custom-call(f32[3,512]{1,0:T(4,128)} %coords_ref.3, ...), custom_call_target="tpu_custom_call" | custom-call | tf_op jit(solution)/shard_map/attend_back_sums/pallas_call | solution.py:852
  199.8 0.0 copy-start.10
  199.8 0.0 copy-start.11
  199.8 47.7 %leave.1 = (f32[128,768]{1,0:T(8,128)}, bf16[3,2,4,24,768]{4,3,2,1,0:T(8,128)(2,1)}, f32[8,768]{1,0:T(8,128)}, f32[8,768]{1,0:T(8,128)}, f32[8,128]{1,0:T(8,128)}, /*index=5*/f32[1,128]{1,0:T(1,128)}) custom-call(bf16[128,768]{1,0:T(8,128)(2,1)} %x_ref.5, f32[128,768]{1,0:T(8,128)} %get-tuple-element.53.dx_ref, f32[5,768]{1,0:T(8,128)} %np_ref.5, ...), custom_call_target="tpu_custom_call" | custom-call | tf_op jit(solution)/shard_map/leave/pallas_call | solution.py:733
  248.2 0.0 copy-done.10
  248.2 0.0 copy-done.11
  248.2 0.0 copy-start.1
  248.2 0.0 copy-start.4
  248.2 0.0 copy-start.5
  248.3 0.6 convert_multiply_fusion
  249.9 0.0 copy-done.1
  249.9 0.7 copy-done.4
  250.6 0.7 copy-done.5
  251.3 4.3 %multiply_subtract_fusion = (f32[768,768]{1,0:T(8,128)}, f32[768,768]{1,0:T(8,128)}, f32[768,768]{1,0:T(8,128)}) fusion(f32[768,768]{1,0:T(8,128)S(1)} %copy-done.1, f32[]{:T(128)} %bitcast.7, f32[]{:T(128)} %bitcast.6, f32[2,2,4,48,768]{4,3,2,1,0:T(8,128)S(1)} %get-tuple-element.95, f32[768,768]{1,0:T(8,128)S(1)} %copy-done.4, f32[768,768]{1,0:T(8,128)S(1)} %copy-done.5), kind=kLoop, calls=%fused_computation.9 | loop fusion | flops 8847360 | bytes 16515080 | tf_op jit(solution)/shard_map/sub | solution.py:884
  255.7 0.0 copy-done.2
  255.7 0.0 copy-done.6
  255.7 1.3 copy-done.7
  257.0 0.0 copy-start.24
  257.0 0.0 copy-start.25
  257.0 0.0 copy-start.23
  257.0 0.0 copy-start.26
  257.1 0.0 copy-start.27
  257.1 0.0 copy-start.28
  257.1 0.0 copy-start.18
  257.1 0.0 copy-start.3
  257.1 0.0 copy-start.13
  257.1 0.0 copy-start.14
  257.1 4.1 %multiply_subtract_fusion.1 = (f32[768,768]{1,0:T(8,128)}, f32[768,768]{1,0:T(8,128)}, f32[768,768]{1,0:T(8,128)}) fusion(f32[768,768]{1,0:T(8,128)S(1)} %copy-done.2, f32[]{:T(128)} %bitcast.7, f32[]{:T(128)} %bitcast.6, f32[2,2,4,48,768]{4,3,2,1,0:T(8,128)S(1)} %get-tuple-element.96, f32[768,768]{1,0:T(8,128)S(1)} %copy-done.6, f32[768,768]{1,0:T(8,128)S(1)} %copy-done.7), kind=kLoop, calls=%fused_computation.11 | loop fusion | flops 8847360 | bytes 16515080 | tf_op jit(solution)/shard_map/sub | solution.py:884
  261.2 0.0 copy-done.15
  261.2 0.0 copy-done.19
  261.2 0.0 copy-done.20
  261.2 0.0 copy-done.21
  261.2 0.6 multiply_subtract_fusion.4
  261.9 0.8 multiply_reduce_fusion
  262.6 0.0 copy-done.24
  262.6 0.0 copy-done.25
  262.7 0.6 multiply_subtract_fusion.5
  263.3 0.0 copy-done.23
  263.3 0.0 copy-done.26
  263.3 0.0 copy-done.27
  263.3 0.0 copy-done.28
  263.3 0.6 multiply_subtract_fusion.6
  263.9 0.0 copy-done.18
  264.0 0.0 copy-done.3
  264.0 0.0 copy-done.13
  264.0 0.0 copy-done.14
  264.0 0.0 copy-start.8
  264.0 0.0 copy-start.9
  264.0 1.5 multiply_subtract_fusion.3
  265.5 0.2 convert_multiply_fusion.2
  265.7 0.7 copy-done.8
  266.3 0.5 copy-done.9
  266.9 0.7 copy-done
  267.5 3.2 %multiply_subtract_fusion.2 = (f32[3,192,768]{2,1,0:T(8,128)}, f32[3,192,768]{2,1,0:T(8,128)}, f32[3,192,768]{2,1,0:T(8,128)}) fusion(f32[3,192,768]{2,1,0:T(8,128)S(1)} %copy-done, f32[]{:T(128)} %bitcast.7, f32[]{:T(128)} %bitcast.6, f32[3,2,4,24,768]{4,3,2,1,0:T(8,128)S(1)} %convert_multiply_fusion.2, f32[3,192,768]{2,1,0:T(8,128)S(1)} %copy-done.8, ...), kind=kLoop, calls=%fused_computation.16 | loop fusion | flops 6635520 | bytes 12386312 | tf_op jit(solution)/shard_map/sub | solution.py:884
  270.8 0.7 copy.53
  271.5 0.0 copy-done.17
  271.5 0.7 copy.54
  (14 shorter events, 0.1 us)
Async XLA Ops:
  0.7 67.5 %copy-start.22 = (f32[768]{0:T(1024)S(1)}, f32[768]{0:T(1024)}, u32[]{:S(2)}) copy-start(f32[768]{0:T(1024)} %param.35) | copy-start | bytes 9220
  199.8 48.4 %copy-start.10 = (bf16[2,2,4,48,768]{4,3,2,1,0:T(8,128)(2,1)S(1)}, bf16[2,2,4,48,768]{4,3,2,1,0:T(8,128)(2,1)}, u32[]{:S(2)}) copy-start(bf16[2,2,4,48,768]{4,3,2,1,0:T(8,128)(2,1)} %get-tuple-element.72) | copy-start | bytes 3538948
  199.8 48.4 %copy-start.11 = (bf16[2,2,4,48,768]{4,3,2,1,0:T(8,128)(2,1)S(1)}, bf16[2,2,4,48,768]{4,3,2,1,0:T(8,128)(2,1)}, u32[]{:S(2)}) copy-start(bf16[2,2,4,48,768]{4,3,2,1,0:T(8,128)(2,1)} %get-tuple-element.70) | copy-start | bytes 3538948
  248.2 1.7 copy-start.1
  248.2 2.4 copy-start.4
  248.2 3.1 %copy-start.5 = (f32[768,768]{1,0:T(8,128)S(1)}, f32[768,768]{1,0:T(8,128)}, u32[]{:S(2)}) copy-start(f32[768,768]{1,0:T(8,128)} %param.43) | copy-start | bytes 7077892
  251.3 4.3 %copy-start.2 = (f32[768,768]{1,0:T(8,128)S(1)}, f32[768,768]{1,0:T(8,128)}, u32[]{:S(2)}) copy-start(f32[768,768]{1,0:T(8,128)} %iw_hbm.1) | copy-start | bytes 7077892
  251.3 4.3 %copy-start.6 = (f32[768,768]{1,0:T(8,128)S(1)}, f32[768,768]{1,0:T(8,128)}, u32[]{:S(2)}) copy-start(f32[768,768]{1,0:T(8,128)} %param.48) | copy-start | bytes 7077892
  251.3 5.6 %copy-start.7 = (f32[768,768]{1,0:T(8,128)S(1)}, f32[768,768]{1,0:T(8,128)}, u32[]{:S(2)}) copy-start(f32[768,768]{1,0:T(8,128)} %param.41) | copy-start | bytes 7077892
  257.0 4.2 %copy-start.15 = (f32[5,768]{1,0:T(8,128)S(1)}, f32[5,768]{1,0:T(8,128)}, u32[]{:S(2)}) copy-start(f32[5,768]{1,0:T(8,128)} %np_ref.5) | copy-start | bytes 46084
  257.0 4.2 %copy-start.19 = (f32[5,768]{1,0:T(8,128)S(1)}, f32[5,768]{1,0:T(8,128)}, u32[]{:S(2)}) copy-start(f32[5,768]{1,0:T(8,128)} %param.51) | copy-start | bytes 46084
  257.0 4.2 %copy-start.20 = (f32[5,768]{1,0:T(8,128)S(1)}, f32[5,768]{1,0:T(8,128)}, u32[]{:S(2)}) copy-start(f32[5,768]{1,0:T(8,128)} %param.44) | copy-start | bytes 46084
  257.0 4.2 %copy-start.21 = (f32[8,768]{1,0:T(8,128)S(1)}, f32[8,768]{1,0:T(8,128)}, u32[]{:S(2)}) copy-start(f32[8,768]{1,0:T(8,128)} %get-tuple-element.73) | copy-start | bytes 73732
  257.0 5.6 %copy-start.24 = (f32[768]{0:T(1024)S(1)}, f32[768]{0:T(1024)}, u32[]{:S(2)}) copy-start(f32[768]{0:T(1024)} %param.49) | copy-start | bytes 9220
  257.0 5.6 %copy-start.25 = (f32[768]{0:T(1024)S(1)}, f32[768]{0:T(1024)}, u32[]{:S(2)}) copy-start(f32[768]{0:T(1024)} %param.42) | copy-start | bytes 9220
  257.0 6.3 %copy-start.23 = (f32[8,128]{1,0:T(8,128)S(1)}, f32[8,128]{1,0:T(8,128)}, u32[]{:S(2)}) copy-start(f32[8,128]{1,0:T(8,128)} %param.33) | copy-start | bytes 12292
  257.0 6.3 %copy-start.26 = (f32[8,128]{1,0:T(8,128)S(1)}, f32[8,128]{1,0:T(8,128)}, u32[]{:S(2)}) copy-start(f32[8,128]{1,0:T(8,128)} %param.47) | copy-start | bytes 12292
  257.1 6.2 %copy-start.27 = (f32[8,128]{1,0:T(8,128)S(1)}, f32[8,128]{1,0:T(8,128)}, u32[]{:S(2)}) copy-start(f32[8,128]{1,0:T(8,128)} %param.40) | copy-start | bytes 12292
  257.1 6.2 %copy-start.28 = (f32[8,128]{1,0:T(8,128)S(1)}, f32[8,128]{1,0:T(8,128)}, u32[]{:S(2)}) copy-start(f32[8,128]{1,0:T(8,128)} %get-tuple-element.69) | copy-start | bytes 12292
  257.1 6.9 %copy-start.18 = (bf16[2,4,24,768]{3,2,1,0:T(8,128)(2,1)S(1)}, bf16[2,4,24,768]{3,2,1,0:T(8,128)(2,1)}, u32[]{:S(2)}) copy-start(bf16[2,4,24,768]{3,2,1,0:T(8,128)(2,1)} %get-tuple-element.68) | copy-start | bytes 884740
  257.1 6.9 %copy-start.3 = (f32[192,768]{1,0:T(8,128)S(1)}, f32[192,768]{1,0:T(8,128)}, u32[]{:S(2)}) copy-start(f32[192,768]{1,0:T(8,128)} %pw_hbm.1) | copy-start | bytes 1769476
  257.1 6.9 %copy-start.13 = (f32[192,768]{1,0:T(8,128)S(1)}, f32[192,768]{1,0:T(8,128)}, u32[]{:S(2)}) copy-start(f32[192,768]{1,0:T(8,128)} %param.46) | copy-start | bytes 1769476
  257.1 6.9 %copy-start.14 = (f32[192,768]{1,0:T(8,128)S(1)}, f32[192,768]{1,0:T(8,128)}, u32[]{:S(2)}) copy-start(f32[192,768]{1,0:T(8,128)} %param.39) | copy-start | bytes 1769476
  263.9 1.6 copy-start.12
  264.0 2.3 copy-start.8
  264.0 2.9 %copy-start.9 = (f32[3,192,768]{2,1,0:T(8,128)S(1)}, f32[3,192,768]{2,1,0:T(8,128)}, u32[]{:S(2)}) copy-start(f32[3,192,768]{2,1,0:T(8,128)} %param.38) | copy-start | bytes 5308420
  265.5 2.0 copy-start
  267.5 3.3 %copy-start.16 = (f32[128,768]{1,0:T(8,128)S(1)}, f32[128,768]{1,0:T(8,128)}, u32[]{:S(2)}) copy-start(f32[128,768]{1,0:T(8,128)} %get-tuple-element.121) | copy-start | bytes 1179652
  267.5 4.0 %copy-start.17 = (f32[128,768]{1,0:T(8,128)S(1)}, f32[128,768]{1,0:T(8,128)}, u32[]{:S(2)}) copy-start(f32[128,768]{1,0:T(8,128)} %get-tuple-element.122) | copy-start | bytes 1179652

commit v3 on v1

v3 whole, which is shorter than its diff:
```python
import functools
import math

import jax
import jax.numpy as jnp
from jax import lax
from jax.experimental import pallas as pl
from jax.experimental.pallas import tpu as pltpu
from jax.sharding import PartitionSpec as P

ln_eps = 1e-05
beta_one = 0.9
beta_two = 0.999
adam_eps = 1e-08
clip_level = 1.0

F32, BF16 = jnp.float32, jnp.bfloat16
MESH = pl.DeviceIdType.MESH
NN = (((1,), (0,)), ((), ()))
NT = (((1,), (1,)), ((), ()))
TN = (((0,), (0,)), ((), ()))
VM = pl.BlockSpec(memory_space=pltpu.VMEM)
HBM = pl.BlockSpec(memory_space=pl.ANY)
DMA = pltpu.SemaphoreType.DMA
KERN = 128
LANE = 128
SUB = 8
TALL = 32
KS = math.sqrt(0.5 * math.log2(math.e))
UNIT = KS / (12.8 / KERN)


def pair_distances(coords_ref, dist, span):
    pts = coords_ref[...]
    cols = jnp.transpose(jnp.concatenate([pts, jnp.zeros((5, span), F32)], 0))
    acc = None
    for a in range(3):
        d = cols[:, a:a + 1] - pts[a:a + 1, :]
        acc = d * d if acc is None else acc + d * d
    dist[...] = jnp.sqrt(acc) * UNIT


def pair_labels(len_ref, b, labs, labr, span, mols):
    lanes = lax.broadcasted_iota(jnp.int32, (SUB, span), 1)
    lc = jnp.zeros((SUB, span), F32)
    end = jnp.int32(0)
    for m in range(mols):
        end = end + len_ref[b, m]
        lc = lc + (lanes >= end).astype(F32)
    labr[...] = lc
    labs[...] = jnp.broadcast_to(jnp.transpose(lc)[:, 0:1], (span, LANE))


def tile_range(len_ref, b, first, last, span, mols):
    lo = jnp.int32(0)
    hi = jnp.int32(span)
    end = jnp.int32(0)
    for m in range(mols):
        end = end + len_ref[b, m]
        lo = jnp.where(end <= first, end, lo)
        hi = jnp.where((end > last) & (end < hi), end, hi)
    return lo // LANE, (hi + LANE - 1) // LANE


def row_of(block, r):
    return jnp.broadcast_to(block[r:r + 1], (SUB, LANE))


def gauss_tile(drow):
    sub = lax.broadcasted_iota(jnp.int32, (SUB, LANE), 0).astype(F32) * KS
    base = drow - sub
    parts = []
    for c in range(KERN // SUB):
        t = base - (KS * SUB * c)
        parts.append(jnp.exp2(-(t * t)))
    return jnp.concatenate(parts, 0).astype(BF16)


def wide(ref, rows):
    return jnp.concatenate([ref[t, rows, :] for t in range(ref.shape[0])], 1)


def fwd_kernel(heads, mols, len_ref, coords_ref, qkv_ref, w_ref, o_ref, p_ref, dist, labs, labr, sc):
    hd, span = qkv_ref.shape[2:]
    b = pl.program_id(0)
    scale = 1.0 / math.sqrt(hd)
    pair_distances(coords_ref, dist, span)
    pair_labels(len_ref, b, labs, labr, span, mols)
    wb = w_ref[...]
    step = LANE

    def fill(i, carry):
        r0 = pl.multiple_of(i * step, step)
        sc[:, pl.ds(r0, step), :] = jnp.full((span // LANE, step, LANE), -1e30, F32)
        return carry

    lax.fori_loop(0, SUB * span // step, fill, 0)

    def group(g, carry):
        i0 = pl.multiple_of(g * TALL, TALL)
        lo, hi = tile_range(len_ref, b, i0, i0 + TALL - 1, span, mols)

        def tile(jt, carry):
            j0 = pl.multiple_of(jt * LANE, LANE)
            lab = labr[:, pl.ds(j0, LANE)]
            dblk = dist[pl.ds(i0, TALL), pl.ds(j0, LANE)]
            lblk = labs[pl.ds(i0, TALL), :]
            for r in range(0, TALL, 2):
                bias = mm(wb, jnp.concatenate([gauss_tile(row_of(dblk, r)), gauss_tile(row_of(dblk, r + 1))], 1))
                for k in range(2):
                    sc[jt, pl.ds(i0 + r + k, SUB, span), :] = jnp.where(
                        row_of(lblk, r + k) == lab, bias[:, k * LANE:(k + 1) * LANE], -1e30)
            return carry

        return lax.fori_loop(lo, hi, tile, carry)

    lax.fori_loop(0, span // TALL, group, 0)

    def head(h, carry):
        for c in range(span // step):
            cols = pl.ds(c * step, step)
            rows = pl.ds(pl.multiple_of(h * span + c * step, step), step)
            s = mm(qkv_ref[0, h, :, cols], qkv_ref[1, h], TN) * scale + wide(sc, rows)
            e = jnp.exp(s - jnp.max(s, axis=-1, keepdims=True))
            p = (e * (1.0 / jnp.sum(e, axis=-1, keepdims=True))).astype(BF16)
            p_ref[rows, :] = p
            o_ref[h, :, cols] = mm(qkv_ref[2, h], p, NT).astype(BF16)
        return carry

    lax.fori_loop(0, heads, head, 0)


def attention(qkv, coords, lengths, pair_low):
    _, heads, hd, rows = qkv.shape
    blocks, mols = lengths.shape
    span = rows // blocks
    w = jnp.pad(pair_low, ((0, SUB - heads), (0, 0)))
    return pl.pallas_call(
        functools.partial(fwd_kernel, heads, mols),
        out_shape=(jax.ShapeDtypeStruct((heads, hd, rows), BF16),
                   jax.ShapeDtypeStruct((blocks * heads * span, span), BF16)),
        grid_spec=pltpu.PrefetchScalarGridSpec(
            num_scalar_prefetch=1, grid=(blocks,),
            in_specs=[pl.BlockSpec((3, span), lambda b, *_: (0, b)),
                      pl.BlockSpec((3, heads, hd, span), lambda b, *_: (0, 0, 0, b)),
                      pl.BlockSpec((SUB, KERN), lambda b, *_: (0, 0))],
            out_specs=[pl.BlockSpec((heads, hd, span), lambda b, *_: (0, 0, b)),
                       pl.BlockSpec((heads * span, span), lambda b, *_: (b, 0))],
            scratch_shapes=[pltpu.VMEM((span, span), F32), pltpu.VMEM((span, LANE), F32),
                            pltpu.VMEM((SUB, span), F32), pltpu.VMEM((span // LANE, SUB * span, LANE), F32)]),
        compiler_params=pltpu.CompilerParams(vmem_limit_bytes=60 << 20),
        name="attend",
    )(lengths, coords, qkv, w)


def back_pairs(heads, coords_ref, qkv_ref, do_ref, p_ref, dqkv_ref, dist, ds, beside):
    hd, span = do_ref.shape[1:]
    scale = 1.0 / math.sqrt(hd)
    step = LANE
    pair_distances(coords_ref, dist, span)
    if heads < SUB:
        ds[...] = jnp.zeros_like(ds)

    def head(h, carry):
        beside(h, 0, heads)
        dk = jnp.zeros((hd, span), F32)
        dv = jnp.zeros((hd, span), F32)
        for c in range(span // step):
            cols = pl.ds(c * step, step)
            rows = pl.ds(pl.multiple_of(h * span + c * step, step), step)
            pb = p_ref[rows, :]
            p = pb.astype(F32)
            dp = mm(do_ref[h, :, cols], qkv_ref[2, h], TN)
            d = p * (dp - jnp.sum(p * dp, axis=-1, keepdims=True))
            for t in range(span // LANE):
                ds[t, rows, :] = d[:, t * LANE:(t + 1) * LANE]
            low = d.astype(BF16)
            dqkv_ref[0, h, :, cols] = (mm(qkv_ref[1, h], low, NT) * scale).astype(BF16)
            dk = dk + mm(qkv_ref[0, h, :, cols], low)
            dv = dv + mm(do_ref[h, :, cols], pb)
        dqkv_ref[1, h] = (dk * scale).astype(BF16)
        dqkv_ref[2, h] = dv.astype(BF16)
        return carry

    lax.fori_loop(0, heads, head, 0)

    def group(g, acc):
        beside(heads + g, heads, heads + span // SUB)
        i0 = pl.multiple_of(g * SUB, SUB)

        left, right = [], []
        for jt in range(span // LANE):
            dblk = dist[pl.ds(i0, SUB), jt * LANE:(jt + 1) * LANE]
            for r in range(SUB // 2):
                pair = (r, r + SUB // 2)
                left.append(jnp.concatenate([ds[jt, pl.ds(i0 + k, SUB, span), :] for k in pair], 0).astype(BF16))
                right.append(jnp.concatenate([gauss_tile(row_of(dblk, k)) for k in pair], 0))
        return acc + mm(jnp.concatenate(left, 1), jnp.concatenate(right, 1), NT)

    acc = lax.fori_loop(0, span // SUB, group, jnp.zeros((2 * SUB, 2 * KERN), F32))
    return acc[:SUB, :KERN] + acc[SUB:, KERN:]


def bwd_kernel(heads, coords_ref, qkv_ref, do_ref, p_ref, dqkv_ref, pair_ref, dist, ds):
    @pl.when(pl.program_id(0) == 0)
    def _():
        pair_ref[...] = jnp.zeros_like(pair_ref)

    pair_ref[...] += back_pairs(heads, coords_ref, qkv_ref, do_ref, p_ref, dqkv_ref, dist, ds, lambda *_: None)


def attention_back(qkv, do, probs, coords):
    _, heads, hd, rows = qkv.shape
    span = probs.shape[1]
    wide = pl.BlockSpec((3, heads, hd, span), lambda b: (0, 0, 0, b))
    return pl.pallas_call(
        functools.partial(bwd_kernel, heads),
        out_shape=(jax.ShapeDtypeStruct(qkv.shape, BF16), jax.ShapeDtypeStruct((SUB, KERN), F32)),
        grid=(rows // span,),
        in_specs=[pl.BlockSpec((3, span), lambda b: (0, b)), wide,
                  pl.BlockSpec((heads, hd, span), lambda b: (0, 0, b)),
                  pl.BlockSpec((heads * span, span), lambda b: (b, 0))],
        out_specs=[wide, pl.BlockSpec((SUB, KERN), lambda b: (0, 0))],
        scratch_shapes=[pltpu.VMEM((span, span), F32), pltpu.VMEM((span // LANE, SUB * span, LANE), F32)],
        compiler_params=pltpu.CompilerParams(vmem_limit_bytes=60 << 20),
        name="attend_back",
    )(coords, qkv, do, probs)


def mm(a, b, dims=NN):
    return lax.dot_general(a, b, dims, preferred_element_type=F32)


def remote(src, dst, send, recv, axis, target):
    return pltpu.make_async_remote_copy(
        src_ref=src, dst_ref=dst, send_sem=send, recv_sem=recv,
        device_id={axis: target}, device_id_type=MESH)


def greet(sizes):
    barrier = pltpu.get_barrier_semaphore()
    total = 0
    for axis, size in sizes.items():
        me = lax.axis_index(axis)
        for k in range(1, size):
            pl.semaphore_signal(barrier, inc=1, device_id={axis: lax.rem(me + k, size)}, device_id_type=MESH)
        total += size - 1
    pl.semaphore_wait(barrier, total)


class Seat:
    def __init__(self, n):
        self.n, self.nx = n, n // 2
        self.me = lax.axis_index("mp")
        self.core = lax.rem(self.me, 2)
        self.x = self.me // 2
        self.sib = self.me + 1 - 2 * self.core

    def chip(self, k):
        return lax.rem(self.x + 1 + k, self.nx)

    def source(self, k):
        return lax.rem(self.x + self.nx - 1 - k, self.nx)


def scatter_scratch(n, rows, width):
    nx = n // 2
    buf = lambda m: pltpu.VMEM((m, rows, width), BF16)
    return [buf(nx), buf(nx), buf(max(nx - 1, 1)), buf(max(nx - 1, 1)), DMA((nx,)), DMA((nx,)),
            DMA((max(nx - 1, 1),)), DMA((max(nx - 1, 1),))]


class Scatter:
    def __init__(self, seat, scratch):
        self.seat = seat
        self.out1, self.in1, self.out2, self.in2, self.s1, self.r1, self.s2, self.r2 = scratch

    def first(self, k):
        return remote(self.out1.at[k], self.in1.at[k], self.s1.at[k], self.r1.at[k], "mp", self.seat.sib)

    def second(self, k):
        target = self.seat.chip(k) * 2 + self.seat.core
        return remote(self.out2.at[k], self.in2.at[k], self.s2.at[k], self.r2.at[k], "mp", target)

    def push(self, block):
        for k in range(self.seat.nx):
            self.out1[k] = block(self.seat.chip(k) * 2 + 1 - self.seat.core).astype(BF16)
            self.first(k).start()

    def pass_on(self, block):
        seat = self.seat
        parts = [block(seat.chip(k) * 2 + seat.core) for k in range(seat.nx)]
        for k in range(seat.nx):
            self.first(k).wait_recv()
            whole = parts[k] + self.in1[k].astype(F32)
            if k < seat.nx - 1:
                self.out2[k] = whole.astype(BF16)
                self.second(k).start()
        return whole

    def finish(self, whole):
        for k in range(self.seat.nx - 1):
            self.second(k).wait_recv()
            whole = whole + self.in2[k].astype(F32)
        return whole

    def drain(self):
        for k in range(self.seat.nx):
            self.first(k).wait_send()
        for k in range(self.seat.nx - 1):
            self.second(k).wait_send()


def gather_scratch(n):
    nx = n // 2
    return [DMA((max(nx - 1, 1),)), DMA((max(nx - 1, 1),)), DMA((nx,)), DMA((nx,))]


class Gather:
    def __init__(self, seat, rows, scratch):
        self.seat, self.rows = seat, rows
        self.sx, self.rx, self.sc, self.rc = scratch

    def across(self, k):
        r = self.rows.at[self.seat.me]
        return remote(r, r, self.sx.at[k], self.rx.at[k], "mp", self.seat.chip(k) * 2 + self.seat.core)

    def along(self, k):
        chip = self.seat.x if k == self.seat.nx - 1 else self.seat.source(k)
        r = self.rows.at[chip * 2 + self.seat.core]
        return remote(r, r, self.sc.at[k], self.rc.at[k], "mp", self.seat.sib)

    def start(self):
        for k in range(self.seat.nx - 1):
            self.across(k).start()
        self.along(self.seat.nx - 1).start()

    def forward(self):
        for k in range(self.seat.nx - 1):
            self.across(k).wait_recv()
            self.along(k).start()

    def finish(self):
        for k in range(self.seat.nx):
            self.along(k).wait_recv()

    def drain(self):
        for k in range(self.seat.nx - 1):
            self.across(k).wait_send()
        for k in range(self.seat.nx):
            self.along(k).wait_send()


def centre(rows):
    c = rows - jnp.mean(rows, axis=-1, keepdims=True)
    r = lax.rsqrt(jnp.mean(c * c, axis=-1, keepdims=True) + ln_eps)
    return c * r, r


def norm_back(rows, gain, e):
    vhat, r = centre(rows)
    ge = e * gain
    dv = r * (ge - jnp.mean(ge, axis=-1, keepdims=True) - vhat * jnp.mean(ge * vhat, axis=-1, keepdims=True))
    return dv, jnp.sum(e * vhat, axis=0, keepdims=True), jnp.sum(e, axis=0, keepdims=True)


def enter_kernel(n, x_ref, dy_ref, np_ref, w_hbm, h_ref, dyall_ref, qkv_ref, w32, wsem, *sems):
    seat = Seat(n)
    load = pltpu.make_async_copy(w_hbm, w32, wsem)
    load.start()
    greet({"mp": n})
    vhat, _ = centre(x_ref[...].astype(F32))
    h_ref[seat.me] = (vhat * np_ref[0:1] + np_ref[1:2]).astype(BF16)
    dyall_ref[seat.me] = dy_ref[...]
    gh = Gather(seat, h_ref, sems[:4])
    gd = Gather(seat, dyall_ref, sems[4:])
    gh.start()
    load.wait()
    gh.forward()
    gd.start()
    gh.finish()
    rows = h_ref.shape[1]
    for s in range(3):
        w = w32[s].astype(BF16)

        def block(b, carry):
            out = mm(w, h_ref[b], NT)
            qkv_ref[s, :, :, pl.ds(pl.multiple_of(b * rows, rows), rows)] = out.reshape(
                *qkv_ref.shape[1:3], rows).astype(BF16)
            return carry

        lax.fori_loop(0, n, block, 0)
    gd.forward()
    gd.finish()
    gh.drain()
    gd.drain()


def enter(n, heads, x, dy, params, qkv_weight):
    rows, width = x.shape
    _, inner, _ = qkv_weight.shape
    return pl.pallas_call(
        functools.partial(enter_kernel, n),
        out_shape=(jax.ShapeDtypeStruct((n, rows, width), BF16), jax.ShapeDtypeStruct((n, rows, width), BF16),
                   jax.ShapeDtypeStruct((3, heads, inner // heads, n * rows), BF16)),
        in_specs=[VM, VM, VM, HBM], out_specs=[VM, VM, VM],
        scratch_shapes=[pltpu.VMEM(qkv_weight.shape, F32), DMA, *gather_scratch(n), *gather_scratch(n)],
        compiler_params=pltpu.CompilerParams(collective_id=0, has_side_effects=True),
        name="enter",
    )(x, dy, params, qkv_weight)


def middle_kernel(n, x_ref, dy_ref, dyall_ref, o_ref, np_ref, bias_ref, pw_hbm, iw_hbm, ow_hbm,
                  block_ref, mid_ref, do_ref, og_ref, ig_ref, pg_ref, bg_ref, small_ref,
                  pw32, iw32, ow32, pw, iw, ow, h2, da, act, dpre, dact, wsem, *rest):
    seat = Seat(n)
    rows, width = x_ref.shape
    loads = [pltpu.make_async_copy(a, b, wsem.at[i])
             for i, (a, b) in enumerate([(pw_hbm, pw32), (ow_hbm, ow32), (iw_hbm, iw32)])]
    for c in loads:
        c.start()
    scat = [Scatter(seat, rest[8 * i:8 * i + 8]) for i in range(3)]
    gath = [Gather(seat, r, rest[24 + 4 * i:28 + 4 * i]) for i, r in enumerate((h2, da))]
    greet({"mp": n})
    at = lambda b: pl.ds(pl.multiple_of(b * rows, rows), rows)

    loads[0].wait()
    pw[...] = pw32[...].astype(BF16)
    attn_block = lambda b: mm(o_ref[:, at(b)], pw[...], TN)
    scat[0].push(attn_block)
    loads[1].wait()
    ow[...] = ow32[...].astype(BF16)
    whole = scat[0].pass_on(attn_block)
    loads[2].wait()
    iw[...] = iw32[...].astype(BF16)

    def back_act(b, carry):
        dact[b] = mm(dyall_ref[b], ow[...], NT)
        return carry

    lax.fori_loop(0, n, back_act, 0)
    mid = x_ref[...].astype(F32) + scat[0].finish(whole)
    vhat, _ = centre(mid)
    h2[seat.me] = (vhat * np_ref[2:3] + np_ref[3:4]).astype(BF16)
    mid_ref[...] = mid
    gath[0].start()
    gath[0].forward()
    gath[0].finish()

    bg_ref[...] = jnp.zeros_like(bg_ref)
    bias = bias_ref[...].astype(BF16).astype(F32)

    def feed_block(b):
        pre = mm(h2[b], iw[...], NT) + bias
        phi = 0.5 + 0.5 * lax.erf(pre * math.sqrt(0.5))
        act[b] = (pre * phi).astype(BF16)
        slope = phi + pre * (jnp.exp(-0.5 * pre * pre) * (1.0 / math.sqrt(2.0 * math.pi)))
        d = (dact[b] * slope).astype(BF16)
        dpre[b] = d
        bg_ref[...] += jnp.sum(d.astype(F32), axis=0, keepdims=True)
        return mm(d, iw[...])

    scat[1].push(feed_block)
    whole = scat[1].pass_on(feed_block)
    out_block = lambda b: mm(act[b], ow[...])
    scat[2].push(out_block)
    dh2 = scat[1].finish(whole)
    dv, gain, shift = norm_back(mid_ref[...], np_ref[2:3], dh2)
    dy = dy_ref[...].astype(F32)
    dx1 = dy + dv
    da[seat.me] = dx1.astype(BF16)
    gath[1].start()
    small_ref[...] = jnp.concatenate(
        [gain, shift, jnp.sum(dy, axis=0, keepdims=True), jnp.zeros((5, width), F32)], 0)
    whole = scat[2].pass_on(out_block)
    gath[1].forward()

    hidden = iw.shape[0]
    step = LANE if hidden % LANE == 0 else hidden

    def grads(i, carry):
        c0 = pl.multiple_of(i * step, step)
        acc_o = jnp.zeros((step, width), F32)
        acc_i = jnp.zeros((step, width), F32)
        for b in range(n):
            acc_o += mm(act[b, :, pl.ds(c0, step)], dyall_ref[b], TN)
            acc_i += mm(dpre[b, :, pl.ds(c0, step)], h2[b], TN)
        og_ref[pl.ds(c0, step), :] = acc_o.astype(BF16)
        ig_ref[pl.ds(c0, step), :] = acc_i.astype(BF16)
        return carry

    lax.fori_loop(0, hidden // step, grads, 0)
    block_ref[...] = mid_ref[...] + scat[2].finish(whole) + np_ref[4:5]
    mid_ref[...] = dx1
    gath[1].finish()

    def heads_block(b, acc):
        out = mm(pw[...], da[b], NT)
        do_ref[:, :, at(b)] = out.reshape(*do_ref.shape[:2], rows).astype(BF16)
        return acc + mm(o_ref[:, at(b)], da[b])

    pg_ref[...] = lax.fori_loop(0, n, heads_block, jnp.zeros(pg_ref.shape, F32)).astype(BF16)
    for c in scat + gath:
        c.drain()


def middle(n, x, dy, dy_all, o, params, bias, proj_weight, in_weight, out_weight):
    rows, width = x.shape
    hidden = in_weight.shape[0]
    inner = proj_weight.shape[0]
    heads, hd, _ = o.shape
    f = lambda *s: jax.ShapeDtypeStruct(s, F32)
    return pl.pallas_call(
        functools.partial(middle_kernel, n),
        out_shape=(f(rows, width), f(rows, width), jax.ShapeDtypeStruct(o.shape, BF16),
                   *[jax.ShapeDtypeStruct((t, width), BF16) for t in (hidden, hidden, inner)], f(1, hidden), f(8, width)),
        in_specs=[VM] * 6 + [HBM] * 3, out_specs=[VM] * 8,
        scratch_shapes=[pltpu.VMEM((inner, width), F32), pltpu.VMEM((hidden, width), F32),
                        pltpu.VMEM((hidden, width), F32), pltpu.VMEM((inner, width), BF16),
                        pltpu.VMEM((hidden, width), BF16), pltpu.VMEM((hidden, width), BF16),
                        pltpu.VMEM((n, rows, width), BF16), pltpu.VMEM((n, rows, width), BF16),
                        pltpu.VMEM((n, rows, hidden), BF16), pltpu.VMEM((n, rows, hidden), BF16),
                        pltpu.VMEM((n, rows, hidden), F32), DMA((3,)),
                        *[s for _ in range(3) for s in scatter_scratch(n, rows, width)],
                        *gather_scratch(n), *gather_scratch(n)],
        compiler_params=pltpu.CompilerParams(collective_id=1, has_side_effects=True, vmem_limit_bytes=60 << 20),
        name="middle",
    )(x, dy, dy_all, o.reshape(inner, -1), params, bias, proj_weight, in_weight, out_weight)


class Grid:
    def __init__(self, ny, nz):
        self.ny, self.nz = ny, nz
        self.me = lax.axis_index("dp")
        self.z, self.y = self.me // ny, lax.rem(self.me, ny)

    def yto(self, k):
        return lax.rem(self.y + 1 + k, self.ny)

    def yfrom(self, k):
        return lax.rem(self.y + self.ny - 1 - k, self.ny)

    def zto(self, k):
        return lax.rem(self.z + 1 + k, self.nz)

    def zfrom(self, k):
        return lax.rem(self.z + self.nz - 1 - k, self.nz)


def sum_scratch(ny, nz, chunk, width):
    y, z = max(ny - 1, 1), max(nz - 1, 1)
    return [pltpu.VMEM((y, nz, chunk, width), BF16), pltpu.VMEM((z, chunk, width), BF16),
            pltpu.VMEM((z, chunk, width), BF16), DMA((y,)), DMA((y,)), DMA((z,)), DMA((z,))]


class Sum:
    count = 7

    def __init__(self, grid, grad, own, scratch):
        self.grid, self.grad, self.own = grid, grad, own
        self.ia, self.ob, self.ib, self.sa, self.ra, self.sb, self.rb = scratch

    def copy_y(self, k):
        g = self.grid
        return remote(self.grad.at[g.yto(k)], self.ia.at[k], self.sa.at[k], self.ra.at[k], "dp",
                      g.z * g.ny + g.yto(k))

    def copy_z(self, k):
        g = self.grid
        return remote(self.ob.at[k], self.ib.at[k], self.sb.at[k], self.rb.at[k], "dp", g.zto(k) * g.ny + g.y)

    def push(self):
        for k in range(self.grid.ny - 1):
            self.copy_y(k).start()

    def pass_on(self):
        g = self.grid
        for k in range(g.ny - 1):
            self.copy_y(k).wait_recv()
        for k in range(g.nz):
            z = g.zto(k)
            whole = self.grad[g.y, z].astype(F32)
            for j in range(g.ny - 1):
                whole = whole + self.ia[j, z].astype(F32)
            if k < g.nz - 1:
                self.ob[k] = whole.astype(BF16)
                self.copy_z(k).start()
            else:
                self.own[...] = whole

    def collect(self):
        whole = self.own[...]
        for k in range(self.grid.nz - 1):
            self.copy_z(k).wait_recv()
            whole = whole + self.ib[k].astype(F32)
        self.own[...] = whole

    def drain(self):
        g = self.grid
        for k in range(g.ny - 1):
            self.copy_y(k).wait_send()
        for k in range(g.nz - 1):
            self.copy_z(k).wait_send()


def spread_scratch(ny, nz):
    y, z = max(ny - 1, 1), max(nz - 1, 1)
    return [DMA((z,)), DMA((z,)), DMA((nz, y)), DMA((nz, y))]


class Spread:
    count = 4

    def __init__(self, grid, own, result, scratch):
        self.grid, self.own, self.result = grid, own, result
        self.sz, self.rz, self.sy, self.ry = scratch

    def back_z(self, k):
        g = self.grid
        r = self.result.at[g.y, g.z]
        return remote(r, r, self.sz.at[k], self.rz.at[k], "dp", g.zto(k) * g.ny + g.y)

    def back_y(self, k, j):
        g = self.grid
        r = self.result.at[g.y, g.z if k == g.nz - 1 else g.zfrom(k)]
        return remote(r, r, self.sy.at[k, j], self.ry.at[k, j], "dp", g.z * g.ny + g.yto(j))

    def start(self):
        g = self.grid
        whole = self.own[...]
        self.result[g.y, g.z] = whole.astype(BF16)
        for k in range(g.nz - 1):
            self.back_z(k).start()
        for k in range(g.ny - 1):
            self.back_y(g.nz - 1, k).start()
        return square(whole)

    def forward(self):
        g = self.grid
        for k in range(g.nz - 1):
            self.back_z(k).wait_recv()
            for j in range(g.ny - 1):
                self.back_y(k, j).start()

    def close(self):
        g = self.grid
        for k in range(g.nz):
            for j in range(g.ny - 1):
                self.back_y(k, j).wait_recv()
        for k in range(g.nz - 1):
            self.back_z(k).wait_send()
        for k in range(g.nz):
            for j in range(g.ny - 1):
                self.back_y(k, j).wait_send()


def take(rest, cls, count):
    size = cls.count
    return [rest[size * i:size * (i + 1)] for i in range(count)], rest[size * count:]


class Share:
    def __init__(self, axis, slots, send, recv):
        self.axis, self.slots, self.send, self.recv = axis, slots, send, recv
        self.size = slots.shape[0]
        self.me = lax.axis_index(axis)

    def copy(self, k):
        r = self.slots.at[self.me]
        return remote(r, r, self.send.at[k], self.recv.at[k], self.axis, lax.rem(self.me + 1 + k, self.size))

    def start(self, value):
        self.slots[self.me] = value
        for k in range(self.size - 1):
            self.copy(k).start()

    def total(self):
        for k in range(self.size - 1):
            self.copy(k).wait_recv()
        out = self.slots[0]
        for i in range(1, self.size):
            out = out + self.slots[i]
        return out

    def drain(self):
        for k in range(self.size - 1):
            self.copy(k).wait_send()


def share_scratch(size, rows, width):
    return [pltpu.VMEM((size, rows, width), F32), DMA((max(size - 1, 1),)), DMA((max(size - 1, 1),))]


def square(v):
    return jnp.sum(jnp.sum(v * v, axis=1, keepdims=True), axis=0, keepdims=True)


def leave_kernel(n, ny, nz, late, x_ref, dx_ref, np_ref, dqkv_ref, h_ref, bg_ref, pair_ref, squares_ref,
                 mid_small_ref, *rest):
    owns, (w_hbm, gi_ref), rest = rest[:late], rest[late:late + 2], rest[late + 2:]
    results, rest = rest[:late], rest[late:]
    (sq_ref, small_ref, bias_ref, pairs_ref, norm_ref, w32, w, qg, qown, wsem), rest = rest[:10], rest[10:]
    seat, grid = Seat(n), Grid(ny, nz)
    rows, width = x_ref.shape
    inner = w.shape[1]
    load = pltpu.make_async_copy(w_hbm, w32, wsem)
    load.start()
    scat, rest = Scatter(seat, rest[:8]), rest[8:]
    parts, rest = take(rest, Sum, 3)
    sums = [Sum(grid, qg.at[s], qown.at[s], p) for s, p in enumerate(parts)]
    parts, rest = take(rest, Spread, 3 + late)
    spreads = [Spread(grid, s.own, sq_ref.at[i], p) for i, (s, p) in enumerate(zip(sums, parts))]
    olds = [Spread(grid, o, r, p) for o, r, p in zip(owns, results, parts[3:])]
    shares = [Share(a, *rest[3 * i:3 * i + 3]) for i, a in enumerate(("mp", "dp", "dp", "dp", "mp", "dp"))]
    small_mp, small_dp, bias_dp, pair_dp, sq_mp, sq_dp = shares
    greet({"mp": n, "dp": ny * nz})
    at = lambda b: pl.ds(pl.multiple_of(b * rows, rows), rows)

    squares = squares_ref[0:1]
    for s in olds:
        squares = squares + s.start()
    load.wait()
    w[...] = w32[...].astype(BF16)

    def first_block(b):
        return sum(mm(dqkv_ref[s, :, at(b)], w[s], TN) for s in range(3))

    scat.push(first_block)
    for s in range(3):
        acc = jnp.zeros((inner, width), F32)
        for b in range(n):
            acc = acc + mm(dqkv_ref[s, :, at(b)], h_ref[b])
        qg[s] = acc.reshape(qg.shape[1:]).astype(BF16)
        sums[s].push()
        if s == 0:
            whole = scat.pass_on(first_block)
            bias_dp.start(jnp.broadcast_to(bg_ref[...], bias_dp.slots.shape[1:]))
            pair_dp.start(pair_ref[...])
    for s in olds:
        s.forward()
    dh1 = scat.finish(whole)
    dv, gain, shift = norm_back(x_ref[...].astype(F32), np_ref[0:1], dh1)
    gi_ref[...] = dx_ref[...] + dv
    small_mp.start(jnp.concatenate([gain, shift, mid_small_ref[0:6]], 0))
    sums[0].pass_on()
    small_dp.start(small_mp.total())
    sums[1].pass_on()
    sums[0].collect()
    squares = squares + spreads[0].start()
    sums[2].pass_on()
    for s in (1, 2):
        sums[s].collect()
        squares = squares + spreads[s].start()
    spreads[0].forward()
    bias = bias_dp.total()
    bias_ref[...] = bias
    pairs = pair_dp.total()
    pairs_ref[...] = pairs
    row = lax.broadcasted_iota(jnp.int32, (8, LANE), 0)
    local = square(bias[0:1]) + square(pairs)
    sq_mp.start(jnp.where(row == 0, squares, jnp.where(row == 1, local, 0.0)))
    small = small_dp.total()
    small_ref[...] = small
    spreads[1].forward()
    sq_dp.start(sq_mp.total())
    spreads[2].forward()
    norm_ref[...] = sq_dp.total()[0:1] + sq_dp.slots[0, 1:2] + square(small)
    for s in olds + spreads:
        s.close()
    for s in [scat] + sums + shares:
        s.drain()


def leave(n, ny, nz, x, dx, params, dqkv, h, bias_grad, pair_grad, squares, small, owns, qkv_weight):
    rows, width = x.shape
    inner = qkv_weight.shape[1]
    ndp = ny * nz
    hidden = bias_grad.shape[1]
    chunks = (3, ny, nz, inner // ndp, width)
    f = lambda *s: jax.ShapeDtypeStruct(s, F32)
    late = len(owns)
    return pl.pallas_call(
        functools.partial(leave_kernel, n, ny, nz, late),
        out_shape=(f(rows, width), *[jax.ShapeDtypeStruct((ny, nz, *o.shape), BF16) for o in owns],
                   jax.ShapeDtypeStruct(chunks, BF16), f(8, width), f(8, hidden), f(8, LANE), f(1, LANE)),
        in_specs=[VM] * (9 + late) + [HBM], out_specs=[VM] * (6 + late),
        scratch_shapes=[pltpu.VMEM(qkv_weight.shape, F32), pltpu.VMEM(qkv_weight.shape, BF16),
                        pltpu.VMEM(chunks, BF16), pltpu.VMEM((3, inner // ndp, width), F32), DMA,
                        *scatter_scratch(n, rows, width),
                        *[s for _ in range(3) for s in sum_scratch(ny, nz, inner // ndp, width)],
                        *[s for _ in range(3 + late) for s in spread_scratch(ny, nz)],
                        *share_scratch(n, 8, width), *share_scratch(ndp, 8, width), *share_scratch(ndp, 8, hidden),
                        *share_scratch(ndp, 8, LANE), *share_scratch(n, 8, LANE), *share_scratch(ndp, 8, LANE)],
        compiler_params=pltpu.CompilerParams(collective_id=2, has_side_effects=True, vmem_limit_bytes=60 << 20),
        name="leave",
    )(x, dx, params, dqkv, h, bias_grad, pair_grad, squares, small, *owns, qkv_weight)


def leave_plain(n, x, dx, params, dqkv, h, grads, bias_grad, pair_grad, small, qkv_weight):
    part = sum(mm(dqkv[s], qkv_weight[s].astype(BF16), TN) for s in range(3))
    dh1 = lax.psum_scatter(part, "mp", scatter_dimension=0, tiled=True)
    dv, gain, shift = norm_back(x.astype(F32), params[0:1], dh1)
    hh = h.reshape(-1, h.shape[-1])
    qg = jnp.concatenate([mm(dqkv[s], hh) for s in range(3)], 0)
    og, ig, pg, qg, bias, pair = lax.psum((*[g.astype(F32) for g in grads], qg, bias_grad, pair_grad), "dp")
    small = lax.psum(jnp.concatenate([gain, shift, small[0:6]], 0), ("dp", "mp"))
    local = sum(square(v) for v in (og, ig, pg, qg, bias, pair))
    total = lax.psum(local, "mp") + square(small)
    return dx + dv, og, ig, pg, qg, small, bias, pair, total


PASS_AT = (4, 10, 24, 38, 45)
COLLECT_AT = (15, 30, 44, 58, 72)
FORWARD_AT = (40, 55)
EARLY = 2


def back_kernel(heads, ny, nz, parts, coords_ref, qkv_ref, do_ref, p_ref, og_ref, ig_ref, pg_ref,
                dqkv_ref, pair_ref, squares_ref, *rest):
    owns, rest = rest[:2 * parts + 1 - EARLY], rest[2 * parts + 1 - EARLY:]
    results, (dist, ds, early), rest = rest[:EARLY], rest[EARLY:EARLY + 3], rest[EARLY + 3:]
    hd, span = do_ref.shape[1:]
    grid = Grid(ny, nz)
    pieces = [g.at[i] for g in (og_ref, ig_ref) for i in range(parts)] + [pg_ref]
    places = [early.at[i] for i in range(EARLY)] + list(owns)
    scratch, rest = take(rest, Sum, len(pieces))
    sums = [Sum(grid, *a) for a in zip(pieces, places, scratch)]
    scratch, rest = take(rest, Spread, EARLY)
    spreads = [Spread(grid, *a) for a in zip(places, results, scratch)]
    greet({"dp": ny * nz})
    for s in sums:
        s.push()
    squares_ref[...] = jnp.zeros_like(squares_ref)

    def collect(i):
        sums[i].collect()
        if i < EARLY:
            squares_ref[...] += spreads[i].start()

    jobs = {}
    for i, s in enumerate(sums):
        jobs.setdefault(PASS_AT[i], []).append(s.pass_on)
        jobs.setdefault(COLLECT_AT[i], []).append(functools.partial(collect, i))
    for i, s in enumerate(spreads):
        jobs.setdefault(FORWARD_AT[i], []).append(s.forward)
    last = heads + span // SUB

    def beside(step, first, end):
        for when in sorted(jobs):
            if first <= when < end:
                @pl.when(step == when)
                def _():
                    for job in jobs[when]:
                        job()

    pair_ref[...] = back_pairs(heads, coords_ref, qkv_ref, do_ref, p_ref, dqkv_ref, dist, ds, beside)
    for when in sorted(jobs):
        if when >= last:
            for job in jobs[when]:
                job()
    for s in spreads:
        s.close()
    for s in sums:
        s.drain()


def attention_back_sums(qkv, do, probs, coords, ny, nz, og, ig, pg):
    _, heads, hd, span = qkv.shape
    width = og.shape[1]
    ndp, parts = ny * nz, 2
    cut = lambda g, p: g.reshape(p, ny, nz, g.shape[0] // (p * ndp), width)
    og, ig, pg = cut(og, parts), cut(ig, parts), cut(pg, 1)[0]
    shapes = [og.shape[1:]] * parts + [ig.shape[1:]] * parts + [pg.shape]
    f = lambda *s: jax.ShapeDtypeStruct(s, F32)
    return pl.pallas_call(
        functools.partial(back_kernel, heads, ny, nz, parts),
        out_shape=(jax.ShapeDtypeStruct(qkv.shape, BF16), f(SUB, KERN), f(SUB, LANE),
                   *[f(*s[2:]) for s in shapes[EARLY:]], *[jax.ShapeDtypeStruct(s, BF16) for s in shapes[:EARLY]]),
        in_specs=[VM] * 7, out_specs=[VM] * (3 + len(shapes)),
        scratch_shapes=[pltpu.VMEM((span, span), F32), pltpu.VMEM((span // LANE, SUB * span, LANE), F32),
                        pltpu.VMEM((EARLY, *shapes[0][2:]), F32),
                        *[s for shape in shapes for s in sum_scratch(ny, nz, shape[2], width)],
                        *[s for _ in range(EARLY) for s in spread_scratch(ny, nz)]],
        compiler_params=pltpu.CompilerParams(collective_id=3, has_side_effects=True, vmem_limit_bytes=60 << 20),
        name="attend_back_sums",
    )(coords, qkv, do, probs, og, ig, pg)


def adam_step(weight, grad, first, second, clip, fix_one, fix_two, rate, decay):
    scaled = grad * clip
    first_new = beta_one * first + (1.0 - beta_one) * scaled
    second_new = beta_two * second + (1.0 - beta_two) * scaled * scaled
    ratio = first_new / fix_one / (jnp.sqrt(second_new / fix_two) + adam_eps)
    return (weight - rate * (ratio + decay * weight), first_new, second_new)


def per_device(n, ndp, block_in, coords, lengths, cotangent, step_count, *state):
    weights, firsts, seconds = state[:7], state[7:14], state[14:]
    qkv_weight, proj_weight, pair_weight, in_weight, in_bias, out_weight, params = weights
    heads = pair_weight.shape[0]
    pair_low = pair_weight.astype(BF16)
    h, dy_all, qkv = enter(n, heads, block_in, cotangent, params, qkv_weight)
    o, probs = attention(qkv, coords, lengths, pair_low)
    block_out, dx, do, og, ig, pg, bg, small = middle(
        n, block_in, cotangent, dy_all, o, params, in_bias.reshape(1, -1), proj_weight, in_weight, out_weight)
    ny = n // 2 if ndp % (n // 2) == 0 else 1
    nz = ndp // ny
    inner = proj_weight.shape[0]
    if lengths.shape[0] == 1 and inner % (8 * ndp) == 0 and og.shape[0] % (32 * ndp) == 0:
        dqkv, pair_grad, squares, *parts = attention_back_sums(qkv, do, probs, coords, ny, nz, og, ig, pg)
        owns, done = parts[:-EARLY], parts[-EARLY:]
        grad_input, *sums, qg, small, bias, pair, total = leave(
            n, ny, nz, block_in, dx, params, dqkv.reshape(3, inner, -1), h, bg, pair_grad, squares, small, owns, qkv_weight)
        *pieces, pg = *done, *sums
        og, ig = pieces[:len(pieces) // 2], pieces[len(pieces) // 2:]
        og, ig = [jnp.concatenate([v.reshape(-1, v.shape[-1]) for v in g], 0) for g in (og, ig)]
    else:
        dqkv, pair_grad = attention_back(qkv, do, probs, coords)
        grad_input, og, ig, pg, qg, small, bias, pair, total = leave_plain(
            n, block_in, dx, params, dqkv.reshape(3, inner, -1), h, (og, ig, pg), bg, pair_grad, small, qkv_weight)
    grad_norm = jnp.sqrt(total[0, 0])
    clip = clip_level / jnp.maximum(grad_norm, clip_level)
    count = step_count[0].astype(F32)
    fix_one = 1.0 - jnp.power(beta_one, count)
    fix_two = 1.0 - jnp.power(beta_two, count)
    grads = (qg.reshape(qkv_weight.shape), pg.reshape(proj_weight.shape), pair[:heads], ig.reshape(in_weight.shape),
             bias[0], og.reshape(out_weight.shape), small[:5])
    rates = (0.9, 2.5, 7.5, 0.9, 7.5, 0.45, 3.0)
    decays = (0.01, 0.01, 0.01, 0.01, 0.0, 0.01, 0.0)
    outs = [block_out, grad_input, grad_norm.reshape(1)]
    for w, g, m, u, rate, decay in zip(weights, grads, firsts, seconds, rates, decays):
        outs.extend(adam_step(w, g.astype(F32), m, u, clip, fix_one, fix_two, rate, decay))
    return tuple(outs)


def solution(mesh):
    rows, mp = P(("dp", "mp"), None), P("mp", None)
    stacked = P(None, "mp", None)
    params = (stacked, mp, mp, mp, P("mp"), mp, P())
    in_specs = (rows, P(None, "dp"), P("dp", None), rows, P(), *params, *params, *params)
    out_specs = (rows, rows, P(), *[s for s in params for _ in range(3)])
    return jax.shard_map(
        functools.partial(per_device, mesh.shape["mp"], mesh.shape["dp"]),
        mesh=mesh, in_specs=in_specs, out_specs=out_specs, check_vma=False)
```

time: 315 us -> 240 us (0.76)
  Pallas kernels: 282 us -> 213 us
    pallas_call x2, Pallas kernels: 176 us -> 121 us  [the longest x1 62.3 us: attention_back_sums(): pl.pallas_call(functools.partial(back_kernel, heads, ny, nz, parts), out_...]
    pallas_call x1, Pallas kernels: 46.5 us -> 32.8 us  [attention(): pl.pallas_call(functools.partial(fwd_kernel, heads, mols), out_shape=(jax...]
    sub x7 -> x6, other arithmetic: 15 us -> 16.4 us  [adam_step(): return (weight - rate * (ratio + decay * weight), first_new, second_new)]
where the time goes in v3:
time: 240 us; the launch traced here: 239 us
  Pallas kernels  213 us (89%)
  other arithmetic  18.6 us (8%)
  local copies, waits for them, and re-layouts  4.05 us (2%)
  between operations  3.56 us (1%)
    pallas_call x1, Pallas kernels, attention_back_sums(): pl.pallas_call(functools.partial(back_kernel, heads, ny, nz, parts), out_...  62.3 us
    pallas_call x1, Pallas kernels, leave(): pl.pallas_call(functools.partial(leave_kernel, n, ny, nz, late), out_shap...  58.6 us
    pallas_call x1, Pallas kernels, middle(): pl.pallas_call(functools.partial(middle_kernel, n), out_shape=(f(rows, wi...  41 us
    pallas_call x1, Pallas kernels, attention(): pl.pallas_call(functools.partial(fwd_kernel, heads, mols), out_shape=(jax...  32.8 us
    pallas_call x1, Pallas kernels, enter(): pl.pallas_call(functools.partial(enter_kernel, n), out_shape=(jax.ShapeDt...  18.6 us
    sub x6, other arithmetic, adam_step(): return (weight - rate * (ratio + decay * weight), first_new, second_new)  16.4 us

profile of v3, /device:TPU:0, one launch (start us, length us, event | category | flops | bytes accessed | tf_op | source)
XLA Modules:
  0.0 239.4 jit_solution(14065104643429224504)
XLA Ops:
  0.7 0.0 copy-start.17
  0.7 18.6 %enter.1 = (bf16[4,128,768]{2,1,0:T(8,128)(2,1)}, bf16[4,128,768]{2,1,0:T(8,128)(2,1)}, bf16[3,8,24,512]{3,2,1,0:T(8,128)(2,1)}) custom-call(bf16[128,768]{1,0:T(8,128)(2,1)} %x_ref.5, bf16[128,768]{1,0:T(8,128)(2,1)} %dy_ref.3, f32[5,768]{1,0:T(8,128)} %np_ref.5, f32[3,192,768]{2,1,0:T(8,128)} %rest_3_.1), custom_call_target="tpu_custom_call" | custom-call | tf_op jit(solution)/shard_map/enter/pallas_call | solution.py:402
  19.3 1.3 convert_element_type.21.w_ref
  20.5 32.8 %attend.1 = (bf16[8,24,512]{2,1,0:T(8,128)(2,1)}, bf16[4096,512]{1,0:T(8,128)(2,1)}) custom-call(s32[1,16]{1,0:T(1,128)} %len_ref.1, f32[3,512]{1,0:T(4,128)} %coords_ref.3, bf16[3,8,24,512]{3,2,1,0:T(8,128)(2,1)} %get-tuple-element.55.qkv_ref, bf16[8,128]{1,0:T(8,128)(2,1)} %convert_element_type.21.w_ref), custom_call_target="tpu_custom_call" | custom-call | tf_op jit(solution)/shard_map/attend/pallas_call | solution.py:138
  53.3 0.0 copy-done.17
  53.3 0.6 reshape.104.bias_ref
  53.9 41.0 %middle.1 = (f32[128,768]{1,0:T(8,128)}, f32[128,768]{1,0:T(8,128)}, bf16[8,24,512]{2,1,0:T(8,128)(2,1)}, bf16[768,768]{1,0:T(8,128)(2,1)}, bf16[768,768]{1,0:T(...) custom-call(bf16[128,768]{1,0:T(8,128)(2,1)} %x_ref.5, bf16[128,768]{1,0:T(8,128)(2,1)} %dy_ref.3, ...), custom_call_target="tpu_custom_call" | custom-call | tf_op jit(solution)/shard_map/middle/pallas_call | solution.py:513
  94.9 62.3 %attend_back_sums.1 = (bf16[3,8,24,512]{3,2,1,0:T(8,128)(2,1)}, f32[8,128]{1,0:T(8,128)}, f32[8,128]{1,0:T(8,128)}, f32[48,768]{1,0:T(8,128)}, f32[48,768]{1,0:T...) custom-call(f32[3,512]{1,0:T(4,128)} %coords_ref.3, ...), custom_call_target="tpu_custom_call" | custom-call | tf_op jit(solution)/shard_map/attend_back_sums/pallas_call | solution.py:875
  157.2 0.0 copy-start.1
  157.2 0.0 copy-start.8
  157.2 0.0 copy-start.9
  157.2 58.6 %leave.1 = (f32[128,768]{1,0:T(8,128)}, bf16[2,4,48,768]{3,2,1,0:T(8,128)(2,1)}, bf16[2,4,48,768]{3,2,1,0:T(8,128)(2,1)}, bf16[2,4,24,768]{3,2,1,0:T(8,128)(2,1)...) custom-call(bf16[128,768]{1,0:T(8,128)(2,1)} %x_ref.5, ...), custom_call_target="tpu_custom_call" | custom-call | tf_op jit(solution)/shard_map/leave/pallas_call | solution.py:782
  217.2 0.0 copy-done.1
  217.2 0.0 copy-done.8
  217.3 0.0 copy-done.9
  217.3 0.0 copy-start.10
  217.3 0.0 copy-start.14
  217.3 0.0 copy-start.15
  217.3 0.0 copy-start.16
  217.3 0.0 copy-start.19
  217.3 0.0 copy-start.20
  217.3 0.0 copy-start.18
  217.3 0.0 copy-start.21
  217.4 0.0 copy-start.22
  217.4 0.0 copy-start.23
  217.4 0.0 copy-start.13
  217.4 0.0 copy-start.2
  217.4 0.0 copy-start.6
  217.4 0.0 copy-start.7
  217.4 9.8 %multiply_subtract_fusion = (f32[768,768]{1,0:T(8,128)}, f32[768,768]{1,0:T(8,128)}, f32[768,768]{1,0:T(8,128)}, f32[768,768]{1,0:T(8,128)}, f32[768,768]{1,0:T(8,128)}, /*index=5*/f32[768,768]{1,0:T(8,128)}) fusion(f32[768,768]{1,0:T(8,128)} %ow_hbm.1, f32[]{:T(128)} %bitcast.9, f32[]{:T(128)} %bitcast.8, f32[]{:T(128)} %bitcast.6, ...), kind=kLoop, calls=%fused_computation.5 | loop fusion | flops 23592960 | bytes 30670860 | tf_op jit(solution)/shard_map/sub | solution.py:894
  227.2 0.0 copy-done.10
  227.2 0.0 copy-done.14
  227.2 0.0 copy-done.15
  227.2 0.0 copy-done.16
  227.2 0.6 multiply_subtract_fusion.4
  227.9 0.8 multiply_reduce_fusion
  228.6 0.0 copy-done.19
  228.6 0.0 copy-done.20
  228.7 0.6 multiply_subtract_fusion.5
  229.3 0.0 copy-done.18
  229.3 0.0 copy-done.21
  229.3 0.0 copy-done.22
  229.3 0.0 copy-done.23
  229.3 0.6 multiply_subtract_fusion.6
  229.9 0.0 copy-done.13
  229.9 0.0 copy-start.5
  230.0 0.0 copy-done.2
  230.0 0.0 copy-done.6
  230.0 0.0 copy-done.7
  230.0 0.0 copy-start.3
  230.0 0.0 copy-start.4
  230.0 1.5 multiply_subtract_fusion.3
  231.5 0.0 copy-start
  231.5 0.0 copy-done.5
  231.5 0.2 convert_multiply_fusion.2
  231.7 0.7 copy-done.3
  232.3 0.5 copy-done.4
  232.9 0.7 copy-done
  233.5 0.0 copy-start.11
  233.5 3.2 %multiply_subtract_fusion.2 = (f32[3,192,768]{2,1,0:T(8,128)}, f32[3,192,768]{2,1,0:T(8,128)}, f32[3,192,768]{2,1,0:T(8,128)}) fusion(f32[3,192,768]{2,1,0:T(8,128)S(1)} %copy-done, f32[]{:T(128)} %bitcast.9, f32[]{:T(128)} %bitcast.8, f32[3,2,4,24,768]{4,3,2,1,0:T(8,128)S(1)} %convert_multiply_fusion.2, f32[3,192,768]{2,1,0:T(8,128)S(1)} %copy-done.3, ...), kind=kLoop, calls=%fused_computation.14 | loop fusion | flops 6635520 | bytes 12386312 | tf_op jit(solution)/shard_map/sub | solution.py:894
  236.8 0.0 copy-done.11
  236.8 0.7 copy.53
  237.5 0.0 copy-done.12
  237.5 0.7 copy.54
  (2 shorter events, 0.0 us)
Async XLA Ops:
  0.7 52.6 %copy-start.17 = (f32[768]{0:T(1024)S(1)}, f32[768]{0:T(1024)}, u32[]{:S(2)}) copy-start(f32[768]{0:T(1024)} %param.35) | copy-start | bytes 9220
  157.2 60.1 %copy-start.1 = (f32[768,768]{1,0:T(8,128)S(1)}, f32[768,768]{1,0:T(8,128)}, u32[]{:S(2)}) copy-start(f32[768,768]{1,0:T(8,128)} %iw_hbm.1) | copy-start | bytes 7077892
  157.2 60.1 %copy-start.8 = (bf16[2,4,48,768]{3,2,1,0:T(8,128)(2,1)S(1)}, bf16[2,4,48,768]{3,2,1,0:T(8,128)(2,1)}, u32[]{:S(2)}) copy-start(bf16[2,4,48,768]{3,2,1,0:T(8,128)(2,1)} %get-tuple-element.81) | copy-start | bytes 1769476
  157.2 60.1 %copy-start.9 = (bf16[2,4,48,768]{3,2,1,0:T(8,128)(2,1)S(1)}, bf16[2,4,48,768]{3,2,1,0:T(8,128)(2,1)}, u32[]{:S(2)}) copy-start(bf16[2,4,48,768]{3,2,1,0:T(8,128)(2,1)} %get-tuple-element.82) | copy-start | bytes 1769476
  217.3 9.9 %copy-start.10 = (f32[5,768]{1,0:T(8,128)S(1)}, f32[5,768]{1,0:T(8,128)}, u32[]{:S(2)}) copy-start(f32[5,768]{1,0:T(8,128)} %np_ref.5) | copy-start | bytes 46084
  217.3 9.9 %copy-start.14 = (f32[5,768]{1,0:T(8,128)S(1)}, f32[5,768]{1,0:T(8,128)}, u32[]{:S(2)}) copy-start(f32[5,768]{1,0:T(8,128)} %param.51) | copy-start | bytes 46084
  217.3 9.9 %copy-start.15 = (f32[5,768]{1,0:T(8,128)S(1)}, f32[5,768]{1,0:T(8,128)}, u32[]{:S(2)}) copy-start(f32[5,768]{1,0:T(8,128)} %param.44) | copy-start | bytes 46084
  217.3 9.9 %copy-start.16 = (f32[8,768]{1,0:T(8,128)S(1)}, f32[8,768]{1,0:T(8,128)}, u32[]{:S(2)}) copy-start(f32[8,768]{1,0:T(8,128)} %get-tuple-element.83) | copy-start | bytes 73732
  217.3 11.3 %copy-start.19 = (f32[768]{0:T(1024)S(1)}, f32[768]{0:T(1024)}, u32[]{:S(2)}) copy-start(f32[768]{0:T(1024)} %param.49) | copy-start | bytes 9220
  217.3 11.3 %copy-start.20 = (f32[768]{0:T(1024)S(1)}, f32[768]{0:T(1024)}, u32[]{:S(2)}) copy-start(f32[768]{0:T(1024)} %param.42) | copy-start | bytes 9220
  217.3 11.9 %copy-start.18 = (f32[8,128]{1,0:T(8,128)S(1)}, f32[8,128]{1,0:T(8,128)}, u32[]{:S(2)}) copy-start(f32[8,128]{1,0:T(8,128)} %param.33) | copy-start | bytes 12292
  217.3 11.9 %copy-start.21 = (f32[8,128]{1,0:T(8,128)S(1)}, f32[8,128]{1,0:T(8,128)}, u32[]{:S(2)}) copy-start(f32[8,128]{1,0:T(8,128)} %param.47) | copy-start | bytes 12292
  217.4 11.9 %copy-start.22 = (f32[8,128]{1,0:T(8,128)S(1)}, f32[8,128]{1,0:T(8,128)}, u32[]{:S(2)}) copy-start(f32[8,128]{1,0:T(8,128)} %param.40) | copy-start | bytes 12292
  217.4 11.9 %copy-start.23 = (f32[8,128]{1,0:T(8,128)S(1)}, f32[8,128]{1,0:T(8,128)}, u32[]{:S(2)}) copy-start(f32[8,128]{1,0:T(8,128)} %get-tuple-element.77) | copy-start | bytes 12292
  217.4 12.5 %copy-start.13 = (bf16[2,4,24,768]{3,2,1,0:T(8,128)(2,1)S(1)}, bf16[2,4,24,768]{3,2,1,0:T(8,128)(2,1)}, u32[]{:S(2)}) copy-start(bf16[2,4,24,768]{3,2,1,0:T(8,128)(2,1)} %get-tuple-element.76) | copy-start | bytes 884740
  217.4 12.6 %copy-start.2 = (f32[192,768]{1,0:T(8,128)S(1)}, f32[192,768]{1,0:T(8,128)}, u32[]{:S(2)}) copy-start(f32[192,768]{1,0:T(8,128)} %pw_hbm.1) | copy-start | bytes 1769476
  217.4 12.6 %copy-start.6 = (f32[192,768]{1,0:T(8,128)S(1)}, f32[192,768]{1,0:T(8,128)}, u32[]{:S(2)}) copy-start(f32[192,768]{1,0:T(8,128)} %param.46) | copy-start | bytes 1769476
  217.4 12.6 %copy-start.7 = (f32[192,768]{1,0:T(8,128)S(1)}, f32[192,768]{1,0:T(8,128)}, u32[]{:S(2)}) copy-start(f32[192,768]{1,0:T(8,128)} %param.39) | copy-start | bytes 1769476
  229.9 1.6 copy-start.5
  230.0 2.3 copy-start.3
  230.0 2.9 %copy-start.4 = (f32[3,192,768]{2,1,0:T(8,128)S(1)}, f32[3,192,768]{2,1,0:T(8,128)}, u32[]{:S(2)}) copy-start(f32[3,192,768]{2,1,0:T(8,128)} %param.38) | copy-start | bytes 5308420
  231.5 2.0 copy-start
  233.5 3.3 %copy-start.11 = (f32[128,768]{1,0:T(8,128)S(1)}, f32[128,768]{1,0:T(8,128)}, u32[]{:S(2)}) copy-start(f32[128,768]{1,0:T(8,128)} %get-tuple-element.132) | copy-start | bytes 1179652
  233.5 4.0 %copy-start.12 = (f32[128,768]{1,0:T(8,128)S(1)}, f32[128,768]{1,0:T(8,128)}, u32[]{:S(2)}) copy-start(f32[128,768]{1,0:T(8,128)} %get-tuple-element.133) | copy-start | bytes 1179652

commit v4 on v3

--- a/solution.py
+++ b/solution.py
@@ -26,6 +26,7 @@
 LANE = 128
 SUB = 8
 TALL = 32
+ATTEND_MIB = 20
 KS = math.sqrt(0.5 * math.log2(math.e))
 UNIT = KS / (12.8 / KERN)
 
@@ -148,7 +149,9 @@
                        pl.BlockSpec((heads * span, span), lambda b, *_: (b, 0))],
             scratch_shapes=[pltpu.VMEM((span, span), F32), pltpu.VMEM((span, LANE), F32),
                             pltpu.VMEM((SUB, span), F32), pltpu.VMEM((span // LANE, SUB * span, LANE), F32)]),
-        compiler_params=pltpu.CompilerParams(vmem_limit_bytes=60 << 20),
+        cost_estimate=pl.CostEstimate(flops=20 * heads * hd * rows * span, bytes_accessed=8 * rows * span,
+                                      transcendentals=KERN * rows * span),
+        compiler_params=pltpu.CompilerParams(vmem_limit_bytes=ATTEND_MIB << 20),
         name="attend",
     )(lengths, coords, qkv, w)
 
@@ -237,9 +240,11 @@
         device_id={axis: target}, device_id_type=MESH)
 
 
-def greet(sizes):
+def greet(sizes, others=()):
     barrier = pltpu.get_barrier_semaphore()
-    total = 0
+    total = len(others)
+    for place in others:
+        pl.semaphore_signal(barrier, inc=1, device_id={"dp": place}, device_id_type=MESH)
     for axis, size in sizes.items():
         me = lax.axis_index(axis)
         for k in range(1, size):
@@ -261,6 +266,27 @@
 
     def source(self, k):
         return lax.rem(self.x + self.nx - 1 - k, self.nx)
+
+
+class Grid:
+    def __init__(self, ny, nz):
+        self.ny, self.nz = ny, nz
+        self.me = lax.axis_index("dp")
+        self.z, self.y = self.me // ny, lax.rem(self.me, ny)
+        self.nh, self.a, self.p = nz // 2, self.z // 2, lax.rem(self.z, 2)
+        self.near = self.z + 1 - 2 * self.p
+
+    def at(self, z, y):
+        return z * self.ny + y
+
+    def other(self, k):
+        return lax.rem(self.a + 1 + k, self.nh)
+
+    def far(self, k):
+        return 2 * self.other(k) + self.p
+
+    def yto(self, k):
+        return lax.rem(self.y + 1 + k, self.ny)
 
 
 def scatter_scratch(n, rows, width):
@@ -364,20 +390,17 @@
     return dv, jnp.sum(e * vhat, axis=0, keepdims=True), jnp.sum(e, axis=0, keepdims=True)
 
 
-def enter_kernel(n, x_ref, dy_ref, np_ref, w_hbm, h_ref, dyall_ref, qkv_ref, w32, wsem, *sems):
+def enter_kernel(n, x_ref, np_ref, w_hbm, h_ref, qkv_ref, w32, wsem, *sems):
     seat = Seat(n)
     load = pltpu.make_async_copy(w_hbm, w32, wsem)
     load.start()
     greet({"mp": n})
     vhat, _ = centre(x_ref[...].astype(F32))
     h_ref[seat.me] = (vhat * np_ref[0:1] + np_ref[1:2]).astype(BF16)
-    dyall_ref[seat.me] = dy_ref[...]
-    gh = Gather(seat, h_ref, sems[:4])
-    gd = Gather(seat, dyall_ref, sems[4:])
+    gh = Gather(seat, h_ref, sems)
     gh.start()
     load.wait()
     gh.forward()
-    gd.start()
     gh.finish()
     rows = h_ref.shape[1]
     for s in range(3):
@@ -390,30 +413,30 @@
             return carry
 
         lax.fori_loop(0, n, block, 0)
-    gd.forward()
-    gd.finish()
     gh.drain()
-    gd.drain()
-
-
-def enter(n, heads, x, dy, params, qkv_weight):
+
+
+def enter(n, heads, x, params, qkv_weight):
     rows, width = x.shape
     _, inner, _ = qkv_weight.shape
     return pl.pallas_call(
         functools.partial(enter_kernel, n),
-        out_shape=(jax.ShapeDtypeStruct((n, rows, width), BF16), jax.ShapeDtypeStruct((n, rows, width), BF16),
+        out_shape=(jax.ShapeDtypeStruct((n, rows, width), BF16),
                    jax.ShapeDtypeStruct((3, heads, inner // heads, n * rows), BF16)),
-        in_specs=[VM, VM, VM, HBM], out_specs=[VM, VM, VM],
-        scratch_shapes=[pltpu.VMEM(qkv_weight.shape, F32), DMA, *gather_scratch(n), *gather_scratch(n)],
-        compiler_params=pltpu.CompilerParams(collective_id=0, has_side_effects=True),
+        in_specs=[VM, VM, HBM], out_specs=[VM, VM],
+        scratch_shapes=[pltpu.VMEM(qkv_weight.shape, F32), DMA, *gather_scratch(n)],
+        compiler_params=pltpu.CompilerParams(collective_id=0, has_side_effects=True, vmem_limit_bytes=60 << 20),
         name="enter",
-    )(x, dy, params, qkv_weight)
-
-
-def middle_kernel(n, x_ref, dy_ref, dyall_ref, o_ref, np_ref, bias_ref, pw_hbm, iw_hbm, ow_hbm,
-                  block_ref, mid_ref, do_ref, og_ref, ig_ref, pg_ref, bg_ref, small_ref,
-                  pw32, iw32, ow32, pw, iw, ow, h2, da, act, dpre, dact, wsem, *rest):
-    seat = Seat(n)
+    )(x, params, qkv_weight)
+
+
+def middle_kernel(n, ny, nz, pushes, x_ref, o_ref, np_ref, bias_ref, pw_hbm, iw_hbm, ow_hbm, *rest):
+    dys, rest = rest[:n], rest[n:]
+    (block_ref, mid_ref, do_ref, og_ref, ig_ref, pg_ref, bg_ref, small_ref), rest = rest[:8], rest[8:]
+    lands, rest = rest[:pushes], rest[pushes:]
+    (pw32, iw32, ow32, pw, iw, ow, h2, da, act, dpre, dact, dyall_ref, wsem), rest = rest[:13], rest[13:]
+    seat, grid = Seat(n), Grid(ny, nz)
+    dy_ref = dys[0]
     rows, width = x_ref.shape
     loads = [pltpu.make_async_copy(a, b, wsem.at[i])
              for i, (a, b) in enumerate([(pw_hbm, pw32), (ow_hbm, ow32), (iw_hbm, iw32)])]
@@ -421,7 +444,19 @@
         c.start()
     scat = [Scatter(seat, rest[8 * i:8 * i + 8]) for i in range(3)]
     gath = [Gather(seat, r, rest[24 + 4 * i:28 + 4 * i]) for i, r in enumerate((h2, da))]
-    greet({"mp": n})
+    places = [grid.z * ny + grid.yto(k) for k in range(ny - 1)]
+    greet({"mp": n}, places if pushes else ())
+
+    def ahead(i, k):
+        part = (og_ref, ig_ref)[i // PARTS]
+        tall = part.shape[0] // (PARTS * ny)
+        start = pl.multiple_of(((i % PARTS) * ny + grid.yto(k)) * tall, 16)
+        return remote(part.at[pl.ds(start, tall), :], lands[i].at[k], rest[32].at[i, k], rest[33].at[i, k],
+                      "dp", places[k])
+
+    copies = [[ahead(i, k) for k in range(ny - 1)] for i in range(pushes)]
+    for k in range(n):
+        dyall_ref[lax.rem(seat.me + k, n)] = dys[k][...]
     at = lambda b: pl.ds(pl.multiple_of(b * rows, rows), rows)
 
     loads[0].wait()
@@ -462,6 +497,24 @@
 
     scat[1].push(feed_block)
     whole = scat[1].pass_on(feed_block)
+    hidden = iw.shape[0]
+    step = LANE if hidden % LANE == 0 else hidden
+
+    def grads(left, right, out, first):
+        def columns(i, carry):
+            c0 = pl.multiple_of(i * step, step)
+            acc = jnp.zeros((step, width), F32)
+            for b in range(n):
+                acc += mm(left[b, :, pl.ds(c0, step)], right[b], TN)
+            out[pl.ds(c0, step), :] = acc.astype(BF16)
+            return carry
+
+        lax.fori_loop(0, hidden // step, columns, 0)
+        for piece in copies[first:first + PARTS]:
+            for copy in piece:
+                copy.start()
+
+    grads(act, dyall_ref, og_ref, 0)
     out_block = lambda b: mm(act[b], ow[...])
     scat[2].push(out_block)
     dh2 = scat[1].finish(whole)
@@ -474,22 +527,7 @@
         [gain, shift, jnp.sum(dy, axis=0, keepdims=True), jnp.zeros((5, width), F32)], 0)
     whole = scat[2].pass_on(out_block)
     gath[1].forward()
-
-    hidden = iw.shape[0]
-    step = LANE if hidden % LANE == 0 else hidden
-
-    def grads(i, carry):
-        c0 = pl.multiple_of(i * step, step)
-        acc_o = jnp.zeros((step, width), F32)
-        acc_i = jnp.zeros((step, width), F32)
-        for b in range(n):
-            acc_o += mm(act[b, :, pl.ds(c0, step)], dyall_ref[b], TN)
-            acc_i += mm(dpre[b, :, pl.ds(c0, step)], h2[b], TN)
-        og_ref[pl.ds(c0, step), :] = acc_o.astype(BF16)
-        ig_ref[pl.ds(c0, step), :] = acc_i.astype(BF16)
-        return carry
-
-    lax.fori_loop(0, hidden // step, grads, 0)
+    grads(dpre, h2, ig_ref, PARTS)
     block_ref[...] = mid_ref[...] + scat[2].finish(whole) + np_ref[4:5]
     mid_ref[...] = dx1
     gath[1].finish()
@@ -502,156 +540,170 @@
     pg_ref[...] = lax.fori_loop(0, n, heads_block, jnp.zeros(pg_ref.shape, F32)).astype(BF16)
     for c in scat + gath:
         c.drain()
-
-
-def middle(n, x, dy, dy_all, o, params, bias, proj_weight, in_weight, out_weight):
+    for piece in copies:
+        for copy in piece:
+            copy.wait()
+
+
+PARTS = 2
+MIDDLE_MIB = 24
+
+
+def middle(n, ny, nz, pushes, x, dys, o, params, bias, proj_weight, in_weight, out_weight):
     rows, width = x.shape
     hidden = in_weight.shape[0]
     inner = proj_weight.shape[0]
     heads, hd, _ = o.shape
     f = lambda *s: jax.ShapeDtypeStruct(s, F32)
     return pl.pallas_call(
-        functools.partial(middle_kernel, n),
+        functools.partial(middle_kernel, n, ny, nz, pushes),
         out_shape=(f(rows, width), f(rows, width), jax.ShapeDtypeStruct(o.shape, BF16),
-                   *[jax.ShapeDtypeStruct((t, width), BF16) for t in (hidden, hidden, inner)], f(1, hidden), f(8, width)),
-        in_specs=[VM] * 6 + [HBM] * 3, out_specs=[VM] * 8,
+                   *[jax.ShapeDtypeStruct((t, width), BF16) for t in (hidden, hidden, inner)], f(1, hidden), f(8, width),
+                   *[jax.ShapeDtypeStruct((ny - 1, hidden // (PARTS * ny), width), BF16)] * pushes),
+        in_specs=[VM] * 4 + [HBM] * 3 + [VM] * n, out_specs=[VM] * (8 + pushes),
         scratch_shapes=[pltpu.VMEM((inner, width), F32), pltpu.VMEM((hidden, width), F32),
                         pltpu.VMEM((hidden, width), F32), pltpu.VMEM((inner, width), BF16),
                         pltpu.VMEM((hidden, width), BF16), pltpu.VMEM((hidden, width), BF16),
                         pltpu.VMEM((n, rows, width), BF16), pltpu.VMEM((n, rows, width), BF16),
                         pltpu.VMEM((n, rows, hidden), BF16), pltpu.VMEM((n, rows, hidden), BF16),
-                        pltpu.VMEM((n, rows, hidden), F32), DMA((3,)),
+                        pltpu.VMEM((n, rows, hidden), F32), pltpu.VMEM((n, rows, width), BF16), DMA((3,)),
                         *[s for _ in range(3) for s in scatter_scratch(n, rows, width)],
-                        *gather_scratch(n), *gather_scratch(n)],
-        compiler_params=pltpu.CompilerParams(collective_id=1, has_side_effects=True, vmem_limit_bytes=60 << 20),
+                        *gather_scratch(n), *gather_scratch(n),
+                        *[DMA((max(pushes, 1), max(ny - 1, 1)))] * 2],
+        compiler_params=pltpu.CompilerParams(collective_id=1, has_side_effects=True, vmem_limit_bytes=MIDDLE_MIB << 20),
         name="middle",
-    )(x, dy, dy_all, o.reshape(inner, -1), params, bias, proj_weight, in_weight, out_weight)
-
-
-class Grid:
-    def __init__(self, ny, nz):
-        self.ny, self.nz = ny, nz
-        self.me = lax.axis_index("dp")
-        self.z, self.y = self.me // ny, lax.rem(self.me, ny)
-
-    def yto(self, k):
-        return lax.rem(self.y + 1 + k, self.ny)
-
-    def yfrom(self, k):
-        return lax.rem(self.y + self.ny - 1 - k, self.ny)
-
-    def zto(self, k):
-        return lax.rem(self.z + 1 + k, self.nz)
-
-    def zfrom(self, k):
-        return lax.rem(self.z + self.nz - 1 - k, self.nz)
-
-
-def sum_scratch(ny, nz, chunk, width):
-    y, z = max(ny - 1, 1), max(nz - 1, 1)
-    return [pltpu.VMEM((y, nz, chunk, width), BF16), pltpu.VMEM((z, chunk, width), BF16),
-            pltpu.VMEM((z, chunk, width), BF16), DMA((y,)), DMA((y,)), DMA((z,)), DMA((z,))]
+    )(x, o.reshape(inner, -1), params, bias, proj_weight, in_weight, out_weight, *dys)
+
+
+def sum_scratch(shape):
+    ny, _, nh, chunk, width = shape
+    y, f = max(ny - 1, 1), max(nh - 1, 1)
+    return [pltpu.VMEM((y, 2, nh, chunk, width), BF16), pltpu.VMEM((nh, chunk, width), F32),
+            pltpu.VMEM((nh, chunk, width), BF16), pltpu.VMEM((nh, chunk, width), BF16),
+            pltpu.VMEM((f, chunk, width), BF16), pltpu.VMEM((f, chunk, width), BF16),
+            DMA((y,)), DMA((y,)), DMA((1,)), DMA((1,)), DMA((f,)), DMA((f,))]
 
 
 class Sum:
-    count = 7
+    count = 12
 
     def __init__(self, grid, grad, own, scratch):
-        self.grid, self.grad, self.own = grid, grad, own
-        self.ia, self.ob, self.ib, self.sa, self.ra, self.sb, self.rb = scratch
+        self.grid, self.grad, self.own, self.pushed = grid, grad, own, True
+        (self.ia, self.keep, self.ob, self.ib, self.oc, self.ic,
+         self.sa, self.ra, self.sb, self.rb, self.sc, self.rc) = scratch
 
     def copy_y(self, k):
         g = self.grid
-        return remote(self.grad.at[g.yto(k)], self.ia.at[k], self.sa.at[k], self.ra.at[k], "dp",
-                      g.z * g.ny + g.yto(k))
-
-    def copy_z(self, k):
-        g = self.grid
-        return remote(self.ob.at[k], self.ib.at[k], self.sb.at[k], self.rb.at[k], "dp", g.zto(k) * g.ny + g.y)
+        return remote(self.grad.at[g.yto(k)], self.ia.at[k], self.sa.at[k], self.ra.at[k], "dp", g.at(g.z, g.yto(k)))
+
+    def copy_near(self):
+        g = self.grid
+        return remote(self.ob, self.ib, self.sb.at[0], self.rb.at[0], "dp", g.at(g.near, g.y))
+
+    def copy_far(self, k):
+        g = self.grid
+        return remote(self.oc.at[k], self.ic.at[k], self.sc.at[k], self.rc.at[k], "dp", g.at(g.far(k), g.y))
 
     def push(self):
         for k in range(self.grid.ny - 1):
             self.copy_y(k).start()
 
-    def pass_on(self):
-        g = self.grid
+    def half(self, p):
+        g = self.grid
+        whole = self.grad[g.y, p].astype(F32)
         for k in range(g.ny - 1):
+            whole = whole + self.ia[k, p].astype(F32)
+        return whole
+
+    def near(self):
+        g = self.grid
+        for k in range(g.ny - 1 if self.pushed else 0):
             self.copy_y(k).wait_recv()
-        for k in range(g.nz):
-            z = g.zto(k)
-            whole = self.grad[g.y, z].astype(F32)
-            for j in range(g.ny - 1):
-                whole = whole + self.ia[j, z].astype(F32)
-            if k < g.nz - 1:
-                self.ob[k] = whole.astype(BF16)
-                self.copy_z(k).start()
-            else:
-                self.own[...] = whole
+        self.ob[...] = self.half(1 - g.p).astype(BF16)
+        self.copy_near().start()
+        self.keep[...] = self.half(g.p)
+
+    def far(self):
+        g = self.grid
+        self.copy_near().wait_recv()
+        for k in range(g.nh - 1):
+            a = g.other(k)
+            self.oc[k] = (self.keep[a] + self.ib[a].astype(F32)).astype(BF16)
+            self.copy_far(k).start()
+        self.own[...] = self.keep[g.a] + self.ib[g.a].astype(F32)
 
     def collect(self):
         whole = self.own[...]
-        for k in range(self.grid.nz - 1):
-            self.copy_z(k).wait_recv()
-            whole = whole + self.ib[k].astype(F32)
+        for k in range(self.grid.nh - 1):
+            self.copy_far(k).wait_recv()
+            whole = whole + self.ic[k].astype(F32)
         self.own[...] = whole
 
     def drain(self):
         g = self.grid
-        for k in range(g.ny - 1):
+        for k in range(g.ny - 1 if self.pushed else 0):
             self.copy_y(k).wait_send()
-        for k in range(g.nz - 1):
-            self.copy_z(k).wait_send()
+        self.copy_near().wait_send()
+        for k in range(g.nh - 1):
+            self.copy_far(k).wait_send()
 
 
 def spread_scratch(ny, nz):
-    y, z = max(ny - 1, 1), max(nz - 1, 1)
-    return [DMA((z,)), DMA((z,)), DMA((nz, y)), DMA((nz, y))]
+    y, f = max(ny - 1, 1), max(nz // 2 - 1, 1)
+    return [DMA((f,)), DMA((f,)), DMA((1,)), DMA((1,)), DMA((2, y)), DMA((2, y))]
 
 
 class Spread:
-    count = 4
+    count = 6
 
     def __init__(self, grid, own, result, scratch):
         self.grid, self.own, self.result = grid, own, result
-        self.sz, self.rz, self.sy, self.ry = scratch
-
-    def back_z(self, k):
-        g = self.grid
-        r = self.result.at[g.y, g.z]
-        return remote(r, r, self.sz.at[k], self.rz.at[k], "dp", g.zto(k) * g.ny + g.y)
-
-    def back_y(self, k, j):
-        g = self.grid
-        r = self.result.at[g.y, g.z if k == g.nz - 1 else g.zfrom(k)]
-        return remote(r, r, self.sy.at[k, j], self.ry.at[k, j], "dp", g.z * g.ny + g.yto(j))
+        self.sf, self.rf, self.sn, self.rn, self.sy, self.ry = scratch
+
+    def to_far(self, k):
+        g = self.grid
+        r = self.result.at[g.y, g.p, g.a]
+        return remote(r, r, self.sf.at[k], self.rf.at[k], "dp", g.at(g.far(k), g.y))
+
+    def to_near(self):
+        g = self.grid
+        r = self.result.at[g.y, g.p]
+        return remote(r, r, self.sn.at[0], self.rn.at[0], "dp", g.at(g.near, g.y))
+
+    def to_y(self, i, k):
+        g = self.grid
+        r = self.result.at[g.y, g.p if i == 0 else 1 - g.p]
+        return remote(r, r, self.sy.at[i, k], self.ry.at[i, k], "dp", g.at(g.z, g.yto(k)))
 
     def start(self):
         g = self.grid
         whole = self.own[...]
-        self.result[g.y, g.z] = whole.astype(BF16)
-        for k in range(g.nz - 1):
-            self.back_z(k).start()
+        self.result[g.y, g.p, g.a] = whole.astype(BF16)
+        for k in range(g.nh - 1):
+            self.to_far(k).start()
+        return square(whole)
+
+    def second(self):
+        g = self.grid
+        for k in range(g.nh - 1):
+            self.to_far(k).wait_recv()
+        self.to_near().start()
         for k in range(g.ny - 1):
-            self.back_y(g.nz - 1, k).start()
-        return square(whole)
-
-    def forward(self):
-        g = self.grid
-        for k in range(g.nz - 1):
-            self.back_z(k).wait_recv()
-            for j in range(g.ny - 1):
-                self.back_y(k, j).start()
+            self.to_y(0, k).start()
+
+    def third(self):
+        self.to_near().wait_recv()
+        for k in range(self.grid.ny - 1):
+            self.to_y(1, k).start()
 
     def close(self):
         g = self.grid
-        for k in range(g.nz):
-            for j in range(g.ny - 1):
-                self.back_y(k, j).wait_recv()
-        for k in range(g.nz - 1):
-            self.back_z(k).wait_send()
-        for k in range(g.nz):
-            for j in range(g.ny - 1):
-                self.back_y(k, j).wait_send()
+        for i in range(2):
+            for k in range(g.ny - 1):
+                self.to_y(i, k).wait()
+        for k in range(g.nh - 1):
+            self.to_far(k).wait_send()
+        self.to_near().wait_send()
 
 
 def take(rest, cls, count):
@@ -716,42 +768,44 @@
     greet({"mp": n, "dp": ny * nz})
     at = lambda b: pl.ds(pl.multiple_of(b * rows, rows), rows)
 
-    squares = squares_ref[0:1]
-    for s in olds:
-        squares = squares + s.start()
-    load.wait()
-    w[...] = w32[...].astype(BF16)
-
-    def first_block(b):
-        return sum(mm(dqkv_ref[s, :, at(b)], w[s], TN) for s in range(3))
-
-    scat.push(first_block)
     for s in range(3):
         acc = jnp.zeros((inner, width), F32)
         for b in range(n):
             acc = acc + mm(dqkv_ref[s, :, at(b)], h_ref[b])
         qg[s] = acc.reshape(qg.shape[1:]).astype(BF16)
         sums[s].push()
-        if s == 0:
-            whole = scat.pass_on(first_block)
-            bias_dp.start(jnp.broadcast_to(bg_ref[...], bias_dp.slots.shape[1:]))
-            pair_dp.start(pair_ref[...])
+    load.wait()
+    w[...] = w32[...].astype(BF16)
+
+    def first_block(b):
+        return sum(mm(dqkv_ref[s, :, at(b)], w[s], TN) for s in range(3))
+
+    scat.push(first_block)
+    squares = squares_ref[0:1]
     for s in olds:
-        s.forward()
+        squares = squares + s.start()
+    whole = scat.pass_on(first_block)
+    bias_dp.start(jnp.broadcast_to(bg_ref[...], bias_dp.slots.shape[1:]))
+    pair_dp.start(pair_ref[...])
+    sums[0].near()
+    for s in olds:
+        s.second()
+    sums[1].near()
     dh1 = scat.finish(whole)
     dv, gain, shift = norm_back(x_ref[...].astype(F32), np_ref[0:1], dh1)
     gi_ref[...] = dx_ref[...] + dv
     small_mp.start(jnp.concatenate([gain, shift, mid_small_ref[0:6]], 0))
-    sums[0].pass_on()
+    sums[0].far()
+    sums[2].near()
+    sums[1].far()
     small_dp.start(small_mp.total())
-    sums[1].pass_on()
-    sums[0].collect()
-    squares = squares + spreads[0].start()
-    sums[2].pass_on()
-    for s in (1, 2):
-        sums[s].collect()
-        squares = squares + spreads[s].start()
-    spreads[0].forward()
+    for s in olds:
+        s.third()
+    sums[2].far()
+    for s, t in zip(sums, spreads):
+        s.collect()
+        squares = squares + t.start()
+    spreads[0].second()
     bias = bias_dp.total()
     bias_ref[...] = bias
     pairs = pair_dp.total()
@@ -761,9 +815,11 @@
     sq_mp.start(jnp.where(row == 0, squares, jnp.where(row == 1, local, 0.0)))
     small = small_dp.total()
     small_ref[...] = small
-    spreads[1].forward()
+    spreads[1].second()
     sq_dp.start(sq_mp.total())
-    spreads[2].forward()
+    spreads[2].second()
+    for s in spreads:
+        s.third()
     norm_ref[...] = sq_dp.total()[0:1] + sq_dp.slots[0, 1:2] + square(small)
     for s in olds + spreads:
         s.close()
@@ -776,22 +832,22 @@
     inner = qkv_weight.shape[1]
     ndp = ny * nz
     hidden = bias_grad.shape[1]
-    chunks = (3, ny, nz, inner // ndp, width)
+    chunks = (3, ny, 2, nz // 2, inner // ndp, width)
     f = lambda *s: jax.ShapeDtypeStruct(s, F32)
     late = len(owns)
     return pl.pallas_call(
         functools.partial(leave_kernel, n, ny, nz, late),
-        out_shape=(f(rows, width), *[jax.ShapeDtypeStruct((ny, nz, *o.shape), BF16) for o in owns],
+        out_shape=(f(rows, width), *[jax.ShapeDtypeStruct((ny, 2, nz // 2, *o.shape), BF16) for o in owns],
                    jax.ShapeDtypeStruct(chunks, BF16), f(8, width), f(8, hidden), f(8, LANE), f(1, LANE)),
         in_specs=[VM] * (9 + late) + [HBM], out_specs=[VM] * (6 + late),
         scratch_shapes=[pltpu.VMEM(qkv_weight.shape, F32), pltpu.VMEM(qkv_weight.shape, BF16),
                         pltpu.VMEM(chunks, BF16), pltpu.VMEM((3, inner // ndp, width), F32), DMA,
                         *scatter_scratch(n, rows, width),
-                        *[s for _ in range(3) for s in sum_scratch(ny, nz, inner // ndp, width)],
+                        *[s for _ in range(3) for s in sum_scratch(chunks[1:])],
                         *[s for _ in range(3 + late) for s in spread_scratch(ny, nz)],
                         *share_scratch(n, 8, width), *share_scratch(ndp, 8, width), *share_scratch(ndp, 8, hidden),
                         *share_scratch(ndp, 8, LANE), *share_scratch(n, 8, LANE), *share_scratch(ndp, 8, LANE)],
-        compiler_params=pltpu.CompilerParams(collective_id=2, has_side_effects=True, vmem_limit_bytes=60 << 20),
+        compiler_params=pltpu.CompilerParams(collective_id=2, has_side_effects=True, vmem_limit_bytes=LEAVE_MIB << 20),
         name="leave",
     )(x, dx, params, dqkv, h, bias_grad, pair_grad, squares, small, *owns, qkv_weight)
 
@@ -809,27 +865,37 @@
     return dx + dv, og, ig, pg, qg, small, bias, pair, total
 
 
-PASS_AT = (4, 10, 24, 38, 45)
-COLLECT_AT = (15, 30, 44, 58, 72)
-FORWARD_AT = (40, 55)
-EARLY = 2
-
-
-def back_kernel(heads, ny, nz, parts, coords_ref, qkv_ref, do_ref, p_ref, og_ref, ig_ref, pg_ref,
-                dqkv_ref, pair_ref, squares_ref, *rest):
+NEAR_AT = (0, 0, 6, 14, 20)
+FAR_AT = (4, 7, 16, 26, 32)
+COLLECT_AT = (10, 15, 28, 38, 42)
+SECOND_AT = (18, 24, 36, 48, 52)
+THIRD_AT = (26, 33, 46, 60, 64)
+FIRST = 1
+EARLY = 5
+BACK_MIB = 24
+LEAVE_MIB = 16
+
+
+def back_kernel(heads, ny, nz, parts, pushes, coords_ref, qkv_ref, do_ref, p_ref, og_ref, ig_ref, pg_ref, *rest):
+    lands, (dqkv_ref, pair_ref, squares_ref), rest = rest[:pushes], rest[pushes:pushes + 3], rest[pushes + 3:]
     owns, rest = rest[:2 * parts + 1 - EARLY], rest[2 * parts + 1 - EARLY:]
-    results, (dist, ds, early), rest = rest[:EARLY], rest[EARLY:EARLY + 3], rest[EARLY + 3:]
+    results, (dist, ds), rest = rest[:EARLY], rest[EARLY:EARLY + 2], rest[EARLY + 2:]
+    early, rest = rest[:EARLY], rest[EARLY:]
     hd, span = do_ref.shape[1:]
     grid = Grid(ny, nz)
     pieces = [g.at[i] for g in (og_ref, ig_ref) for i in range(parts)] + [pg_ref]
-    places = [early.at[i] for i in range(EARLY)] + list(owns)
+    places = [*early, *owns]
     scratch, rest = take(rest, Sum, len(pieces))
     sums = [Sum(grid, *a) for a in zip(pieces, places, scratch)]
     scratch, rest = take(rest, Spread, EARLY)
     spreads = [Spread(grid, *a) for a in zip(places, results, scratch)]
+    for s, land in zip(sums, lands):
+        s.ia, s.pushed = land, False
     greet({"dp": ny * nz})
-    for s in sums:
+    for s in sums[pushes:]:
         s.push()
+    for s in sums[:FIRST]:
+        s.near()
     squares_ref[...] = jnp.zeros_like(squares_ref)
 
     def collect(i):
@@ -839,10 +905,13 @@
 
     jobs = {}
     for i, s in enumerate(sums):
-        jobs.setdefault(PASS_AT[i], []).append(s.pass_on)
+        if i >= FIRST:
+            jobs.setdefault(NEAR_AT[i], []).append(s.near)
+        jobs.setdefault(FAR_AT[i], []).append(s.far)
         jobs.setdefault(COLLECT_AT[i], []).append(functools.partial(collect, i))
     for i, s in enumerate(spreads):
-        jobs.setdefault(FORWARD_AT[i], []).append(s.forward)
+        jobs.setdefault(SECOND_AT[i], []).append(s.second)
+        jobs.setdefault(THIRD_AT[i], []).append(s.third)
     last = heads + span // SUB
 
     def beside(step, first, end):
@@ -864,26 +933,30 @@
         s.drain()
 
 
-def attention_back_sums(qkv, do, probs, coords, ny, nz, og, ig, pg):
+def attention_back_sums(qkv, do, probs, coords, ny, nz, og, ig, pg, lands):
     _, heads, hd, span = qkv.shape
     width = og.shape[1]
-    ndp, parts = ny * nz, 2
-    cut = lambda g, p: g.reshape(p, ny, nz, g.shape[0] // (p * ndp), width)
+    ndp, parts, pushes = ny * nz, PARTS, len(lands)
+    lands = [v.reshape(ny - 1, 2, nz // 2, -1, width) for v in lands]
+    cut = lambda g, p: g.reshape(p, ny, 2, nz // 2, g.shape[0] // (p * ndp), width)
     og, ig, pg = cut(og, parts), cut(ig, parts), cut(pg, 1)[0]
     shapes = [og.shape[1:]] * parts + [ig.shape[1:]] * parts + [pg.shape]
     f = lambda *s: jax.ShapeDtypeStruct(s, F32)
     return pl.pallas_call(
-        functools.partial(back_kernel, heads, ny, nz, parts),
+        functools.partial(back_kernel, heads, ny, nz, parts, pushes),
         out_shape=(jax.ShapeDtypeStruct(qkv.shape, BF16), f(SUB, KERN), f(SUB, LANE),
-                   *[f(*s[2:]) for s in shapes[EARLY:]], *[jax.ShapeDtypeStruct(s, BF16) for s in shapes[:EARLY]]),
-        in_specs=[VM] * 7, out_specs=[VM] * (3 + len(shapes)),
+                   *[f(*s[3:]) for s in shapes[EARLY:]], *[jax.ShapeDtypeStruct(s, BF16) for s in shapes[:EARLY]]),
+        in_specs=[VM] * (7 + pushes), out_specs=[VM] * (3 + len(shapes)),
         scratch_shapes=[pltpu.VMEM((span, span), F32), pltpu.VMEM((span // LANE, SUB * span, LANE), F32),
-                        pltpu.VMEM((EARLY, *shapes[0][2:]), F32),
-                        *[s for shape in shapes for s in sum_scratch(ny, nz, shape[2], width)],
+                        *[pltpu.VMEM(shape[3:], F32) for shape in shapes[:EARLY]],
+                        *[s for shape in shapes for s in sum_scratch(shape)],
                         *[s for _ in range(EARLY) for s in spread_scratch(ny, nz)]],
-        compiler_params=pltpu.CompilerParams(collective_id=3, has_side_effects=True, vmem_limit_bytes=60 << 20),
+        compiler_params=pltpu.CompilerParams(collective_id=3, has_side_effects=True, vmem_limit_bytes=BACK_MIB << 20),
         name="attend_back_sums",
-    )(coords, qkv, do, probs, og, ig, pg)
+    )(coords, qkv, do, probs, og, ig, pg, *lands)
+
+
+PUSHES = 2
 
 
 def adam_step(weight, grad, first, second, clip, fix_one, fix_two, rate, decay):
@@ -899,15 +972,18 @@
     qkv_weight, proj_weight, pair_weight, in_weight, in_bias, out_weight, params = weights
     heads = pair_weight.shape[0]
     pair_low = pair_weight.astype(BF16)
-    h, dy_all, qkv = enter(n, heads, block_in, cotangent, params, qkv_weight)
+    h, qkv = enter(n, heads, block_in, params, qkv_weight)
     o, probs = attention(qkv, coords, lengths, pair_low)
-    block_out, dx, do, og, ig, pg, bg, small = middle(
-        n, block_in, cotangent, dy_all, o, params, in_bias.reshape(1, -1), proj_weight, in_weight, out_weight)
+    dy, _ = lax.optimization_barrier((cotangent, qkv))
+    dys = [cotangent] + [lax.ppermute(dy, "mp", [((i + k) % n, i) for i in range(n)]) for k in range(1, n)]
     ny = n // 2 if ndp % (n // 2) == 0 else 1
     nz = ndp // ny
-    inner = proj_weight.shape[0]
-    if lengths.shape[0] == 1 and inner % (8 * ndp) == 0 and og.shape[0] % (32 * ndp) == 0:
-        dqkv, pair_grad, squares, *parts = attention_back_sums(qkv, do, probs, coords, ny, nz, og, ig, pg)
+    inner, hidden = proj_weight.shape[0], in_weight.shape[0]
+    beside = lengths.shape[0] == 1 and nz % 2 == 0 and inner % (8 * ndp) == 0 and hidden % (16 * PARTS * ndp) == 0
+    block_out, dx, do, og, ig, pg, bg, small, *lands = middle(
+        n, ny, nz, PUSHES if beside else 0, block_in, dys, o, params, in_bias.reshape(1, -1), proj_weight, in_weight, out_weight)
+    if beside:
+        dqkv, pair_grad, squares, *parts = attention_back_sums(qkv, do, probs, coords, ny, nz, og, ig, pg, lands)
         owns, done = parts[:-EARLY], parts[-EARLY:]
         grad_input, *sums, qg, small, bias, pair, total = leave(
             n, ny, nz, block_in, dx, params, dqkv.reshape(3, inner, -1), h, bg, pair_grad, squares, small, owns, qkv_weight)

time: 240 us -> 212 us (0.88)
  Pallas kernels: 213 us -> 185 us
  other arithmetic: 18.6 us -> 13.9 us
  local copies, waits for them, and re-layouts: 4.05 us -> 7.37 us
    pallas_call x1, Pallas kernels: 58.6 us -> 43.5 us  [leave(): pl.pallas_call(functools.partial(leave_kernel, n, ny, nz, late), out_shap...]
    pallas_call x2, Pallas kernels: 103 us -> 97.6 us  [the longest x1 58.2 us: attention_back_sums(): pl.pallas_call(functools.partial(back_kernel, heads, ny, nz, parts, pushe...]
    pallas_call x1, Pallas kernels: 32.8 us -> 28.7 us  [attention(): pl.pallas_call(functools.partial(fwd_kernel, heads, mols), out_shape=(jax...]
    pallas_call x1, Pallas kernels: 18.6 us -> 14.7 us  [enter(): pl.pallas_call(functools.partial(enter_kernel, n), out_shape=(jax.ShapeDt...]
    sub x6, other arithmetic: 16.4 us -> 12.9 us  [adam_step(): return (weight - rate * (ratio + decay * weight), first_new, second_new)]
    unnamed x50 -> x60, local copies, waits for them, and re-layouts: 3.47 us -> 6.68 us
  transfers between devices with their start and end apart: 0 -> 3, of which waited for: 0 -> 0; matrix products, arithmetic and copies ran while one was open for 0% -> 1% of each run, Pallas kernels for 0% -> 14%
where the time goes in v4:
time: 212 us; the launch traced here: 211 us
  Pallas kernels  185 us (87%)
  other arithmetic  13.9 us (7%)
  local copies, waits for them, and re-layouts  7.37 us (3%)
  between operations  2.99 us (1%)
  starting transfers between devices  2.26 us (1%)
    pallas_call x1, Pallas kernels, attention_back_sums(): pl.pallas_call(functools.partial(back_kernel, heads, ny, nz, parts, pushe...  58.2 us
    pallas_call x1, Pallas kernels, leave(): pl.pallas_call(functools.partial(leave_kernel, n, ny, nz, late), out_shap...  43.5 us
    pallas_call x1, Pallas kernels, middle(): pl.pallas_call(functools.partial(middle_kernel, n, ny, nz, pushes), out_s...  39.4 us
    pallas_call x1, Pallas kernels, attention(): pl.pallas_call(functools.partial(fwd_kernel, heads, mols), out_shape=(jax...  28.7 us
    pallas_call x1, Pallas kernels, enter(): pl.pallas_call(functools.partial(enter_kernel, n), out_shape=(jax.ShapeDt...  14.7 us
    sub x6, other arithmetic, adam_step(): return (weight - rate * (ratio + decay * weight), first_new, second_new)  12.9 us
    unnamed x60, local copies, waits for them, and re-layouts  6.68 us
  transfers between devices with their start and end apart: 3, of which 0 were waited for; matrix products, arithmetic and copies ran while one was open for 1% of the time, Pallas kernels for 14%

profile of v4, /device:TPU:0, one launch (start us, length us, event | category | flops | bytes accessed | tf_op | source)
XLA Modules:
  0.0 211.1 jit_solution(4515425011225166395)
XLA Ops:
  0.7 14.7 %enter.1 = (bf16[4,128,768]{2,1,0:T(8,128)(2,1)}, bf16[3,8,24,512]{3,2,1,0:T(8,128)(2,1)}) custom-call(bf16[128,768]{1,0:T(8,128)(2,1)} %x_ref.5, f32[5,768]{1,0:T(8,128)} %np_ref.5, f32[3,192,768]{2,1,0:T(8,128)} %rest_0_.3), custom_call_target="tpu_custom_call" | custom-call | tf_op jit(solution)/shard_map/enter/pallas_call | solution.py:422
  15.4 1.9 collective-permute-start
  17.3 0.4 collective-permute-start.1
  17.7 0.0 collective-permute-start.2
  17.7 0.7 convert_element_type.21.w_ref
  18.3 0.7 reshape.110.bias_ref
  19.8 0.0 copy-start.6
  19.8 1.1 copy-done.6
  20.8 0.7 copy-done.10
  21.5 0.7 copy-done.12
  22.2 0.0 copy-start.8
  22.2 0.0 copy-start.9
  22.2 28.7 %attend.1 = (bf16[8,24,512]{2,1,0:T(8,128)(2,1)S(1)}, bf16[4096,512]{1,0:T(8,128)(2,1)S(1)}) custom-call(s32[1,16]{1,0:T(1,128)S(1)} %copy-done.12, f32[3,512]{1,0:T(4,128)S(1)} %copy-done.10, bf16[3,8,24,512]{3,2,1,0:T(8,128)(2,1)S(1)} %copy-done.6, bf16[8,128]{1,0:T(8,128)(2,1)S(1)} %convert_element_type.21.w_ref), custom_call_target="tpu_custom_call" | custom-call | flops 1006632960 | bytes 2097152 | tf_op jit(solution)/shard_map/attend/pallas_call | solution.py:139
  51.0 0.0 collective-permute-done.rest_1_
  51.0 0.0 collective-permute-done.1.rest_2_
  51.0 0.0 collective-permute-done.2.rest_3_
  51.0 0.0 copy-done.1
  51.0 0.0 copy-done.2
  51.0 0.0 copy-done.3
  51.0 0.0 copy-done.4
  51.0 0.0 copy-done.8
  51.1 0.0 copy-done.9
  51.1 0.0 copy-start.7
  51.1 0.0 copy-start.11
  51.1 39.4 %middle.1 = (f32[128,768]{1,0:T(8,128)S(1)}, f32[128,768]{1,0:T(8,128)S(1)}, bf16[8,24,512]{2,1,0:T(8,128)(2,1)S(1)}, bf16[768,768]{1,0:T(8,128)(2,1)S(1)}, bf16...) custom-call(bf16[128,768]{1,0:T(8,128)(2,1)S(1)} %copy-done.4, ...), custom_call_target="tpu_custom_call" | custom-call | tf_op jit(solution)/shard_map/middle/pallas_call | solution.py:558
  90.5 0.0 copy-done.7
  90.5 0.0 copy-done.11
  90.5 0.0 copy-start
  90.5 0.0 copy-start.5
  90.6 58.2 %attend_back_sums.1 = (bf16[3,8,24,512]{3,2,1,0:T(8,128)(2,1)S(1)}, f32[8,128]{1,0:T(8,128)S(1)}, f32[8,128]{1,0:T(8,128)S(1)}, bf16[2,2,2,48,768]{4,3,2,1,0:T(8...) custom-call(f32[3,512]{1,0:T(4,128)S(1)} %copy-done.11, ...), custom_call_target="tpu_custom_call" | custom-call | tf_op jit(solution)/shard_map/attend_back_sums/pallas_call | solution.py:945
  148.7 0.0 copy-done
  148.7 0.0 copy-done.5
  148.7 43.5 %leave.1 = (f32[128,768]{1,0:T(8,128)S(1)}, bf16[3,2,2,2,24,768]{5,4,3,2,1,0:T(8,128)(2,1)S(1)}, f32[8,768]{1,0:T(8,128)S(1)}, f32[8,768]{1,0:T(8,128)S(1)}, f32[8,128]{1,0:T(8,128)S(1)}, /*index=5*/f32[1,128]{1,0:T(1,128)S(1)}) custom-call(bf16[128,768]{1,0:T(8,128)(2,1)S(1)} %copy-done.4, f32[128,768]{1,0:T(8,128)S(1)} %get-tuple-element.57.dx_ref, ...), custom_call_target="tpu_custom_call" | custom-call | tf_op jit(solution)/shard_map/leave/pallas_call | solution.py:838
  192.2 0.0 copy-start.21
  192.2 0.0 copy-start.22
  192.3 0.0 copy-start.23
  192.3 0.0 copy-start.25
  192.3 0.0 copy-start.26
  192.3 0.0 copy-start.24
  192.3 0.0 copy-start.27
  192.3 0.0 copy-start.28
  192.3 0.0 copy-start.19
  192.3 0.0 copy-start.20
  192.5 0.2 convert_multiply_fusion.2
  192.7 0.0 copy-start.17
  192.8 0.0 copy-start.18
  192.8 0.2 copy-done.21
  193.0 0.0 copy-done.22
  193.0 0.6 multiply_subtract_fusion.4
  193.6 0.0 copy-done.25
  193.6 0.6 multiply_subtract_fusion.5
  194.3 0.6 multiply_subtract_fusion.6
  194.9 1.5 multiply_subtract_fusion.3
  196.4 0.0 copy-done.18
  196.4 0.0 copy-start.15
  196.4 0.0 copy-start.16
  196.4 3.2 %multiply_subtract_fusion.2 = (f32[3,192,768]{2,1,0:T(8,128)}, f32[3,192,768]{2,1,0:T(8,128)}, f32[3,192,768]{2,1,0:T(8,128)}) fusion(f32[3,192,768]{2,1,0:T(8,128)S(1)} %copy-done, f32[]{:T(128)} %bitcast.11, f32[]{:T(128)} %bitcast.10, f32[3,2,2,2,24,768]{5,4,3,2,1,0:T(8,128)S(1)} %convert_multiply_fusion.2, f32[3,192,768]{2,1,0:T(8,128)S(1)} %copy-done.17, ...), kind=kLoop, calls=%fused_computation.14 | loop fusion | flops 6635520 | bytes 12386312 | tf_op jit(solution)/shard_map/sub | solution.py:967
  199.7 0.0 copy-done.13
  199.7 1.0 copy-done.14
  200.7 0.7 copy-done.15
  201.4 0.7 copy-done.16
  202.1 6.3 %multiply_subtract_fusion = (f32[768,768]{1,0:T(8,128)}, f32[768,768]{1,0:T(8,128)}, f32[768,768]{1,0:T(8,128)}, f32[768,768]{1,0:T(8,128)}, f32[768,768]{1,0:T(8,128)}, /*index=5*/f32[768,768]{1,0:T(8,128)}) fusion(f32[768,768]{1,0:T(8,128)S(1)} %copy-done.2, f32[]{:T(128)} %bitcast.11, f32[]{:T(128)} %bitcast.10, f32[]{:T(128)} %bitcast.8, ...), kind=kLoop, calls=%fused_computation.5 | loop fusion | flops 23592960 | bytes 30670860 | tf_op jit(solution)/shard_map/sub | solution.py:967
  208.4 0.7 copy.53
  209.2 0.7 copy.54
  (18 shorter events, 0.1 us)
Async XLA Ops:
  15.4 35.6 %collective-permute-start = (bf16[128,768]{1,0:T(8,128)(2,1)}, bf16[128,768]{1,0:T(8,128)(2,1)S(1)}, u32[]{:S(2)}, u32[]{:S(2)}) collective-permute-start(bf16[128,768]{1,0:T(8,128)(2,1)} %rest_0_.2), channel_id=1, source_target_pairs={{1,0},{2,1},{3,2},{0,3},{5,4},{6,5},{7,6},{4,7},{9,8},{10,9},{11,1... | collective-permute-start | bytes 589832 | tf_op jit(solution)/shard_map/ppermute | solution.py:978
  17.3 33.7 %collective-permute-start.1 = (bf16[128,768]{1,0:T(8,128)(2,1)}, bf16[128,768]{1,0:T(8,128)(2,1)S(1)}, u32[]{:S(2)}, u32[]{:S(2)}) collective-permute-start(bf16[128,768]{1,0:T(8,128)(2,1)} %rest_0_.2), channel_id=1, source_target_pairs={{2,0},{3,1},{0,2},{1,3},{6,4},{7,5},{4,6},{5,7},{10,8},{11,9},{8,1... | collective-permute-start | bytes 589832 | tf_op jit(solution)/shard_map/ppermute | solution.py:978
  17.7 33.3 %collective-permute-start.2 = (bf16[128,768]{1,0:T(8,128)(2,1)}, bf16[128,768]{1,0:T(8,128)(2,1)S(1)}, u32[]{:S(2)}, u32[]{:S(2)}) collective-permute-start(bf16[128,768]{1,0:T(8,128)(2,1)} %rest_0_.2), channel_id=1, source_target_pairs={{3,0},{0,1},{1,2},{2,3},{7,4},{4,5},{5,6},{6,7},{11,8},{8,9},{9,10... | collective-permute-start | bytes 589832 | tf_op jit(solution)/shard_map/ppermute | solution.py:978
  19.8 1.1 copy-start.6
  20.8 0.7 copy-start.10
  21.5 0.7 copy-start.12
  22.2 28.8 %copy-start.1 = (f32[768,768]{1,0:T(8,128)S(1)}, f32[768,768]{1,0:T(8,128)}, u32[]{:S(2)}) copy-start(f32[768,768]{1,0:T(8,128)} %iw_hbm.1) | copy-start | bytes 7077892
  22.2 28.8 %copy-start.2 = (f32[768,768]{1,0:T(8,128)S(1)}, f32[768,768]{1,0:T(8,128)}, u32[]{:S(2)}) copy-start(f32[768,768]{1,0:T(8,128)} %ow_hbm.1) | copy-start | bytes 7077892
  22.2 28.8 %copy-start.3 = (f32[192,768]{1,0:T(8,128)S(1)}, f32[192,768]{1,0:T(8,128)}, u32[]{:S(2)}) copy-start(f32[192,768]{1,0:T(8,128)} %pw_hbm.1) | copy-start | bytes 1769476
  22.2 28.8 %copy-start.4 = (bf16[128,768]{1,0:T(8,128)(2,1)S(1)}, bf16[128,768]{1,0:T(8,128)(2,1)}, u32[]{:S(2)}) copy-start(bf16[128,768]{1,0:T(8,128)(2,1)} %x_ref.5) | copy-start | bytes 589828
  22.2 28.8 %copy-start.8 = (f32[5,768]{1,0:T(8,128)S(1)}, f32[5,768]{1,0:T(8,128)}, u32[]{:S(2)}) copy-start(f32[5,768]{1,0:T(8,128)} %np_ref.5) | copy-start | bytes 46084
  22.2 28.8 %copy-start.9 = (bf16[128,768]{1,0:T(8,128)(2,1)S(1)}, bf16[128,768]{1,0:T(8,128)(2,1)}, u32[]{:S(2)}) copy-start(bf16[128,768]{1,0:T(8,128)(2,1)} %rest_0_.2) | copy-start | bytes 589828
  51.1 39.4 %copy-start.7 = (bf16[3,8,24,512]{3,2,1,0:T(8,128)(2,1)S(1)}, bf16[3,8,24,512]{3,2,1,0:T(8,128)(2,1)}, u32[]{:S(2)}) copy-start(bf16[3,8,24,512]{3,2,1,0:T(8,128)(2,1)} %get-tuple-element.53.qkv_ref) | copy-start | bytes 1769476
  51.1 39.4 %copy-start.11 = (f32[3,512]{1,0:T(4,128)S(1)}, f32[3,512]{1,0:T(4,128)}, u32[]{:S(2)}) copy-start(f32[3,512]{1,0:T(4,128)} %coords_ref.3) | copy-start | bytes 18436
  90.5 58.2 %copy-start = (f32[3,192,768]{2,1,0:T(8,128)S(1)}, f32[3,192,768]{2,1,0:T(8,128)}, u32[]{:S(2)}) copy-start(f32[3,192,768]{2,1,0:T(8,128)} %rest_0_.3) | copy-start | bytes 5308420
  90.5 58.2 %copy-start.5 = (bf16[4,128,768]{2,1,0:T(8,128)(2,1)S(1)}, bf16[4,128,768]{2,1,0:T(8,128)(2,1)}, u32[]{:S(2)}) copy-start(bf16[4,128,768]{2,1,0:T(8,128)(2,1)} %get-tuple-element.66.h_ref) | copy-start | bytes 2359300
  192.2 0.7 copy-start.21
  192.2 0.7 copy-start.22
  192.3 1.4 copy-start.23
  192.3 1.4 copy-start.25
  192.3 1.4 copy-start.26
  192.3 2.0 copy-start.24
  192.3 2.0 copy-start.27
  192.3 2.0 copy-start.28
  192.3 2.6 %copy-start.19 = (f32[192,768]{1,0:T(8,128)S(1)}, f32[192,768]{1,0:T(8,128)}, u32[]{:S(2)}) copy-start(f32[192,768]{1,0:T(8,128)} %param.46) | copy-start | bytes 1769476
  192.3 2.6 %copy-start.20 = (f32[192,768]{1,0:T(8,128)S(1)}, f32[192,768]{1,0:T(8,128)}, u32[]{:S(2)}) copy-start(f32[192,768]{1,0:T(8,128)} %param.39) | copy-start | bytes 1769476
  192.7 3.6 %copy-start.17 = (f32[3,192,768]{2,1,0:T(8,128)S(1)}, f32[3,192,768]{2,1,0:T(8,128)}, u32[]{:S(2)}) copy-start(f32[3,192,768]{2,1,0:T(8,128)} %param.45) | copy-start | bytes 5308420
  192.8 3.6 %copy-start.18 = (f32[3,192,768]{2,1,0:T(8,128)S(1)}, f32[3,192,768]{2,1,0:T(8,128)}, u32[]{:S(2)}) copy-start(f32[3,192,768]{2,1,0:T(8,128)} %param.38) | copy-start | bytes 5308420
  196.4 3.3 %copy-start.13 = (f32[768,768]{1,0:T(8,128)S(1)}, f32[768,768]{1,0:T(8,128)}, u32[]{:S(2)}) copy-start(f32[768,768]{1,0:T(8,128)} %param.50) | copy-start | bytes 7077892
  196.4 4.3 %copy-start.14 = (f32[768,768]{1,0:T(8,128)S(1)}, f32[768,768]{1,0:T(8,128)}, u32[]{:S(2)}) copy-start(f32[768,768]{1,0:T(8,128)} %param.43) | copy-start | bytes 7077892
  196.4 5.0 %copy-start.15 = (f32[768,768]{1,0:T(8,128)S(1)}, f32[768,768]{1,0:T(8,128)}, u32[]{:S(2)}) copy-start(f32[768,768]{1,0:T(8,128)} %param.48) | copy-start | bytes 7077892
  196.4 5.7 %copy-start.16 = (f32[768,768]{1,0:T(8,128)S(1)}, f32[768,768]{1,0:T(8,128)}, u32[]{:S(2)}) copy-start(f32[768,768]{1,0:T(8,128)} %param.41) | copy-start | bytes 7077892

commit v5 on v4

--- a/solution.py
+++ b/solution.py
@@ -156,7 +156,7 @@
     )(lengths, coords, qkv, w)
 
 
-def back_pairs(heads, coords_ref, qkv_ref, do_ref, p_ref, dqkv_ref, dist, ds, beside):
+def back_pairs(heads, coords_ref, qkv_ref, do_ref, p_ref, dqkv_ref, dist, ds, beside, between):
     hd, span = do_ref.shape[1:]
     scale = 1.0 / math.sqrt(hd)
     step = LANE
@@ -186,9 +186,10 @@
         return carry
 
     lax.fori_loop(0, heads, head, 0)
+    between()
 
     def group(g, acc):
-        beside(heads + g, heads, heads + span // SUB)
+        beside(100 + g, 100, 100 + span // SUB)
         i0 = pl.multiple_of(g * SUB, SUB)
 
         left, right = [], []
@@ -209,7 +210,8 @@
     def _():
         pair_ref[...] = jnp.zeros_like(pair_ref)
 
-    pair_ref[...] += back_pairs(heads, coords_ref, qkv_ref, do_ref, p_ref, dqkv_ref, dist, ds, lambda *_: None)
+    pair_ref[...] += back_pairs(heads, coords_ref, qkv_ref, do_ref, p_ref, dqkv_ref, dist, ds,
+                                lambda *_: None, lambda: None)
 
 
 def attention_back(qkv, do, probs, coords):
@@ -747,109 +749,144 @@
     return jnp.sum(jnp.sum(v * v, axis=1, keepdims=True), axis=0, keepdims=True)
 
 
-def leave_kernel(n, ny, nz, late, x_ref, dx_ref, np_ref, dqkv_ref, h_ref, bg_ref, pair_ref, squares_ref,
-                 mid_small_ref, *rest):
-    owns, (w_hbm, gi_ref), rest = rest[:late], rest[late:late + 2], rest[late + 2:]
-    results, rest = rest[:late], rest[late:]
-    (sq_ref, small_ref, bias_ref, pairs_ref, norm_ref, w32, w, qg, qown, wsem), rest = rest[:10], rest[10:]
+NEAR_AT = (-1, -1, 5, 100, 105, 113, 120, 128)
+FAR_AT = (2, 5, 99, 111, 113, 123, 131, 140)
+COLLECT_AT = (7, 99, 106, 123, 124, 133, 144, 154)
+SECOND_AT = (101, 110, 120, 139, 140, 149, 159, 167)
+THIRD_AT = (114, 126, 139, 154, 157, 168, 168, 168)
+NORM_AT = 118
+SMALL_AT = 130
+REAR_MIB = 36
+
+
+def rear_kernel(n, ny, nz, pushes, coords_ref, qkv_ref, do_ref, p_ref, og_ref, ig_ref, pg_ref, x_ref, dx_ref, np_ref,
+                h_ref, bg_ref, mid_small_ref, w_hbm, *rest):
+    lands, rest = rest[:pushes], rest[pushes:]
+    early = 2 * PARTS + 1
+    results, (sq_ref, gi_ref, small_ref, bias_ref, pairs_ref, norm_ref), rest = rest[:early], rest[early:early + 6], rest[early + 6:]
+    (dist, ds, dqkv, flat, w32, w, qg, qown, kept, squares, wsem), rest = rest[:11], rest[11:]
+    owns, rest = rest[:early], rest[early:]
+    _, heads, hd, span = qkv_ref.shape
+    inner = heads * hd
+    rows, width = x_ref.shape
     seat, grid = Seat(n), Grid(ny, nz)
-    rows, width = x_ref.shape
-    inner = w.shape[1]
+    pieces = [g.at[i] for g in (og_ref, ig_ref) for i in range(PARTS)] + [pg_ref] + [qg.at[s] for s in range(3)]
+    places = [*owns, *[qown.at[s] for s in range(3)]]
+    targets = [*results, *[sq_ref.at[s] for s in range(3)]]
+    scat, rest = Scatter(seat, rest[:8]), rest[8:]
+    scratch, rest = take(rest, Sum, early + 3)
+    sums = [Sum(grid, *a) for a in zip(pieces, places, scratch)]
+    scratch, rest = take(rest, Spread, early + 3)
+    spreads = [Spread(grid, *a) for a in zip(places, targets, scratch)]
+    shares = [Share(a, *rest[3 * i:3 * i + 3]) for i, a in enumerate(("mp", "dp", "dp", "dp", "mp", "dp"))]
+    small_mp, small_dp, bias_dp, pair_dp, sq_mp, sq_dp = shares
+    for s, land in zip(sums, lands):
+        s.ia, s.pushed = land, False
+    at = lambda b: pl.ds(pl.multiple_of(b * rows, rows), rows)
     load = pltpu.make_async_copy(w_hbm, w32, wsem)
     load.start()
-    scat, rest = Scatter(seat, rest[:8]), rest[8:]
-    parts, rest = take(rest, Sum, 3)
-    sums = [Sum(grid, qg.at[s], qown.at[s], p) for s, p in enumerate(parts)]
-    parts, rest = take(rest, Spread, 3 + late)
-    spreads = [Spread(grid, s.own, sq_ref.at[i], p) for i, (s, p) in enumerate(zip(sums, parts))]
-    olds = [Spread(grid, o, r, p) for o, r, p in zip(owns, results, parts[3:])]
-    shares = [Share(a, *rest[3 * i:3 * i + 3]) for i, a in enumerate(("mp", "dp", "dp", "dp", "mp", "dp"))]
-    small_mp, small_dp, bias_dp, pair_dp, sq_mp, sq_dp = shares
     greet({"mp": n, "dp": ny * nz})
-    at = lambda b: pl.ds(pl.multiple_of(b * rows, rows), rows)
-
-    for s in range(3):
-        acc = jnp.zeros((inner, width), F32)
-        for b in range(n):
-            acc = acc + mm(dqkv_ref[s, :, at(b)], h_ref[b])
-        qg[s] = acc.reshape(qg.shape[1:]).astype(BF16)
-        sums[s].push()
-    load.wait()
-    w[...] = w32[...].astype(BF16)
-
-    def first_block(b):
-        return sum(mm(dqkv_ref[s, :, at(b)], w[s], TN) for s in range(3))
-
-    scat.push(first_block)
-    squares = squares_ref[0:1]
-    for s in olds:
-        squares = squares + s.start()
-    whole = scat.pass_on(first_block)
-    bias_dp.start(jnp.broadcast_to(bg_ref[...], bias_dp.slots.shape[1:]))
-    pair_dp.start(pair_ref[...])
-    sums[0].near()
-    for s in olds:
-        s.second()
-    sums[1].near()
-    dh1 = scat.finish(whole)
-    dv, gain, shift = norm_back(x_ref[...].astype(F32), np_ref[0:1], dh1)
-    gi_ref[...] = dx_ref[...] + dv
-    small_mp.start(jnp.concatenate([gain, shift, mid_small_ref[0:6]], 0))
-    sums[0].far()
-    sums[2].near()
-    sums[1].far()
-    small_dp.start(small_mp.total())
-    for s in olds:
-        s.third()
-    sums[2].far()
-    for s, t in zip(sums, spreads):
-        s.collect()
-        squares = squares + t.start()
-    spreads[0].second()
+    for s in sums[pushes:early]:
+        s.push()
+    squares[...] = jnp.zeros_like(squares)
+
+    def collect(i):
+        sums[i].collect()
+        squares[...] += spreads[i].start()
+
+    def project():
+        for s in range(3):
+            flat[s] = dqkv[s].astype(F32).reshape(inner, span).astype(BF16)
+            acc = jnp.zeros((inner, width), F32)
+            for b in range(n):
+                acc = acc + mm(flat[s, :, at(b)], h_ref[b])
+            qg[s] = acc.reshape(qg.shape[1:]).astype(BF16)
+            sums[early + s].push()
+        load.wait()
+        w[...] = w32[...].astype(BF16)
+        block = lambda b: sum(mm(flat[s, :, at(b)], w[s], TN) for s in range(3))
+        scat.push(block)
+        kept[...] = scat.pass_on(block)
+        bias_dp.start(jnp.broadcast_to(bg_ref[...], bias_dp.slots.shape[1:]))
+
+    def norm():
+        dh1 = scat.finish(kept[...])
+        dv, gain, shift = norm_back(x_ref[...].astype(F32), np_ref[0:1], dh1)
+        gi_ref[...] = dx_ref[...] + dv
+        small_mp.start(jnp.concatenate([gain, shift, mid_small_ref[0:6]], 0))
+
+    jobs = {99: [project], NORM_AT: [norm], SMALL_AT: [lambda: small_dp.start(small_mp.total())]}
+    for i, s in enumerate(sums):
+        for when, job in ((NEAR_AT[i], s.near), (FAR_AT[i], s.far), (COLLECT_AT[i], functools.partial(collect, i)),
+                          (SECOND_AT[i], spreads[i].second), (THIRD_AT[i], spreads[i].third)):
+            jobs.setdefault(when, []).append(job)
+
+    def now(first, end):
+        for when in sorted(jobs):
+            if first <= when < end:
+                for job in jobs[when]:
+                    job()
+
+    def beside(step, first, end):
+        for when in sorted(jobs):
+            if first <= when < end:
+                @pl.when(step == when)
+                def _():
+                    for job in jobs[when]:
+                        job()
+
+    now(-1, 0)
+    pair = back_pairs(heads, coords_ref, qkv_ref, do_ref, p_ref, dqkv, dist, ds, beside, lambda: now(99, 100))
+    pair_dp.start(pair)
+    last = 100 + span // SUB
+    now(last, last + 4)
     bias = bias_dp.total()
     bias_ref[...] = bias
+    small = small_dp.total()
+    small_ref[...] = small
     pairs = pair_dp.total()
     pairs_ref[...] = pairs
     row = lax.broadcasted_iota(jnp.int32, (8, LANE), 0)
     local = square(bias[0:1]) + square(pairs)
-    sq_mp.start(jnp.where(row == 0, squares, jnp.where(row == 1, local, 0.0)))
-    small = small_dp.total()
-    small_ref[...] = small
-    spreads[1].second()
+    sq_mp.start(jnp.where(row == 0, squares[...], jnp.where(row == 1, local, 0.0)))
+    now(last + 4, 1000)
     sq_dp.start(sq_mp.total())
-    spreads[2].second()
+    norm_ref[...] = sq_dp.total()[0:1] + sq_dp.slots[0, 1:2] + square(small)
     for s in spreads:
-        s.third()
-    norm_ref[...] = sq_dp.total()[0:1] + sq_dp.slots[0, 1:2] + square(small)
-    for s in olds + spreads:
         s.close()
     for s in [scat] + sums + shares:
         s.drain()
 
 
-def leave(n, ny, nz, x, dx, params, dqkv, h, bias_grad, pair_grad, squares, small, owns, qkv_weight):
+def rear(n, ny, nz, qkv, do, probs, coords, og, ig, pg, lands, x, dx, params, h, bias_grad, small, qkv_weight):
+    _, heads, hd, span = qkv.shape
     rows, width = x.shape
-    inner = qkv_weight.shape[1]
-    ndp = ny * nz
-    hidden = bias_grad.shape[1]
+    inner, hidden = heads * hd, bias_grad.shape[1]
+    ndp, pushes = ny * nz, len(lands)
+    cut = lambda g, p: g.reshape(p, ny, 2, nz // 2, g.shape[0] // (p * ndp), width)
+    lands = [v.reshape(ny - 1, 2, nz // 2, -1, width) for v in lands]
+    og, ig, pg = cut(og, PARTS), cut(ig, PARTS), cut(pg, 1)[0]
     chunks = (3, ny, 2, nz // 2, inner // ndp, width)
+    shapes = [og.shape[1:]] * PARTS + [ig.shape[1:]] * PARTS + [pg.shape]
+    every = shapes + [chunks[1:]] * 3
     f = lambda *s: jax.ShapeDtypeStruct(s, F32)
-    late = len(owns)
     return pl.pallas_call(
-        functools.partial(leave_kernel, n, ny, nz, late),
-        out_shape=(f(rows, width), *[jax.ShapeDtypeStruct((ny, 2, nz // 2, *o.shape), BF16) for o in owns],
-                   jax.ShapeDtypeStruct(chunks, BF16), f(8, width), f(8, hidden), f(8, LANE), f(1, LANE)),
-        in_specs=[VM] * (9 + late) + [HBM], out_specs=[VM] * (6 + late),
-        scratch_shapes=[pltpu.VMEM(qkv_weight.shape, F32), pltpu.VMEM(qkv_weight.shape, BF16),
-                        pltpu.VMEM(chunks, BF16), pltpu.VMEM((3, inner // ndp, width), F32), DMA,
+        functools.partial(rear_kernel, n, ny, nz, pushes),
+        out_shape=(*[jax.ShapeDtypeStruct(s, BF16) for s in (*shapes, chunks)],
+                   f(rows, width), f(8, width), f(8, hidden), f(8, LANE), f(1, LANE)),
+        in_specs=[VM] * 13 + [HBM] + [VM] * pushes, out_specs=[VM] * (len(shapes) + 6),
+        scratch_shapes=[pltpu.VMEM((span, span), F32), pltpu.VMEM((span // LANE, SUB * span, LANE), F32),
+                        pltpu.VMEM(qkv.shape, BF16), pltpu.VMEM((3, inner, span), BF16),
+                        pltpu.VMEM(qkv_weight.shape, F32), pltpu.VMEM(qkv_weight.shape, BF16), pltpu.VMEM(chunks, BF16),
+                        pltpu.VMEM((3, inner // ndp, width), F32), pltpu.VMEM((rows, width), F32),
+                        pltpu.VMEM((1, LANE), F32), DMA, *[pltpu.VMEM(s[3:], F32) for s in shapes],
                         *scatter_scratch(n, rows, width),
-                        *[s for _ in range(3) for s in sum_scratch(chunks[1:])],
-                        *[s for _ in range(3 + late) for s in spread_scratch(ny, nz)],
+                        *[v for s in every for v in sum_scratch(s)], *[v for _ in every for v in spread_scratch(ny, nz)],
                         *share_scratch(n, 8, width), *share_scratch(ndp, 8, width), *share_scratch(ndp, 8, hidden),
                         *share_scratch(ndp, 8, LANE), *share_scratch(n, 8, LANE), *share_scratch(ndp, 8, LANE)],
-        compiler_params=pltpu.CompilerParams(collective_id=2, has_side_effects=True, vmem_limit_bytes=LEAVE_MIB << 20),
-        name="leave",
-    )(x, dx, params, dqkv, h, bias_grad, pair_grad, squares, small, *owns, qkv_weight)
+        compiler_params=pltpu.CompilerParams(collective_id=2, has_side_effects=True, vmem_limit_bytes=REAR_MIB << 20),
+        name="rear",
+    )(coords, qkv, do, probs, og, ig, pg, x, dx, params, h, bias_grad, small, qkv_weight, *lands)
 
 
 def leave_plain(n, x, dx, params, dqkv, h, grads, bias_grad, pair_grad, small, qkv_weight):
@@ -863,97 +900,6 @@
     local = sum(square(v) for v in (og, ig, pg, qg, bias, pair))
     total = lax.psum(local, "mp") + square(small)
     return dx + dv, og, ig, pg, qg, small, bias, pair, total
-
-
-NEAR_AT = (0, 0, 6, 14, 20)
-FAR_AT = (4, 7, 16, 26, 32)
-COLLECT_AT = (10, 15, 28, 38, 42)
-SECOND_AT = (18, 24, 36, 48, 52)
-THIRD_AT = (26, 33, 46, 60, 64)
-FIRST = 1
-EARLY = 5
-BACK_MIB = 24
-LEAVE_MIB = 16
-
-
-def back_kernel(heads, ny, nz, parts, pushes, coords_ref, qkv_ref, do_ref, p_ref, og_ref, ig_ref, pg_ref, *rest):
-    lands, (dqkv_ref, pair_ref, squares_ref), rest = rest[:pushes], rest[pushes:pushes + 3], rest[pushes + 3:]
-    owns, rest = rest[:2 * parts + 1 - EARLY], rest[2 * parts + 1 - EARLY:]
-    results, (dist, ds), rest = rest[:EARLY], rest[EARLY:EARLY + 2], rest[EARLY + 2:]
-    early, rest = rest[:EARLY], rest[EARLY:]
-    hd, span = do_ref.shape[1:]
-    grid = Grid(ny, nz)
-    pieces = [g.at[i] for g in (og_ref, ig_ref) for i in range(parts)] + [pg_ref]
-    places = [*early, *owns]
-    scratch, rest = take(rest, Sum, len(pieces))
-    sums = [Sum(grid, *a) for a in zip(pieces, places, scratch)]
-    scratch, rest = take(rest, Spread, EARLY)
-    spreads = [Spread(grid, *a) for a in zip(places, results, scratch)]
-    for s, land in zip(sums, lands):
-        s.ia, s.pushed = land, False
-    greet({"dp": ny * nz})
-    for s in sums[pushes:]:
-        s.push()
-    for s in sums[:FIRST]:
-        s.near()
-    squares_ref[...] = jnp.zeros_like(squares_ref)
-
-    def collect(i):
-        sums[i].collect()
-        if i < EARLY:
-            squares_ref[...] += spreads[i].start()
-
-    jobs = {}
-    for i, s in enumerate(sums):
-        if i >= FIRST:
-            jobs.setdefault(NEAR_AT[i], []).append(s.near)
-        jobs.setdefault(FAR_AT[i], []).append(s.far)
-        jobs.setdefault(COLLECT_AT[i], []).append(functools.partial(collect, i))
-    for i, s in enumerate(spreads):
-        jobs.setdefault(SECOND_AT[i], []).append(s.second)
-        jobs.setdefault(THIRD_AT[i], []).append(s.third)
-    last = heads + span // SUB
-
-    def beside(step, first, end):
-        for when in sorted(jobs):
-            if first <= when < end:
-                @pl.when(step == when)
-                def _():
-                    for job in jobs[when]:
-                        job()
-
-    pair_ref[...] = back_pairs(heads, coords_ref, qkv_ref, do_ref, p_ref, dqkv_ref, dist, ds, beside)
-    for when in sorted(jobs):
-        if when >= last:
-            for job in jobs[when]:
-                job()
-    for s in spreads:
-        s.close()
-    for s in sums:
-        s.drain()
-
-
-def attention_back_sums(qkv, do, probs, coords, ny, nz, og, ig, pg, lands):
-    _, heads, hd, span = qkv.shape
-    width = og.shape[1]
-    ndp, parts, pushes = ny * nz, PARTS, len(lands)
-    lands = [v.reshape(ny - 1, 2, nz // 2, -1, width) for v in lands]
-    cut = lambda g, p: g.reshape(p, ny, 2, nz // 2, g.shape[0] // (p * ndp), width)
-    og, ig, pg = cut(og, parts), cut(ig, parts), cut(pg, 1)[0]
-    shapes = [og.shape[1:]] * parts + [ig.shape[1:]] * parts + [pg.shape]
-    f = lambda *s: jax.ShapeDtypeStruct(s, F32)
-    return pl.pallas_call(
-        functools.partial(back_kernel, heads, ny, nz, parts, pushes),
-        out_shape=(jax.ShapeDtypeStruct(qkv.shape, BF16), f(SUB, KERN), f(SUB, LANE),
-                   *[f(*s[3:]) for s in shapes[EARLY:]], *[jax.ShapeDtypeStruct(s, BF16) for s in shapes[:EARLY]]),
-        in_specs=[VM] * (7 + pushes), out_specs=[VM] * (3 + len(shapes)),
-        scratch_shapes=[pltpu.VMEM((span, span), F32), pltpu.VMEM((span // LANE, SUB * span, LANE), F32),
-                        *[pltpu.VMEM(shape[3:], F32) for shape in shapes[:EARLY]],
-                        *[s for shape in shapes for s in sum_scratch(shape)],
-                        *[s for _ in range(EARLY) for s in spread_scratch(ny, nz)]],
-        compiler_params=pltpu.CompilerParams(collective_id=3, has_side_effects=True, vmem_limit_bytes=BACK_MIB << 20),
-        name="attend_back_sums",
-    )(coords, qkv, do, probs, og, ig, pg, *lands)
 
 
 PUSHES = 2
@@ -983,12 +929,9 @@
     block_out, dx, do, og, ig, pg, bg, small, *lands = middle(
         n, ny, nz, PUSHES if beside else 0, block_in, dys, o, params, in_bias.reshape(1, -1), proj_weight, in_weight, out_weight)
     if beside:
-        dqkv, pair_grad, squares, *parts = attention_back_sums(qkv, do, probs, coords, ny, nz, og, ig, pg, lands)
-        owns, done = parts[:-EARLY], parts[-EARLY:]
-        grad_input, *sums, qg, small, bias, pair, total = leave(
-            n, ny, nz, block_in, dx, params, dqkv.reshape(3, inner, -1), h, bg, pair_grad, squares, small, owns, qkv_weight)
-        *pieces, pg = *done, *sums
-        og, ig = pieces[:len(pieces) // 2], pieces[len(pieces) // 2:]
+        *pieces, pg, qg, grad_input, small, bias, pair, total = rear(
+            n, ny, nz, qkv, do, probs, coords, og, ig, pg, lands, block_in, dx, params, h, bg, small, qkv_weight)
+        og, ig = pieces[:PARTS], pieces[PARTS:]
         og, ig = [jnp.concatenate([v.reshape(-1, v.shape[-1]) for v in g], 0) for g in (og, ig)]
     else:
         dqkv, pair_grad = attention_back(qkv, do, probs, coords)

time: 212 us -> 196 us (0.925)
  Pallas kernels: 185 us -> 170 us
    pallas_call x2 -> x1, Pallas kernels: 102 us -> 86.6 us  [rear(): pl.pallas_call(functools.partial(rear_kernel, n, ny, nz, pushes), out_sha...]
  transfers between devices with their start and end apart: 3 -> 3, of which waited for: 0 -> 0; matrix products, arithmetic and copies ran while one was open for 1% -> 1% of each run, Pallas kernels for 14% -> 15%
where the time goes in v5:
time: 196 us
  Pallas kernels  170 us (87%)
  other arithmetic  14 us (7%)
  local copies, waits for them, and re-layouts  7.32 us (4%)
  between operations  2.98 us (2%)
  starting transfers between devices  2.26 us (1%)
    pallas_call x1, Pallas kernels, rear(): pl.pallas_call(functools.partial(rear_kernel, n, ny, nz, pushes), out_sha...  86.6 us
    pallas_call x1, Pallas kernels, middle(): pl.pallas_call(functools.partial(middle_kernel, n, ny, nz, pushes), out_s...  39.4 us
    pallas_call x1, Pallas kernels, attention(): pl.pallas_call(functools.partial(fwd_kernel, heads, mols), out_shape=(jax...  28.7 us
    pallas_call x1, Pallas kernels, enter(): pl.pallas_call(functools.partial(enter_kernel, n), out_shape=(jax.ShapeDt...  14.7 us
    sub x6, other arithmetic, adam_step(): return (weight - rate * (ratio + decay * weight), first_new, second_new)  13 us
    unnamed x60, local copies, waits for them, and re-layouts  6.63 us
  transfers between devices with their start and end apart: 3, of which 0 were waited for; matrix products, arithmetic and copies ran while one was open for 1% of the time, Pallas kernels for 15%

profile of v5, /device:TPU:0, one launch (start us, length us, event | category | flops | bytes accessed | tf_op | source)
XLA Modules:
  0.0 196.1 jit_solution(2858350230058710076)
XLA Ops:
  0.7 14.7 %enter.1 = (bf16[4,128,768]{2,1,0:T(8,128)(2,1)}, bf16[3,8,24,512]{3,2,1,0:T(8,128)(2,1)}) custom-call(bf16[128,768]{1,0:T(8,128)(2,1)} %x_ref.5, f32[5,768]{1,0:T(8,128)} %np_ref.5, f32[3,192,768]{2,1,0:T(8,128)} %w_hbm.3), custom_call_target="tpu_custom_call" | custom-call | tf_op jit(solution)/shard_map/enter/pallas_call | solution.py:424
  15.4 1.9 collective-permute-start
  17.3 0.4 collective-permute-start.1
  17.7 0.0 collective-permute-start.2
  17.7 0.7 convert_element_type.21.w_ref
  18.4 0.7 reshape.107.bias_ref
  19.8 0.0 copy-start.6
  19.8 1.1 copy-done.6
  20.8 0.7 copy-done.10
  21.5 0.7 copy-done.12
  22.2 0.0 copy-start.8
  22.2 0.0 copy-start.9
  22.2 28.7 %attend.1 = (bf16[8,24,512]{2,1,0:T(8,128)(2,1)S(1)}, bf16[4096,512]{1,0:T(8,128)(2,1)S(1)}) custom-call(s32[1,16]{1,0:T(1,128)S(1)} %copy-done.12, f32[3,512]{1,0:T(4,128)S(1)} %copy-done.10, bf16[3,8,24,512]{3,2,1,0:T(8,128)(2,1)S(1)} %copy-done.6, bf16[8,128]{1,0:T(8,128)(2,1)S(1)} %convert_element_type.21.w_ref), custom_call_target="tpu_custom_call" | custom-call | flops 1006632960 | bytes 2097152 | tf_op jit(solution)/shard_map/attend/pallas_call | solution.py:139
  51.0 0.0 collective-permute-done.rest_1_
  51.0 0.0 collective-permute-done.1.rest_2_
  51.0 0.0 collective-permute-done.2.rest_3_
  51.0 0.0 copy-done.1
  51.0 0.0 copy-done.2
  51.0 0.0 copy-done.3
  51.0 0.0 copy-done.4
  51.1 0.0 copy-done.8
  51.1 0.0 copy-done.9
  51.1 0.0 copy-start
  51.1 0.0 copy-start.5
  51.1 0.0 copy-start.7
  51.1 0.0 copy-start.11
  51.1 39.4 %middle.1 = (f32[128,768]{1,0:T(8,128)S(1)}, f32[128,768]{1,0:T(8,128)S(1)}, bf16[8,24,512]{2,1,0:T(8,128)(2,1)S(1)}, bf16[768,768]{1,0:T(8,128)(2,1)S(1)}, bf16...) custom-call(bf16[128,768]{1,0:T(8,128)(2,1)S(1)} %copy-done.4, ...), custom_call_target="tpu_custom_call" | custom-call | tf_op jit(solution)/shard_map/middle/pallas_call | solution.py:560
  90.5 0.0 copy-done
  90.5 0.0 copy-done.5
  90.5 0.0 copy-done.7
  90.5 0.0 copy-done.11
  90.6 86.6 %rear.1 = (bf16[2,2,2,48,768]{4,3,2,1,0:T(8,128)(2,1)S(1)}, bf16[2,2,2,48,768]{4,3,2,1,0:T(8,128)(2,1)S(1)}, bf16[2,2,2,48,768]{4,3,2,1,0:T(8,128)(2,1)S(1)}, bf...) custom-call(f32[3,512]{1,0:T(4,128)S(1)} %copy-done.11, ...), custom_call_target="tpu_custom_call" | custom-call | tf_op jit(solution)/shard_map/rear/pallas_call | solution.py:873
  177.2 0.0 copy-start.21
  177.2 0.0 copy-start.22
  177.2 0.0 copy-start.23
  177.3 0.0 copy-start.25
  177.3 0.0 copy-start.26
  177.3 0.0 copy-start.24
  177.3 0.0 copy-start.27
  177.3 0.0 copy-start.28
  177.3 0.0 copy-start.19
  177.3 0.0 copy-start.20
  177.5 0.2 convert_multiply_fusion.2
  177.7 0.0 copy-start.17
  177.7 0.0 copy-start.18
  177.8 0.2 copy-done.21
  178.0 0.0 copy-done.22
  178.0 0.6 multiply_subtract_fusion.4
  178.6 0.0 copy-done.23
  178.6 0.0 copy-done.25
  178.6 0.0 copy-done.26
  178.6 0.6 multiply_subtract_fusion.5
  179.2 0.0 copy-done.24
  179.3 0.6 multiply_subtract_fusion.6
  179.9 1.5 multiply_subtract_fusion.3
  181.4 0.0 copy-start.15
  181.4 0.0 copy-start.16
  181.4 3.3 %multiply_subtract_fusion.2 = (f32[3,192,768]{2,1,0:T(8,128)}, f32[3,192,768]{2,1,0:T(8,128)}, f32[3,192,768]{2,1,0:T(8,128)}) fusion(f32[3,192,768]{2,1,0:T(8,128)S(1)} %copy-done, f32[]{:T(128)} %bitcast.10, f32[]{:T(128)} %bitcast.9, f32[3,2,2,2,24,768]{5,4,3,2,1,0:T(8,128)S(1)} %convert_multiply_fusion.2, f32[3,192,768]{2,1,0:T(8,128)S(1)} %copy-done.17, ...), kind=kLoop, calls=%fused_computation.14 | loop fusion | flops 6635520 | bytes 12386312 | tf_op jit(solution)/shard_map/sub | solution.py:913
  184.7 1.0 copy-done.14
  185.7 0.7 copy-done.15
  186.4 0.7 copy-done.16
  187.1 6.4 %multiply_subtract_fusion = (f32[768,768]{1,0:T(8,128)}, f32[768,768]{1,0:T(8,128)}, f32[768,768]{1,0:T(8,128)}, f32[768,768]{1,0:T(8,128)}, f32[768,768]{1,0:T(8,128)}, /*index=5*/f32[768,768]{1,0:T(8,128)}) fusion(f32[768,768]{1,0:T(8,128)S(1)} %copy-done.2, f32[]{:T(128)} %bitcast.10, f32[]{:T(128)} %bitcast.9, f32[]{:T(128)} %bitcast.7, ...), kind=kLoop, calls=%fused_computation.5 | loop fusion | flops 23592960 | bytes 30670860 | tf_op jit(solution)/shard_map/sub | solution.py:913
  193.4 0.7 copy.53
  194.2 0.7 copy.54
  (17 shorter events, 0.1 us)
Async XLA Ops:
  15.4 35.6 %collective-permute-start = (bf16[128,768]{1,0:T(8,128)(2,1)}, bf16[128,768]{1,0:T(8,128)(2,1)S(1)}, u32[]{:S(2)}, u32[]{:S(2)}) collective-permute-start(bf16[128,768]{1,0:T(8,128)(2,1)} %rest_0_.1), channel_id=1, source_target_pairs={{1,0},{2,1},{3,2},{0,3},{5,4},{6,5},{7,6},{4,7},{9,8},{10,9},{11,1... | collective-permute-start | bytes 589832 | tf_op jit(solution)/shard_map/ppermute | solution.py:924
  17.3 33.7 %collective-permute-start.1 = (bf16[128,768]{1,0:T(8,128)(2,1)}, bf16[128,768]{1,0:T(8,128)(2,1)S(1)}, u32[]{:S(2)}, u32[]{:S(2)}) collective-permute-start(bf16[128,768]{1,0:T(8,128)(2,1)} %rest_0_.1), channel_id=1, source_target_pairs={{2,0},{3,1},{0,2},{1,3},{6,4},{7,5},{4,6},{5,7},{10,8},{11,9},{8,1... | collective-permute-start | bytes 589832 | tf_op jit(solution)/shard_map/ppermute | solution.py:924
  17.7 33.3 %collective-permute-start.2 = (bf16[128,768]{1,0:T(8,128)(2,1)}, bf16[128,768]{1,0:T(8,128)(2,1)S(1)}, u32[]{:S(2)}, u32[]{:S(2)}) collective-permute-start(bf16[128,768]{1,0:T(8,128)(2,1)} %rest_0_.1), channel_id=1, source_target_pairs={{3,0},{0,1},{1,2},{2,3},{7,4},{4,5},{5,6},{6,7},{11,8},{8,9},{9,10... | collective-permute-start | bytes 589832 | tf_op jit(solution)/shard_map/ppermute | solution.py:924
  19.8 1.1 copy-start.6
  20.8 0.7 copy-start.10
  21.5 0.7 copy-start.12
  22.2 28.8 %copy-start.1 = (f32[768,768]{1,0:T(8,128)S(1)}, f32[768,768]{1,0:T(8,128)}, u32[]{:S(2)}) copy-start(f32[768,768]{1,0:T(8,128)} %iw_hbm.1) | copy-start | bytes 7077892
  22.2 28.8 %copy-start.2 = (f32[768,768]{1,0:T(8,128)S(1)}, f32[768,768]{1,0:T(8,128)}, u32[]{:S(2)}) copy-start(f32[768,768]{1,0:T(8,128)} %ow_hbm.1) | copy-start | bytes 7077892
  22.2 28.8 %copy-start.3 = (f32[192,768]{1,0:T(8,128)S(1)}, f32[192,768]{1,0:T(8,128)}, u32[]{:S(2)}) copy-start(f32[192,768]{1,0:T(8,128)} %pw_hbm.1) | copy-start | bytes 1769476
  22.2 28.8 %copy-start.4 = (bf16[128,768]{1,0:T(8,128)(2,1)S(1)}, bf16[128,768]{1,0:T(8,128)(2,1)}, u32[]{:S(2)}) copy-start(bf16[128,768]{1,0:T(8,128)(2,1)} %x_ref.5) | copy-start | bytes 589828
  22.2 28.8 %copy-start.8 = (f32[5,768]{1,0:T(8,128)S(1)}, f32[5,768]{1,0:T(8,128)}, u32[]{:S(2)}) copy-start(f32[5,768]{1,0:T(8,128)} %np_ref.5) | copy-start | bytes 46084
  22.2 28.8 %copy-start.9 = (bf16[128,768]{1,0:T(8,128)(2,1)S(1)}, bf16[128,768]{1,0:T(8,128)(2,1)}, u32[]{:S(2)}) copy-start(bf16[128,768]{1,0:T(8,128)(2,1)} %rest_0_.1) | copy-start | bytes 589828
  51.1 39.5 %copy-start = (f32[3,192,768]{2,1,0:T(8,128)S(1)}, f32[3,192,768]{2,1,0:T(8,128)}, u32[]{:S(2)}) copy-start(f32[3,192,768]{2,1,0:T(8,128)} %w_hbm.3) | copy-start | bytes 5308420
  51.1 39.4 %copy-start.5 = (bf16[4,128,768]{2,1,0:T(8,128)(2,1)S(1)}, bf16[4,128,768]{2,1,0:T(8,128)(2,1)}, u32[]{:S(2)}) copy-start(bf16[4,128,768]{2,1,0:T(8,128)(2,1)} %get-tuple-element.60.h_ref) | copy-start | bytes 2359300
  51.1 39.4 %copy-start.7 = (bf16[3,8,24,512]{3,2,1,0:T(8,128)(2,1)S(1)}, bf16[3,8,24,512]{3,2,1,0:T(8,128)(2,1)}, u32[]{:S(2)}) copy-start(bf16[3,8,24,512]{3,2,1,0:T(8,128)(2,1)} %get-tuple-element.50.qkv_ref) | copy-start | bytes 1769476
  51.1 39.4 %copy-start.11 = (f32[3,512]{1,0:T(4,128)S(1)}, f32[3,512]{1,0:T(4,128)}, u32[]{:S(2)}) copy-start(f32[3,512]{1,0:T(4,128)} %coords_ref.3) | copy-start | bytes 18436
  177.2 0.7 copy-start.21
  177.2 0.7 copy-start.22
  177.2 1.4 copy-start.23
  177.3 1.4 copy-start.25
  177.3 1.4 copy-start.26
  177.3 2.0 %copy-start.24 = (f32[8,128]{1,0:T(8,128)S(1)}, f32[8,128]{1,0:T(8,128)}, u32[]{:S(2)}) copy-start(f32[8,128]{1,0:T(8,128)} %param.33) | copy-start | bytes 12292
  177.3 2.0 %copy-start.27 = (f32[8,128]{1,0:T(8,128)S(1)}, f32[8,128]{1,0:T(8,128)}, u32[]{:S(2)}) copy-start(f32[8,128]{1,0:T(8,128)} %param.47) | copy-start | bytes 12292
  177.3 2.0 copy-start.28
  177.3 2.6 %copy-start.19 = (f32[192,768]{1,0:T(8,128)S(1)}, f32[192,768]{1,0:T(8,128)}, u32[]{:S(2)}) copy-start(f32[192,768]{1,0:T(8,128)} %param.46) | copy-start | bytes 1769476
  177.3 2.6 %copy-start.20 = (f32[192,768]{1,0:T(8,128)S(1)}, f32[192,768]{1,0:T(8,128)}, u32[]{:S(2)}) copy-start(f32[192,768]{1,0:T(8,128)} %param.39) | copy-start | bytes 1769476
  177.7 3.6 %copy-start.17 = (f32[3,192,768]{2,1,0:T(8,128)S(1)}, f32[3,192,768]{2,1,0:T(8,128)}, u32[]{:S(2)}) copy-start(f32[3,192,768]{2,1,0:T(8,128)} %param.45) | copy-start | bytes 5308420
  177.7 3.6 %copy-start.18 = (f32[3,192,768]{2,1,0:T(8,128)S(1)}, f32[3,192,768]{2,1,0:T(8,128)}, u32[]{:S(2)}) copy-start(f32[3,192,768]{2,1,0:T(8,128)} %param.38) | copy-start | bytes 5308420
  181.4 3.3 %copy-start.13 = (f32[768,768]{1,0:T(8,128)S(1)}, f32[768,768]{1,0:T(8,128)}, u32[]{:S(2)}) copy-start(f32[768,768]{1,0:T(8,128)} %param.50) | copy-start | bytes 7077892
  181.4 4.3 %copy-start.14 = (f32[768,768]{1,0:T(8,128)S(1)}, f32[768,768]{1,0:T(8,128)}, u32[]{:S(2)}) copy-start(f32[768,768]{1,0:T(8,128)} %param.43) | copy-start | bytes 7077892
  181.4 5.0 %copy-start.15 = (f32[768,768]{1,0:T(8,128)S(1)}, f32[768,768]{1,0:T(8,128)}, u32[]{:S(2)}) copy-start(f32[768,768]{1,0:T(8,128)} %param.48) | copy-start | bytes 7077892
  181.4 5.7 %copy-start.16 = (f32[768,768]{1,0:T(8,128)S(1)}, f32[768,768]{1,0:T(8,128)}, u32[]{:S(2)}) copy-start(f32[768,768]{1,0:T(8,128)} %param.41) | copy-start | bytes 7077892

commit v6 on v5

--- a/solution.py
+++ b/solution.py
@@ -87,7 +87,7 @@
     scale = 1.0 / math.sqrt(hd)
     pair_distances(coords_ref, dist, span)
     pair_labels(len_ref, b, labs, labr, span, mols)
-    wb = w_ref[...]
+    wb = w_ref[...].astype(BF16)
     step = LANE
 
     def fill(i, carry):
@@ -131,11 +131,11 @@
     lax.fori_loop(0, heads, head, 0)
 
 
-def attention(qkv, coords, lengths, pair_low):
+def attention(qkv, coords, lengths, pair_weight):
     _, heads, hd, rows = qkv.shape
     blocks, mols = lengths.shape
     span = rows // blocks
-    w = jnp.pad(pair_low, ((0, SUB - heads), (0, 0)))
+    w = jnp.pad(pair_weight, ((0, SUB - heads), (0, 0))) if heads < SUB else pair_weight
     return pl.pallas_call(
         functools.partial(fwd_kernel, heads, mols),
         out_shape=(jax.ShapeDtypeStruct((heads, hd, rows), BF16),
@@ -310,14 +310,19 @@
         target = self.seat.chip(k) * 2 + self.seat.core
         return remote(self.out2.at[k], self.in2.at[k], self.s2.at[k], self.r2.at[k], "mp", target)
 
+    def push_one(self, k, block):
+        self.out1[k] = block(self.seat.chip(k) * 2 + 1 - self.seat.core).astype(BF16)
+        self.first(k).start()
+
     def push(self, block):
         for k in range(self.seat.nx):
-            self.out1[k] = block(self.seat.chip(k) * 2 + 1 - self.seat.core).astype(BF16)
-            self.first(k).start()
-
-    def pass_on(self, block):
+            self.push_one(k, block)
+
+    def pass_on(self, block, own=None):
         seat = self.seat
-        parts = [block(seat.chip(k) * 2 + seat.core) for k in range(seat.nx)]
+        parts = [block(seat.chip(k) * 2 + seat.core) for k in range(seat.nx - (own is not None))]
+        if own is not None:
+            parts.append(own[...])
         for k in range(seat.nx):
             self.first(k).wait_recv()
             whole = parts[k] + self.in1[k].astype(F32)
@@ -368,8 +373,11 @@
             self.across(k).wait_recv()
             self.along(k).start()
 
-    def finish(self):
-        for k in range(self.seat.nx):
+    def sibling(self):
+        self.along(self.seat.nx - 1).wait_recv()
+
+    def finish(self, sibling=True):
+        for k in range(self.seat.nx - (not sibling)):
             self.along(k).wait_recv()
 
     def drain(self):
@@ -436,7 +444,7 @@
     dys, rest = rest[:n], rest[n:]
     (block_ref, mid_ref, do_ref, og_ref, ig_ref, pg_ref, bg_ref, small_ref), rest = rest[:8], rest[8:]
     lands, rest = rest[:pushes], rest[pushes:]
-    (pw32, iw32, ow32, pw, iw, ow, h2, da, act, dpre, dact, dyall_ref, wsem), rest = rest[:13], rest[13:]
+    (pw32, iw32, ow32, pw, iw, ow, h2, da, act, dpre, dact, dyall_ref, kept, wsem), rest = rest[:14], rest[14:]
     seat, grid = Seat(n), Grid(ny, nz)
     dy_ref = dys[0]
     rows, width = x_ref.shape
@@ -481,9 +489,6 @@
     h2[seat.me] = (vhat * np_ref[2:3] + np_ref[3:4]).astype(BF16)
     mid_ref[...] = mid
     gath[0].start()
-    gath[0].forward()
-    gath[0].finish()
-
     bg_ref[...] = jnp.zeros_like(bg_ref)
     bias = bias_ref[...].astype(BF16).astype(F32)
 
@@ -497,8 +502,15 @@
         bg_ref[...] += jnp.sum(d.astype(F32), axis=0, keepdims=True)
         return mm(d, iw[...])
 
-    scat[1].push(feed_block)
-    whole = scat[1].pass_on(feed_block)
+    last = seat.nx - 1
+    kept[...] = feed_block(seat.me)
+    gath[0].sibling()
+    scat[1].push_one(last, feed_block)
+    gath[0].forward()
+    gath[0].finish(sibling=False)
+    for k in range(last):
+        scat[1].push_one(k, feed_block)
+    whole = scat[1].pass_on(feed_block, kept)
     hidden = iw.shape[0]
     step = LANE if hidden % LANE == 0 else hidden
 
@@ -568,7 +580,7 @@
                         pltpu.VMEM((hidden, width), BF16), pltpu.VMEM((hidden, width), BF16),
                         pltpu.VMEM((n, rows, width), BF16), pltpu.VMEM((n, rows, width), BF16),
                         pltpu.VMEM((n, rows, hidden), BF16), pltpu.VMEM((n, rows, hidden), BF16),
-                        pltpu.VMEM((n, rows, hidden), F32), pltpu.VMEM((n, rows, width), BF16), DMA((3,)),
+                        pltpu.VMEM((n, rows, hidden), F32), pltpu.VMEM((n, rows, width), BF16), pltpu.VMEM((rows, width), F32), DMA((3,)),
                         *[s for _ in range(3) for s in scatter_scratch(n, rows, width)],
                         *gather_scratch(n), *gather_scratch(n),
                         *[DMA((max(pushes, 1), max(ny - 1, 1)))] * 2],
@@ -778,8 +790,8 @@
     sums = [Sum(grid, *a) for a in zip(pieces, places, scratch)]
     scratch, rest = take(rest, Spread, early + 3)
     spreads = [Spread(grid, *a) for a in zip(places, targets, scratch)]
-    shares = [Share(a, *rest[3 * i:3 * i + 3]) for i, a in enumerate(("mp", "dp", "dp", "dp", "mp", "dp"))]
-    small_mp, small_dp, bias_dp, pair_dp, sq_mp, sq_dp = shares
+    shares = [Share(a, *rest[3 * i:3 * i + 3]) for i, a in enumerate(("mp", "dp", "dp", "dp", "mp", "dp", "mp"))]
+    small_mp, small_dp, bias_dp, pair_dp, sq_mp, sq_dp, local_mp = shares
     for s, land in zip(sums, lands):
         s.ia, s.pushed = land, False
     at = lambda b: pl.ds(pl.multiple_of(b * rows, rows), rows)
@@ -840,18 +852,17 @@
     pair_dp.start(pair)
     last = 100 + span // SUB
     now(last, last + 4)
+    sq_mp.start(jnp.broadcast_to(squares[...], (8, LANE)))
+    now(last + 4, 1000)
     bias = bias_dp.total()
     bias_ref[...] = bias
+    pairs = pair_dp.total()
+    pairs_ref[...] = pairs
+    local_mp.start(jnp.broadcast_to(square(bias[0:1]) + square(pairs), (8, LANE)))
+    sq_dp.start(sq_mp.total())
     small = small_dp.total()
     small_ref[...] = small
-    pairs = pair_dp.total()
-    pairs_ref[...] = pairs
-    row = lax.broadcasted_iota(jnp.int32, (8, LANE), 0)
-    local = square(bias[0:1]) + square(pairs)
-    sq_mp.start(jnp.where(row == 0, squares[...], jnp.where(row == 1, local, 0.0)))
-    now(last + 4, 1000)
-    sq_dp.start(sq_mp.total())
-    norm_ref[...] = sq_dp.total()[0:1] + sq_dp.slots[0, 1:2] + square(small)
+    norm_ref[...] = sq_dp.total()[0:1] + local_mp.total()[0:1] + square(small)
     for s in spreads:
         s.close()
     for s in [scat] + sums + shares:
@@ -883,7 +894,8 @@
                         *scatter_scratch(n, rows, width),
                         *[v for s in every for v in sum_scratch(s)], *[v for _ in every for v in spread_scratch(ny, nz)],
                         *share_scratch(n, 8, width), *share_scratch(ndp, 8, width), *share_scratch(ndp, 8, hidden),
-                        *share_scratch(ndp, 8, LANE), *share_scratch(n, 8, LANE), *share_scratch(ndp, 8, LANE)],
+                        *share_scratch(ndp, 8, LANE), *share_scratch(n, 8, LANE), *share_scratch(ndp, 8, LANE),
+                        *share_scratch(n, 8, LANE)],
         compiler_params=pltpu.CompilerParams(collective_id=2, has_side_effects=True, vmem_limit_bytes=REAR_MIB << 20),
         name="rear",
     )(coords, qkv, do, probs, og, ig, pg, x, dx, params, h, bias_grad, small, qkv_weight, *lands)
@@ -917,9 +929,8 @@
     weights, firsts, seconds = state[:7], state[7:14], state[14:]
     qkv_weight, proj_weight, pair_weight, in_weight, in_bias, out_weight, params = weights
     heads = pair_weight.shape[0]
-    pair_low = pair_weight.astype(BF16)
     h, qkv = enter(n, heads, block_in, params, qkv_weight)
-    o, probs = attention(qkv, coords, lengths, pair_low)
+    o, probs = attention(qkv, coords, lengths, pair_weight)
     dy, _ = lax.optimization_barrier((cotangent, qkv))
     dys = [cotangent] + [lax.ppermute(dy, "mp", [((i + k) % n, i) for i in range(n)]) for k in range(1, n)]
     ny = n // 2 if ndp % (n // 2) == 0 else 1

time: 196 us -> 194 us (0.990)
  Pallas kernels: 170 us -> 168 us
    pallas_call x1, Pallas kernels: 39.4 us -> 37.1 us  [middle(): pl.pallas_call(functools.partial(middle_kernel, n, ny, nz, pushes), out_s...]
    unnamed x60 -> x62, local copies, waits for them, and re-layouts: 6.63 us -> 7.32 us
  transfers between devices with their start and end apart: 3 -> 3, of which waited for: 0 -> 0; matrix products, arithmetic and copies ran while one was open for 1% -> 0% of each run, Pallas kernels for 15% -> 15%
where the time goes in v6:
time: 194 us
  Pallas kernels  168 us (87%)
  other arithmetic  13.3 us (7%)
  local copies, waits for them, and re-layouts  8.01 us (4%)
  between operations  2.98 us (2%)
  starting transfers between devices  2.26 us (1%)
    pallas_call x1, Pallas kernels, rear(): pl.pallas_call(functools.partial(rear_kernel, n, ny, nz, pushes), out_sha...  86.6 us
    pallas_call x1, Pallas kernels, middle(): pl.pallas_call(functools.partial(middle_kernel, n, ny, nz, pushes), out_s...  37.1 us
    pallas_call x1, Pallas kernels, attention(): pl.pallas_call(functools.partial(fwd_kernel, heads, mols), out_shape=(jax...  29.2 us
    pallas_call x1, Pallas kernels, enter(): pl.pallas_call(functools.partial(enter_kernel, n), out_shape=(jax.ShapeDt...  14.7 us
    sub x6, other arithmetic, adam_step(): return (weight - rate * (ratio + decay * weight), first_new, second_new)  13 us
    unnamed x62, local copies, waits for them, and re-layouts  7.32 us
  transfers between devices with their start and end apart: 3, of which 0 were waited for; matrix products, arithmetic and copies ran while one was open for 0% of the time, Pallas kernels for 15%

profile of v6, /device:TPU:0, one launch (start us, length us, event | category | flops | bytes accessed | tf_op | source)
XLA Modules:
  0.0 194.2 jit_solution(5392068680693401812)
XLA Ops:
  0.7 14.7 %enter.1 = (bf16[4,128,768]{2,1,0:T(8,128)(2,1)}, bf16[3,8,24,512]{3,2,1,0:T(8,128)(2,1)}) custom-call(bf16[128,768]{1,0:T(8,128)(2,1)} %x_ref.5, f32[5,768]{1,0:T(8,128)} %np_ref.5, f32[3,192,768]{2,1,0:T(8,128)} %w_hbm.3), custom_call_target="tpu_custom_call" | custom-call | tf_op jit(solution)/shard_map/enter/pallas_call | solution.py:432
  15.4 1.9 collective-permute-start
  17.3 0.4 collective-permute-start.1
  17.7 0.0 collective-permute-start.2
  17.7 0.7 reshape.107.bias_ref
  19.1 0.0 copy-start.6
  19.1 1.1 copy-done.6
  20.2 0.7 copy-done.10
  20.9 0.7 copy-done.12
  21.5 0.7 copy-done.14
  22.2 0.0 copy-start.8
  22.2 0.0 copy-start.9
  22.2 29.2 %attend.1 = (bf16[8,24,512]{2,1,0:T(8,128)(2,1)S(1)}, bf16[4096,512]{1,0:T(8,128)(2,1)S(1)}) custom-call(s32[1,16]{1,0:T(1,128)S(1)} %copy-done.14, f32[3,512]{1,0:T(4,128)S(1)} %copy-done.10, bf16[3,8,24,512]{3,2,1,0:T(8,128)(2,1)S(1)} %copy-done.6, f32[8,128]{1,0:T(8,128)S(1)} %copy-done.12), custom_call_target="tpu_custom_call" | custom-call | flops 1006632960 | bytes 2097152 | tf_op jit(solution)/shard_map/attend/pallas_call | solution.py:139
  51.4 0.0 collective-permute-done.rest_1_
  51.4 0.0 collective-permute-done.1.rest_2_
  51.5 0.0 collective-permute-done.2.rest_3_
  51.5 0.0 copy-done.1
  51.5 0.0 copy-done.2
  51.5 0.0 copy-done.3
  51.5 0.0 copy-done.4
  51.5 0.0 copy-done.8
  51.5 0.0 copy-done.9
  51.5 0.0 copy-start
  51.5 0.0 copy-start.5
  51.5 0.0 copy-start.7
  51.6 0.0 copy-start.11
  51.6 37.1 %middle.1 = (f32[128,768]{1,0:T(8,128)S(1)}, f32[128,768]{1,0:T(8,128)S(1)}, bf16[8,24,512]{2,1,0:T(8,128)(2,1)S(1)}, bf16[768,768]{1,0:T(8,128)(2,1)S(1)}, bf16...) custom-call(bf16[128,768]{1,0:T(8,128)(2,1)S(1)} %copy-done.4, ...), custom_call_target="tpu_custom_call" | custom-call | tf_op jit(solution)/shard_map/middle/pallas_call | solution.py:572
  88.7 0.0 copy-done
  88.7 0.0 copy-done.5
  88.7 0.0 copy-done.7
  88.7 0.0 copy-done.11
  88.7 86.6 %rear.1 = (bf16[2,2,2,48,768]{4,3,2,1,0:T(8,128)(2,1)S(1)}, bf16[2,2,2,48,768]{4,3,2,1,0:T(8,128)(2,1)S(1)}, bf16[2,2,2,48,768]{4,3,2,1,0:T(8,128)(2,1)S(1)}, bf...) custom-call(f32[3,512]{1,0:T(4,128)S(1)} %copy-done.11, ...), custom_call_target="tpu_custom_call" | custom-call | tf_op jit(solution)/shard_map/rear/pallas_call | solution.py:884
  175.3 0.0 copy-start.23
  175.3 0.0 copy-start.24
  175.4 0.0 copy-start.25
  175.4 0.0 copy-start.26
  175.4 0.0 copy-start.27
  175.4 0.0 copy-start.13
  175.4 0.0 copy-start.28
  175.4 0.0 copy-start.29
  175.4 0.0 copy-start.21
  175.4 0.0 copy-start.22
  175.6 0.2 convert_multiply_fusion.2
  175.8 0.0 copy-start.19
  175.9 0.0 copy-start.20
  175.9 0.2 copy-done.23
  176.1 0.0 copy-done.24
  176.1 0.6 multiply_subtract_fusion.4
  176.7 0.0 copy-done.25
  176.7 0.0 copy-done.26
  176.7 0.0 copy-done.27
  176.7 0.6 multiply_subtract_fusion.5
  177.4 0.0 copy-done.13
  177.4 0.6 multiply_subtract_fusion.6
  178.0 1.5 multiply_subtract_fusion.3
  179.5 0.0 copy-start.17
  179.5 0.0 copy-start.18
  179.5 3.3 %multiply_subtract_fusion.2 = (f32[3,192,768]{2,1,0:T(8,128)}, f32[3,192,768]{2,1,0:T(8,128)}, f32[3,192,768]{2,1,0:T(8,128)}) fusion(f32[3,192,768]{2,1,0:T(8,128)S(1)} %copy-done, f32[]{:T(128)} %bitcast.10, f32[]{:T(128)} %bitcast.9, f32[3,2,2,2,24,768]{5,4,3,2,1,0:T(8,128)S(1)} %convert_multiply_fusion.2, f32[3,192,768]{2,1,0:T(8,128)S(1)} %copy-done.19, ...), kind=kLoop, calls=%fused_computation.14 | loop fusion | flops 6635520 | bytes 12386312 | tf_op jit(solution)/shard_map/sub | solution.py:925
  182.8 1.0 copy-done.16
  183.8 0.7 copy-done.17
  184.5 0.7 copy-done.18
  185.2 6.4 %multiply_subtract_fusion = (f32[768,768]{1,0:T(8,128)}, f32[768,768]{1,0:T(8,128)}, f32[768,768]{1,0:T(8,128)}, f32[768,768]{1,0:T(8,128)}, f32[768,768]{1,0:T(8,128)}, /*index=5*/f32[768,768]{1,0:T(8,128)}) fusion(f32[768,768]{1,0:T(8,128)S(1)} %copy-done.2, f32[]{:T(128)} %bitcast.10, f32[]{:T(128)} %bitcast.9, f32[]{:T(128)} %bitcast.7, ...), kind=kLoop, calls=%fused_computation.5 | loop fusion | flops 23592960 | bytes 30670860 | tf_op jit(solution)/shard_map/sub | solution.py:925
  191.6 0.7 copy.53
  192.3 0.7 copy.54
  (18 shorter events, 0.1 us)
Async XLA Ops:
  15.4 36.0 %collective-permute-start = (bf16[128,768]{1,0:T(8,128)(2,1)}, bf16[128,768]{1,0:T(8,128)(2,1)S(1)}, u32[]{:S(2)}, u32[]{:S(2)}) collective-permute-start(bf16[128,768]{1,0:T(8,128)(2,1)} %rest_0_.1), channel_id=1, source_target_pairs={{1,0},{2,1},{3,2},{0,3},{5,4},{6,5},{7,6},{4,7},{9,8},{10,9},{11,1... | collective-permute-start | bytes 589832 | tf_op jit(solution)/shard_map/ppermute | solution.py:935
  17.3 34.2 %collective-permute-start.1 = (bf16[128,768]{1,0:T(8,128)(2,1)}, bf16[128,768]{1,0:T(8,128)(2,1)S(1)}, u32[]{:S(2)}, u32[]{:S(2)}) collective-permute-start(bf16[128,768]{1,0:T(8,128)(2,1)} %rest_0_.1), channel_id=1, source_target_pairs={{2,0},{3,1},{0,2},{1,3},{6,4},{7,5},{4,6},{5,7},{10,8},{11,9},{8,1... | collective-permute-start | bytes 589832 | tf_op jit(solution)/shard_map/ppermute | solution.py:935
  17.7 33.8 %collective-permute-start.2 = (bf16[128,768]{1,0:T(8,128)(2,1)}, bf16[128,768]{1,0:T(8,128)(2,1)S(1)}, u32[]{:S(2)}, u32[]{:S(2)}) collective-permute-start(bf16[128,768]{1,0:T(8,128)(2,1)} %rest_0_.1), channel_id=1, source_target_pairs={{3,0},{0,1},{1,2},{2,3},{7,4},{4,5},{5,6},{6,7},{11,8},{8,9},{9,10... | collective-permute-start | bytes 589832 | tf_op jit(solution)/shard_map/ppermute | solution.py:935
  19.1 1.1 copy-start.6
  20.2 0.7 copy-start.10
  20.8 0.7 copy-start.12
  21.5 0.7 copy-start.14
  22.2 29.3 %copy-start.1 = (f32[768,768]{1,0:T(8,128)S(1)}, f32[768,768]{1,0:T(8,128)}, u32[]{:S(2)}) copy-start(f32[768,768]{1,0:T(8,128)} %iw_hbm.1) | copy-start | bytes 7077892
  22.2 29.3 %copy-start.2 = (f32[768,768]{1,0:T(8,128)S(1)}, f32[768,768]{1,0:T(8,128)}, u32[]{:S(2)}) copy-start(f32[768,768]{1,0:T(8,128)} %ow_hbm.1) | copy-start | bytes 7077892
  22.2 29.3 %copy-start.3 = (f32[192,768]{1,0:T(8,128)S(1)}, f32[192,768]{1,0:T(8,128)}, u32[]{:S(2)}) copy-start(f32[192,768]{1,0:T(8,128)} %pw_hbm.1) | copy-start | bytes 1769476
  22.2 29.3 %copy-start.4 = (bf16[128,768]{1,0:T(8,128)(2,1)S(1)}, bf16[128,768]{1,0:T(8,128)(2,1)}, u32[]{:S(2)}) copy-start(bf16[128,768]{1,0:T(8,128)(2,1)} %x_ref.5) | copy-start | bytes 589828
  22.2 29.3 %copy-start.8 = (f32[5,768]{1,0:T(8,128)S(1)}, f32[5,768]{1,0:T(8,128)}, u32[]{:S(2)}) copy-start(f32[5,768]{1,0:T(8,128)} %np_ref.5) | copy-start | bytes 46084
  22.2 29.3 %copy-start.9 = (bf16[128,768]{1,0:T(8,128)(2,1)S(1)}, bf16[128,768]{1,0:T(8,128)(2,1)}, u32[]{:S(2)}) copy-start(bf16[128,768]{1,0:T(8,128)(2,1)} %rest_0_.1) | copy-start | bytes 589828
  51.5 37.1 %copy-start = (f32[3,192,768]{2,1,0:T(8,128)S(1)}, f32[3,192,768]{2,1,0:T(8,128)}, u32[]{:S(2)}) copy-start(f32[3,192,768]{2,1,0:T(8,128)} %w_hbm.3) | copy-start | bytes 5308420
  51.5 37.1 %copy-start.5 = (bf16[4,128,768]{2,1,0:T(8,128)(2,1)S(1)}, bf16[4,128,768]{2,1,0:T(8,128)(2,1)}, u32[]{:S(2)}) copy-start(bf16[4,128,768]{2,1,0:T(8,128)(2,1)} %get-tuple-element.60.h_ref) | copy-start | bytes 2359300
  51.5 37.1 %copy-start.7 = (bf16[3,8,24,512]{3,2,1,0:T(8,128)(2,1)S(1)}, bf16[3,8,24,512]{3,2,1,0:T(8,128)(2,1)}, u32[]{:S(2)}) copy-start(bf16[3,8,24,512]{3,2,1,0:T(8,128)(2,1)} %get-tuple-element.50.qkv_ref) | copy-start | bytes 1769476
  51.6 37.1 %copy-start.11 = (f32[3,512]{1,0:T(4,128)S(1)}, f32[3,512]{1,0:T(4,128)}, u32[]{:S(2)}) copy-start(f32[3,512]{1,0:T(4,128)} %coords_ref.3) | copy-start | bytes 18436
  175.3 0.7 copy-start.23
  175.3 0.7 copy-start.24
  175.4 1.4 copy-start.25
  175.4 1.4 copy-start.26
  175.4 1.4 copy-start.27
  175.4 2.0 %copy-start.13 = (f32[8,128]{1,0:T(8,128)S(1)}, f32[8,128]{1,0:T(8,128)}, u32[]{:S(2)}) copy-start(f32[8,128]{1,0:T(8,128)} %w_ref.1) | copy-start | bytes 12292
  175.4 2.0 %copy-start.28 = (f32[8,128]{1,0:T(8,128)S(1)}, f32[8,128]{1,0:T(8,128)}, u32[]{:S(2)}) copy-start(f32[8,128]{1,0:T(8,128)} %param.47) | copy-start | bytes 12292
  175.4 2.0 %copy-start.29 = (f32[8,128]{1,0:T(8,128)S(1)}, f32[8,128]{1,0:T(8,128)}, u32[]{:S(2)}) copy-start(f32[8,128]{1,0:T(8,128)} %param.40) | copy-start | bytes 12292
  175.4 2.6 %copy-start.21 = (f32[192,768]{1,0:T(8,128)S(1)}, f32[192,768]{1,0:T(8,128)}, u32[]{:S(2)}) copy-start(f32[192,768]{1,0:T(8,128)} %param.46) | copy-start | bytes 1769476
  175.4 2.6 %copy-start.22 = (f32[192,768]{1,0:T(8,128)S(1)}, f32[192,768]{1,0:T(8,128)}, u32[]{:S(2)}) copy-start(f32[192,768]{1,0:T(8,128)} %param.39) | copy-start | bytes 1769476
  175.8 3.6 %copy-start.19 = (f32[3,192,768]{2,1,0:T(8,128)S(1)}, f32[3,192,768]{2,1,0:T(8,128)}, u32[]{:S(2)}) copy-start(f32[3,192,768]{2,1,0:T(8,128)} %param.45) | copy-start | bytes 5308420
  175.9 3.6 %copy-start.20 = (f32[3,192,768]{2,1,0:T(8,128)S(1)}, f32[3,192,768]{2,1,0:T(8,128)}, u32[]{:S(2)}) copy-start(f32[3,192,768]{2,1,0:T(8,128)} %param.38) | copy-start | bytes 5308420
  179.5 3.3 %copy-start.15 = (f32[768,768]{1,0:T(8,128)S(1)}, f32[768,768]{1,0:T(8,128)}, u32[]{:S(2)}) copy-start(f32[768,768]{1,0:T(8,128)} %param.50) | copy-start | bytes 7077892
  179.5 4.3 %copy-start.16 = (f32[768,768]{1,0:T(8,128)S(1)}, f32[768,768]{1,0:T(8,128)}, u32[]{:S(2)}) copy-start(f32[768,768]{1,0:T(8,128)} %param.43) | copy-start | bytes 7077892
  179.5 5.0 %copy-start.17 = (f32[768,768]{1,0:T(8,128)S(1)}, f32[768,768]{1,0:T(8,128)}, u32[]{:S(2)}) copy-start(f32[768,768]{1,0:T(8,128)} %param.48) | copy-start | bytes 7077892
  179.5 5.7 %copy-start.18 = (f32[768,768]{1,0:T(8,128)S(1)}, f32[768,768]{1,0:T(8,128)}, u32[]{:S(2)}) copy-start(f32[768,768]{1,0:T(8,128)} %param.41) | copy-start | bytes 7077892

commit v7 on v6

--- a/solution.py
+++ b/solution.py
@@ -128,7 +128,7 @@
             o_ref[h, :, cols] = mm(qkv_ref[2, h], p, NT).astype(BF16)
         return carry
 
-    lax.fori_loop(0, heads, head, 0)
+    lax.fori_loop(0, heads, head, 0, unroll=4)
 
 
 def attention(qkv, coords, lengths, pair_weight):

time: 194 us -> 191 us (0.985)
  Pallas kernels: 168 us -> 164 us
    pallas_call x1, Pallas kernels: 29.2 us -> 24.6 us  [attention(): pl.pallas_call(functools.partial(fwd_kernel, heads, mols), out_shape=(jax...]
  transfers between devices with their start and end apart: 3 -> 3, of which waited for: 0 -> 0; matrix products, arithmetic and copies ran while one was open for 0% -> 0% of each run, Pallas kernels for 15% -> 13%
where the time goes in v7:
time: 191 us; the launch traced here: 190 us
  Pallas kernels  164 us (86%)
  other arithmetic  13.3 us (7%)
  local copies, waits for them, and re-layouts  8.01 us (4%)
  between operations  2.98 us (2%)
  starting transfers between devices  2.26 us (1%)
    pallas_call x1, Pallas kernels, rear(): pl.pallas_call(functools.partial(rear_kernel, n, ny, nz, pushes), out_sha...  86.1 us
    pallas_call x1, Pallas kernels, middle(): pl.pallas_call(functools.partial(middle_kernel, n, ny, nz, pushes), out_s...  38.3 us
    pallas_call x1, Pallas kernels, attention(): pl.pallas_call(functools.partial(fwd_kernel, heads, mols), out_shape=(jax...  24.6 us
    pallas_call x1, Pallas kernels, enter(): pl.pallas_call(functools.partial(enter_kernel, n), out_shape=(jax.ShapeDt...  14.7 us
    sub x6, other arithmetic, adam_step(): return (weight - rate * (ratio + decay * weight), first_new, second_new)  13 us
    unnamed x62, local copies, waits for them, and re-layouts  7.32 us
  transfers between devices with their start and end apart: 3, of which 0 were waited for; matrix products, arithmetic and copies ran while one was open for 0% of the time, Pallas kernels for 13%

profile of v7, /device:TPU:0, one launch (start us, length us, event | category | flops | bytes accessed | tf_op | source)
XLA Modules:
  0.0 190.2 jit_solution(17224771923311656981)
XLA Ops:
  0.7 14.7 %enter.1 = (bf16[4,128,768]{2,1,0:T(8,128)(2,1)}, bf16[3,8,24,512]{3,2,1,0:T(8,128)(2,1)}) custom-call(bf16[128,768]{1,0:T(8,128)(2,1)} %x_ref.5, f32[5,768]{1,0:T(8,128)} %np_ref.5, f32[3,192,768]{2,1,0:T(8,128)} %w_hbm.3), custom_call_target="tpu_custom_call" | custom-call | tf_op jit(solution)/shard_map/enter/pallas_call | solution.py:432
  15.4 1.9 collective-permute-start
  17.3 0.4 collective-permute-start.1
  17.7 0.0 collective-permute-start.2
  17.7 0.7 reshape.107.bias_ref
  19.1 0.0 copy-start.6
  19.1 1.1 copy-done.6
  20.2 0.7 copy-done.10
  20.9 0.7 copy-done.12
  21.5 0.7 copy-done.14
  22.2 0.0 copy-start.8
  22.2 0.0 copy-start.9
  22.2 24.6 %attend.1 = (bf16[8,24,512]{2,1,0:T(8,128)(2,1)S(1)}, bf16[4096,512]{1,0:T(8,128)(2,1)S(1)}) custom-call(s32[1,16]{1,0:T(1,128)S(1)} %copy-done.14, f32[3,512]{1,0:T(4,128)S(1)} %copy-done.10, bf16[3,8,24,512]{3,2,1,0:T(8,128)(2,1)S(1)} %copy-done.6, f32[8,128]{1,0:T(8,128)S(1)} %copy-done.12), custom_call_target="tpu_custom_call" | custom-call | flops 1006632960 | bytes 2097152 | tf_op jit(solution)/shard_map/attend/pallas_call | solution.py:139
  46.8 0.0 collective-permute-done.rest_1_
  46.8 0.0 collective-permute-done.1.rest_2_
  46.9 0.0 collective-permute-done.2.rest_3_
  46.9 0.0 copy-done.1
  46.9 0.0 copy-done.2
  46.9 0.0 copy-done.3
  46.9 0.0 copy-done.4
  46.9 0.0 copy-done.8
  46.9 0.0 copy-done.9
  46.9 0.0 copy-start
  46.9 0.0 copy-start.5
  46.9 0.0 copy-start.7
  47.0 0.0 copy-start.11
  47.0 38.3 %middle.1 = (f32[128,768]{1,0:T(8,128)S(1)}, f32[128,768]{1,0:T(8,128)S(1)}, bf16[8,24,512]{2,1,0:T(8,128)(2,1)S(1)}, bf16[768,768]{1,0:T(8,128)(2,1)S(1)}, bf16...) custom-call(bf16[128,768]{1,0:T(8,128)(2,1)S(1)} %copy-done.4, ...), custom_call_target="tpu_custom_call" | custom-call | tf_op jit(solution)/shard_map/middle/pallas_call | solution.py:572
  85.2 0.0 copy-done
  85.2 0.0 copy-done.5
  85.2 0.0 copy-done.7
  85.3 0.0 copy-done.11
  85.3 86.1 %rear.1 = (bf16[2,2,2,48,768]{4,3,2,1,0:T(8,128)(2,1)S(1)}, bf16[2,2,2,48,768]{4,3,2,1,0:T(8,128)(2,1)S(1)}, bf16[2,2,2,48,768]{4,3,2,1,0:T(8,128)(2,1)S(1)}, bf...) custom-call(f32[3,512]{1,0:T(4,128)S(1)} %copy-done.11, ...), custom_call_target="tpu_custom_call" | custom-call | tf_op jit(solution)/shard_map/rear/pallas_call | solution.py:884
  171.4 0.0 copy-start.23
  171.4 0.0 copy-start.24
  171.4 0.0 copy-start.25
  171.4 0.0 copy-start.26
  171.4 0.0 copy-start.27
  171.4 0.0 copy-start.13
  171.4 0.0 copy-start.28
  171.4 0.0 copy-start.29
  171.5 0.0 copy-start.21
  171.5 0.0 copy-start.22
  171.7 0.2 convert_multiply_fusion.2
  171.9 0.0 copy-start.19
  171.9 0.0 copy-start.20
  171.9 0.2 copy-done.23
  172.1 0.0 copy-done.24
  172.1 0.6 multiply_subtract_fusion.4
  172.8 0.0 copy-done.25
  172.8 0.0 copy-done.26
  172.8 0.6 multiply_subtract_fusion.5
  173.4 0.6 multiply_subtract_fusion.6
  174.0 0.0 copy-done.22
  174.0 1.5 multiply_subtract_fusion.3
  175.5 0.0 copy-done.20
  175.5 0.0 copy-start.17
  175.5 0.0 copy-start.18
  175.6 3.3 %multiply_subtract_fusion.2 = (f32[3,192,768]{2,1,0:T(8,128)}, f32[3,192,768]{2,1,0:T(8,128)}, f32[3,192,768]{2,1,0:T(8,128)}) fusion(f32[3,192,768]{2,1,0:T(8,128)S(1)} %copy-done, f32[]{:T(128)} %bitcast.10, f32[]{:T(128)} %bitcast.9, f32[3,2,2,2,24,768]{5,4,3,2,1,0:T(8,128)S(1)} %convert_multiply_fusion.2, f32[3,192,768]{2,1,0:T(8,128)S(1)} %copy-done.19, ...), kind=kLoop, calls=%fused_computation.14 | loop fusion | flops 6635520 | bytes 12386312 | tf_op jit(solution)/shard_map/sub | solution.py:925
  178.8 1.0 copy-done.16
  179.8 0.7 copy-done.17
  180.5 0.7 copy-done.18
  181.2 6.4 %multiply_subtract_fusion = (f32[768,768]{1,0:T(8,128)}, f32[768,768]{1,0:T(8,128)}, f32[768,768]{1,0:T(8,128)}, f32[768,768]{1,0:T(8,128)}, f32[768,768]{1,0:T(8,128)}, /*index=5*/f32[768,768]{1,0:T(8,128)}) fusion(f32[768,768]{1,0:T(8,128)S(1)} %copy-done.2, f32[]{:T(128)} %bitcast.10, f32[]{:T(128)} %bitcast.9, f32[]{:T(128)} %bitcast.7, ...), kind=kLoop, calls=%fused_computation.5 | loop fusion | flops 23592960 | bytes 30670860 | tf_op jit(solution)/shard_map/sub | solution.py:925
  187.6 0.7 copy.53
  188.3 0.7 copy.54
  (18 shorter events, 0.1 us)
Async XLA Ops:
  15.4 31.4 %collective-permute-start = (bf16[128,768]{1,0:T(8,128)(2,1)}, bf16[128,768]{1,0:T(8,128)(2,1)S(1)}, u32[]{:S(2)}, u32[]{:S(2)}) collective-permute-start(bf16[128,768]{1,0:T(8,128)(2,1)} %rest_0_.1), channel_id=1, source_target_pairs={{1,0},{2,1},{3,2},{0,3},{5,4},{6,5},{7,6},{4,7},{9,8},{10,9},{11,1... | collective-permute-start | bytes 589832 | tf_op jit(solution)/shard_map/ppermute | solution.py:935
  17.3 29.6 %collective-permute-start.1 = (bf16[128,768]{1,0:T(8,128)(2,1)}, bf16[128,768]{1,0:T(8,128)(2,1)S(1)}, u32[]{:S(2)}, u32[]{:S(2)}) collective-permute-start(bf16[128,768]{1,0:T(8,128)(2,1)} %rest_0_.1), channel_id=1, source_target_pairs={{2,0},{3,1},{0,2},{1,3},{6,4},{7,5},{4,6},{5,7},{10,8},{11,9},{8,1... | collective-permute-start | bytes 589832 | tf_op jit(solution)/shard_map/ppermute | solution.py:935
  17.7 29.2 %collective-permute-start.2 = (bf16[128,768]{1,0:T(8,128)(2,1)}, bf16[128,768]{1,0:T(8,128)(2,1)S(1)}, u32[]{:S(2)}, u32[]{:S(2)}) collective-permute-start(bf16[128,768]{1,0:T(8,128)(2,1)} %rest_0_.1), channel_id=1, source_target_pairs={{3,0},{0,1},{1,2},{2,3},{7,4},{4,5},{5,6},{6,7},{11,8},{8,9},{9,10... | collective-permute-start | bytes 589832 | tf_op jit(solution)/shard_map/ppermute | solution.py:935
  19.1 1.1 copy-start.6
  20.2 0.7 copy-start.10
  20.8 0.7 copy-start.12
  21.5 0.7 copy-start.14
  22.2 24.7 %copy-start.1 = (f32[768,768]{1,0:T(8,128)S(1)}, f32[768,768]{1,0:T(8,128)}, u32[]{:S(2)}) copy-start(f32[768,768]{1,0:T(8,128)} %iw_hbm.1) | copy-start | bytes 7077892
  22.2 24.7 %copy-start.2 = (f32[768,768]{1,0:T(8,128)S(1)}, f32[768,768]{1,0:T(8,128)}, u32[]{:S(2)}) copy-start(f32[768,768]{1,0:T(8,128)} %ow_hbm.1) | copy-start | bytes 7077892
  22.2 24.7 %copy-start.3 = (f32[192,768]{1,0:T(8,128)S(1)}, f32[192,768]{1,0:T(8,128)}, u32[]{:S(2)}) copy-start(f32[192,768]{1,0:T(8,128)} %pw_hbm.1) | copy-start | bytes 1769476
  22.2 24.7 %copy-start.4 = (bf16[128,768]{1,0:T(8,128)(2,1)S(1)}, bf16[128,768]{1,0:T(8,128)(2,1)}, u32[]{:S(2)}) copy-start(bf16[128,768]{1,0:T(8,128)(2,1)} %x_ref.5) | copy-start | bytes 589828
  22.2 24.7 %copy-start.8 = (f32[5,768]{1,0:T(8,128)S(1)}, f32[5,768]{1,0:T(8,128)}, u32[]{:S(2)}) copy-start(f32[5,768]{1,0:T(8,128)} %np_ref.5) | copy-start | bytes 46084
  22.2 24.7 %copy-start.9 = (bf16[128,768]{1,0:T(8,128)(2,1)S(1)}, bf16[128,768]{1,0:T(8,128)(2,1)}, u32[]{:S(2)}) copy-start(bf16[128,768]{1,0:T(8,128)(2,1)} %rest_0_.1) | copy-start | bytes 589828
  46.9 38.3 %copy-start = (f32[3,192,768]{2,1,0:T(8,128)S(1)}, f32[3,192,768]{2,1,0:T(8,128)}, u32[]{:S(2)}) copy-start(f32[3,192,768]{2,1,0:T(8,128)} %w_hbm.3) | copy-start | bytes 5308420
  46.9 38.3 %copy-start.5 = (bf16[4,128,768]{2,1,0:T(8,128)(2,1)S(1)}, bf16[4,128,768]{2,1,0:T(8,128)(2,1)}, u32[]{:S(2)}) copy-start(bf16[4,128,768]{2,1,0:T(8,128)(2,1)} %get-tuple-element.60.h_ref) | copy-start | bytes 2359300
  46.9 38.3 %copy-start.7 = (bf16[3,8,24,512]{3,2,1,0:T(8,128)(2,1)S(1)}, bf16[3,8,24,512]{3,2,1,0:T(8,128)(2,1)}, u32[]{:S(2)}) copy-start(bf16[3,8,24,512]{3,2,1,0:T(8,128)(2,1)} %get-tuple-element.50.qkv_ref) | copy-start | bytes 1769476
  47.0 38.3 %copy-start.11 = (f32[3,512]{1,0:T(4,128)S(1)}, f32[3,512]{1,0:T(4,128)}, u32[]{:S(2)}) copy-start(f32[3,512]{1,0:T(4,128)} %coords_ref.3) | copy-start | bytes 18436
  171.4 0.7 copy-start.23
  171.4 0.7 copy-start.24
  171.4 1.4 copy-start.25
  171.4 1.4 copy-start.26
  171.4 1.4 copy-start.27
  171.4 2.0 %copy-start.13 = (f32[8,128]{1,0:T(8,128)S(1)}, f32[8,128]{1,0:T(8,128)}, u32[]{:S(2)}) copy-start(f32[8,128]{1,0:T(8,128)} %w_ref.1) | copy-start | bytes 12292
  171.4 2.0 %copy-start.28 = (f32[8,128]{1,0:T(8,128)S(1)}, f32[8,128]{1,0:T(8,128)}, u32[]{:S(2)}) copy-start(f32[8,128]{1,0:T(8,128)} %param.47) | copy-start | bytes 12292
  171.4 2.0 %copy-start.29 = (f32[8,128]{1,0:T(8,128)S(1)}, f32[8,128]{1,0:T(8,128)}, u32[]{:S(2)}) copy-start(f32[8,128]{1,0:T(8,128)} %param.40) | copy-start | bytes 12292
  171.5 2.6 %copy-start.21 = (f32[192,768]{1,0:T(8,128)S(1)}, f32[192,768]{1,0:T(8,128)}, u32[]{:S(2)}) copy-start(f32[192,768]{1,0:T(8,128)} %param.46) | copy-start | bytes 1769476
  171.5 2.6 %copy-start.22 = (f32[192,768]{1,0:T(8,128)S(1)}, f32[192,768]{1,0:T(8,128)}, u32[]{:S(2)}) copy-start(f32[192,768]{1,0:T(8,128)} %param.39) | copy-start | bytes 1769476
  171.9 3.6 %copy-start.19 = (f32[3,192,768]{2,1,0:T(8,128)S(1)}, f32[3,192,768]{2,1,0:T(8,128)}, u32[]{:S(2)}) copy-start(f32[3,192,768]{2,1,0:T(8,128)} %param.45) | copy-start | bytes 5308420
  171.9 3.6 %copy-start.20 = (f32[3,192,768]{2,1,0:T(8,128)S(1)}, f32[3,192,768]{2,1,0:T(8,128)}, u32[]{:S(2)}) copy-start(f32[3,192,768]{2,1,0:T(8,128)} %param.38) | copy-start | bytes 5308420
  175.5 3.3 %copy-start.15 = (f32[768,768]{1,0:T(8,128)S(1)}, f32[768,768]{1,0:T(8,128)}, u32[]{:S(2)}) copy-start(f32[768,768]{1,0:T(8,128)} %param.50) | copy-start | bytes 7077892
  175.5 4.3 %copy-start.16 = (f32[768,768]{1,0:T(8,128)S(1)}, f32[768,768]{1,0:T(8,128)}, u32[]{:S(2)}) copy-start(f32[768,768]{1,0:T(8,128)} %param.43) | copy-start | bytes 7077892
  175.5 5.0 %copy-start.17 = (f32[768,768]{1,0:T(8,128)S(1)}, f32[768,768]{1,0:T(8,128)}, u32[]{:S(2)}) copy-start(f32[768,768]{1,0:T(8,128)} %param.48) | copy-start | bytes 7077892
  175.5 5.7 %copy-start.18 = (f32[768,768]{1,0:T(8,128)S(1)}, f32[768,768]{1,0:T(8,128)}, u32[]{:S(2)}) copy-start(f32[768,768]{1,0:T(8,128)} %param.41) | copy-start | bytes 7077892
